TPU v7x, 512 devices: a whole 4x8x8 slice. The times are simulated.
512 devices in a mesh: dp: 32 (over y, x_lo, core), mp: 16 (over z, x_hi).
Axes of the slice: x: 4 (x_hi: 2, x_lo: 2; x = x_hi * 2 + x_lo), y: 8, z: 8, core: 2. Of those that a mesh axis runs over, the one named last changes fastest.
Arguments:
- hidden: bfloat16 [4096, 2048], P('dp', 'mp'), may hold values from -6 to 6
- q_weight: bfloat16 [2048, 3072], P('dp', 'mp'), may hold values from -0.125 to 0.125
- dkv_weight: bfloat16 [2048, 576], P('mp', 'dp'), may hold values from -0.125 to 0.125
- latent_gain: float32 [512], replicated, may hold values from 0.1 to 1.9
- kvb_weight: bfloat16 [512, 16, 256], P('dp', 'mp'), may hold values from -0.25 to 0.25
- out_weight: bfloat16 [2048, 2048], P('mp', 'dp'), may hold values from -0.125 to 0.125
- cache: bfloat16 [8192, 64, 576], P(('dp', 'mp')), may hold values from -200 to 200
- cache_len: int32 [64], P('dp'), may hold values from 64 to 8128
- draft_count: int32 [64], P('dp'), may hold values from 32 to 64
- parents: int32 [64, 64], P('dp'), may hold values from 0 to 62, as said below
- accept_node: int32 [64], P('dp'), may hold values from 0 to 63, as said below
- page_table: int32 [64, 128], P('dp'), may hold values from 0 to 255, as said below
Outputs:
- attended: bfloat16 [4096, 2048], P(('dp', 'mp'))
- new_cache: bfloat16 [8192, 64, 576], P(('dp', 'mp'))
Inputs may be any that keep to these rules, and one draw needn't show every extreme that they name: `page_table`: within each group of 2 consecutive requests the entries are a permutation of 0 to 255; entry v is slot v % 16 of the group's device v // 16 along mp. parents[q, 0] = 0 and parents[q, i] < i for i >= 1. `accept_node`: less than the request's draft_count.
All inputs are finite; a program needn't handle non-finite values.
Results may differ from a plain program's by a relative error of at most 0.03.
Values may be sent and summed in bfloat16 or wider, within the bound.
No kernel may reach another device: no remote copies, remote signals or barrier semaphores. Data moves between devices by JAX's collectives and lax.ppermute only.
A program may use at most 64 MiB of HBM per device.

v0:
```python
import jax
import jax.numpy as jnp
from jax import lax
from jax.sharding import PartitionSpec as P

NOPE = 128
ROPE = 64
LAT = 512


def tree_reach(parent_row):
    count = parent_row.shape[0]
    index = jnp.arange(count, dtype=jnp.int32)
    linked = jnp.logical_or(
        parent_row[:, None] == index[None, :], index[:, None] == index[None, :]
    ).astype(jnp.float32)
    for _ in range(max(1, (count - 1).bit_length())):
        linked = jnp.minimum(jnp.dot(linked, linked, precision=lax.Precision.HIGHEST), 1.0)
    return linked


def angles(positions, width):
    half_dim = width // 2
    inverse = 10000.0 ** (-(jnp.arange(half_dim, dtype=jnp.float32) * 2.0) / width)
    phase = positions[..., None] * inverse
    return (jnp.cos(phase), jnp.sin(phase))


def rotary(values, cosine, sine):
    half_dim = values.shape[-1] // 2
    first = values[..., :half_dim]
    second = values[..., half_dim:]
    return jnp.concatenate(
        [first * cosine - second * sine, second * cosine + first * sine], axis=-1
    )


def lookup(index_rows, table):
    choices_hot = index_rows[:, None] == jnp.arange(table.shape[0], dtype=jnp.int32)[None, :]
    return jnp.sum(jnp.where(choices_hot, table[None, :], jnp.zeros((), table.dtype)), axis=1)


def tree_part(q_rows, fresh_req, linked, value_maps, scale_val):
    reqs, draft, heads, width = q_rows.shape
    tree_scores = (
        jnp.einsum("rthc,rjc->rthj", q_rows, fresh_req, preferred_element_type=jnp.float32)
        * scale_val
    )
    tree_live = (linked > 0.5)[:, :, None, :]
    tree_top = jnp.max(jnp.where(tree_live, tree_scores, -1e30), axis=3)
    tree_weights = jnp.where(tree_live, jnp.exp(tree_scores - tree_top[..., None]), 0.0)
    tree_sum = jnp.sum(tree_weights, axis=3).reshape(reqs * draft, heads)
    tree_lat = jnp.einsum(
        "rthj,rjl->rthl",
        tree_weights.astype(jnp.bfloat16),
        fresh_req[..., :LAT],
        preferred_element_type=jnp.float32,
    )
    tree_v = jnp.einsum(
        "thl,lhv->thv",
        tree_lat.reshape(reqs * draft, heads, LAT),
        value_maps.astype(jnp.float32),
        precision=lax.Precision.HIGHEST,
    )
    return (tree_top.reshape(reqs * draft, heads), tree_sum, tree_v)


def joined(cache_top, cache_v, cache_sum, tree_top, tree_sum, tree_v):
    joint = jnp.maximum(cache_top, tree_top)
    left_scale = jnp.exp(cache_top - joint)
    right_scale = jnp.exp(tree_top - joint)
    combined = (cache_v * left_scale[..., None] + tree_v * right_scale[..., None]) / (
        cache_sum * left_scale + tree_sum * right_scale
    )[..., None]
    return combined.astype(jnp.bfloat16).reshape(
        combined.shape[0], combined.shape[1] * combined.shape[2]
    )


def per_device(
    hidden,
    q_weight,
    dkv_weight,
    latent_gain,
    kvb_weight,
    out_weight,
    cache,
    cache_len,
    draft_count,
    parents,
    accept_node,
    page_table,
):
    highest = lax.Precision.HIGHEST
    mp_size = lax.axis_size("mp")
    mp_rank = lax.axis_index("mp")
    reqs, draft = parents.shape
    tokens = reqs * draft
    heads_mine = kvb_weight.shape[1]
    heads_all = heads_mine * mp_size
    slot_count, page_len, width = cache.shape
    scale_val = (NOPE + ROPE) ** (-0.5)
    share = tokens // mp_size
    full_x = lax.all_gather(hidden, "mp", axis=1, tiled=True)
    query = jnp.dot(
        full_x,
        lax.all_gather(q_weight, "dp", axis=0, tiled=True),
        preferred_element_type=jnp.float32,
    )
    query = query.astype(jnp.bfloat16).reshape(tokens, heads_mine, NOPE + ROPE)
    linked = jax.vmap(tree_reach)(parents)
    depth = jnp.sum(linked, axis=2) - 1.0
    positions = (cache_len.astype(jnp.float32)[:, None] + depth).reshape(tokens)
    cosine, sine = angles(positions, ROPE)
    down_cols = lax.all_gather(dkv_weight, "dp", axis=1, tiled=True)
    down_full = lax.all_gather(down_cols, "mp", axis=0, tiled=True)
    compressed = jnp.dot(full_x, down_full, preferred_element_type=jnp.float32)
    latent = compressed[:, :LAT]
    normed = (
        latent * lax.rsqrt(jnp.mean(latent * latent, axis=-1, keepdims=True) + 1e-06) * latent_gain
    )
    fresh = jnp.concatenate([normed, rotary(compressed[:, LAT:], cosine, sine)], axis=-1).astype(
        jnp.bfloat16
    )
    fresh_req = fresh.reshape(reqs, draft, width)
    up_maps = lax.all_gather(kvb_weight, "dp", axis=0, tiled=True)
    q_rope = rotary(query[..., NOPE:].astype(jnp.float32), cosine[:, None, :], sine[:, None, :])
    q_latent = jnp.einsum(
        "thn,lhn->thl", query[..., :NOPE], up_maps[:, :, :NOPE], preferred_element_type=jnp.float32
    )
    mine_abs = jnp.concatenate([q_latent, q_rope], axis=-1).astype(jnp.bfloat16)
    q_all = lax.all_gather(mine_abs, "mp", axis=1, tiled=True)
    value_all = lax.all_gather(up_maps[:, :, NOPE:], "mp", axis=1, tiled=True)
    slot_ids = mp_rank * slot_count + jnp.arange(slot_count, dtype=jnp.int32)
    matched = (page_table[:, :, None] == slot_ids[None, None, :]).astype(jnp.int32)
    slot_req = jnp.sum(matched * jnp.arange(reqs, dtype=jnp.int32)[:, None, None], axis=(0, 1))
    slot_page = jnp.sum(
        matched * jnp.arange(page_table.shape[1], dtype=jnp.int32)[None, :, None], axis=(0, 1)
    )
    key_pos = (
        slot_page[:, None] * page_len + jnp.arange(page_len, dtype=jnp.int32)[None, :]
    ).reshape(slot_count * page_len)
    key_req = jnp.repeat(slot_req, page_len)
    keys = cache.reshape(slot_count * page_len, width)
    top_list = []
    sum_list = []
    out_list = []
    for request in range(reqs):
        rows = q_all[request * draft : (request + 1) * draft].reshape(draft * heads_all, width)
        scores = (
            lax.dot_general(
                rows, keys, (((1,), (1,)), ((), ())), preferred_element_type=jnp.float32
            )
            * scale_val
        )
        live = jnp.logical_and(key_req == request, key_pos < cache_len[request])[None, :]
        top_row = jnp.max(jnp.where(live, scores, -1e30), axis=1)
        weights = jnp.where(live, jnp.exp(scores - top_row[:, None]), 0.0)
        top_list.append(top_row)
        sum_list.append(jnp.sum(weights, axis=1))
        out_list.append(
            jnp.dot(weights.astype(jnp.bfloat16), keys[:, :LAT], preferred_element_type=jnp.float32)
        )
    local_top = jnp.concatenate(top_list).reshape(tokens, heads_all)
    local_sum = jnp.concatenate(sum_list).reshape(tokens, heads_all)
    local_out = jnp.concatenate(out_list, axis=0).reshape(tokens, heads_all, LAT)
    global_top = lax.pmax(local_top, "mp")
    factor = jnp.exp(local_top - global_top)
    partial_v = jnp.einsum(
        "thl,lhv->thv",
        local_out * factor[..., None],
        value_all.astype(jnp.float32),
        precision=highest,
    )
    out_full = lax.all_gather(out_weight, "dp", axis=1, tiled=True)
    row_index = mp_rank * share + jnp.arange(share, dtype=jnp.int32)
    cache_v, cache_sum = (
        lax.psum_scatter(
            partial_v.astype(jnp.bfloat16), "mp", scatter_dimension=1, tiled=True
        ).astype(jnp.float32),
        lax.psum_scatter(
            (local_sum * factor).astype(jnp.bfloat16), "mp", scatter_dimension=1, tiled=True
        ).astype(jnp.float32),
    )
    mine_top = lax.dynamic_slice_in_dim(global_top, mp_rank * heads_mine, heads_mine, 1)
    mine_q = lax.dynamic_slice_in_dim(q_all, mp_rank * heads_mine, heads_mine, 1)
    tree_top, tree_sum, tree_v = tree_part(
        mine_q.reshape(reqs, draft, heads_mine, width),
        fresh_req,
        linked,
        up_maps[:, :, NOPE:],
        scale_val,
    )
    head_out = joined(mine_top, cache_v, cache_sum, tree_top, tree_sum, tree_v)
    mine_rows = lax.psum_scatter(
        jnp.dot(head_out, out_full, preferred_element_type=jnp.float32).astype(jnp.bfloat16),
        "mp",
        scatter_dimension=0,
        tiled=True,
    ).astype(jnp.float32)
    row_count = lookup(row_index // draft, draft_count)
    attended = jnp.where((row_index % draft < row_count)[:, None], mine_rows, 0.0).astype(
        jnp.bfloat16
    )
    accept_hot = (accept_node[:, None] == jnp.arange(draft, dtype=jnp.int32)[None, :]).astype(
        jnp.float32
    )
    path = jnp.einsum("ri,rij->rj", accept_hot, linked, precision=highest)
    deepest = jnp.sum(path, axis=1) - 1.0
    picker = jnp.logical_and(
        path[:, None, :] > 0.5,
        depth[:, None, :] == jnp.arange(draft, dtype=jnp.int32).astype(jnp.float32)[None, :, None],
    )
    entries = jnp.einsum(
        "rdt,rtc->rdc", picker.astype(jnp.bfloat16), fresh_req, preferred_element_type=jnp.float32
    )
    entries = entries.astype(jnp.bfloat16).reshape(tokens, width)
    key_len = lookup(key_req, cache_len)
    key_deep = lookup(key_req, deepest)
    offset = key_pos - key_len
    column = jnp.arange(tokens, dtype=jnp.int32)
    chosen = jnp.logical_and(
        key_req[:, None] == (column // draft)[None, :], offset[:, None] == (column % draft)[None, :]
    )
    chosen = jnp.logical_and(chosen, (offset.astype(jnp.float32) <= key_deep)[:, None])
    placed = jnp.dot(
        chosen.astype(jnp.bfloat16), entries, preferred_element_type=jnp.float32
    ).astype(jnp.bfloat16)
    new_cache = jnp.where(jnp.any(chosen, axis=1)[:, None], placed, keys).reshape(cache.shape)
    return (attended, new_cache)


def solution(mesh):
    return jax.shard_map(
        per_device,
        mesh=mesh,
        in_specs=(
            P("dp", "mp"),
            P("dp", "mp"),
            P("mp", "dp"),
            P(),
            P("dp", "mp", None),
            P("mp", "dp"),
            P(("dp", "mp"), None, None),
            P("dp"),
            P("dp"),
            P("dp", None),
            P("dp"),
            P("dp", None),
        ),
        out_specs=(P(("dp", "mp"), None), P(("dp", "mp"), None, None)),
        check_vma=False,
    )
```

profile of v0, /device:TPU:1, one launch (start us, length us, event | category | flops | bytes accessed | tf_op | source)
XLA Modules:
  0.0 828.5 jit_solution(14350531714993052761)
XLA Ops:
  10.2 44.0 %all_gather.24 = bf16[128,2048]{1,0:T(8,128)(2,1)S(1)} all-gather(bf16[128,128]{1,0:T(8,128)(2,1)} %param.12), channel_id=1, replica_groups=mesh['dp'=32,'mp'=16] {'mp'}, dimensions={1}, use_global_device_ids=true | all-gather | bytes 557056 | tf_op jit(solution)/shard_map/all_gather | solution.py:104
  54.3 44.4 %all_gather.25 = bf16[2048,192]{1,0:T(8,128)(2,1)S(1)} all-gather(bf16[64,192]{1,0:T(8,128)(2,1)} %param.13), channel_id=1, replica_groups=mesh['dp'=32,'mp'=16] {'dp'}, dimensions={0}, use_global_device_ids=true | all-gather | bytes 811008 | tf_op jit(solution)/shard_map/all_gather | solution.py:107
  99.6 31.4 %all_gather.26 = bf16[512,1,256]{2,0,1:T(8,128)(2,1)S(1)} all-gather(bf16[16,1,256]{2,0,1:T(8,128)(2,1)S(1)} %copy-done.8), channel_id=1, replica_groups=mesh['dp'=32,'mp'=16] {'dp'}, dimensions={0}, use_global_device_ids=true | all-gather | bytes 270336 | tf_op jit(solution)/shard_map/all_gather | solution.py:126
  132.2 32.6 %all-gather = bf16[32,18,128]{2,1,0:T(8,128)(2,1)S(1)} all-gather(bf16[1,18,128]{2,1,0:T(8,128)(2,1)S(1)} %bitcast.116), channel_id=1, replica_groups=mesh['dp'=32,'mp'=16] {'dp'}, dimensions={0}, use_global_device_ids=true | all-gather | bytes 152064 | tf_op jit(solution)/shard_map/all_gather | solution.py:115
  168.0 32.5 %all_gather.31 = bf16[128,2048]{0,1:T(8,128)(2,1)S(1)} all-gather(bf16[128,64]{0,1:T(8,128)(2,1)S(1)} %copy-done.7), channel_id=1, replica_groups=mesh['dp'=32,'mp'=16] {'dp'}, dimensions={1}, use_global_device_ids=true | all-gather | bytes 540672 | tf_op jit(solution)/shard_map/all_gather | solution.py:175
  200.5 1.5 copy.98
  205.7 10.2 %all-gather.5.cloned.1.call-done = bf16[128,16,576]{0,2,1:T(8,128)(2,1)} async-done(((bf16[128,1,576]{0,2,1:T(8,128)(2,1)}), bf16[128,16,576]{0,2,1:T(8,128)(2,1)}) %all-gather.5.cloned.1.call-update) | async-done | bytes 2359312 | tf_op jit(solution)/shard_map/all_gather | solution.py:132
  215.9 4.7 fusion.95
  220.6 4.5 copy.85
  225.1 3.4 copy.84
  228.5 5.6 select_reduce_fusion.1
  234.2 5.2 select_reduce_fusion
  239.4 4.6 fusion.1
  244.5 32.2 %pmax.7 = f32[128,16]{0,1:T(8,128)S(1)} all-reduce(f32[128,16]{0,1:T(8,128)S(1)} %pad_maximum_fusion.5), channel_id=1, replica_groups=mesh['dp'=32,'mp'=16] {'mp'}, use_global_device_ids=true, to_apply=%region_6.7 | all-reduce | flops 2048 | bytes 16384 | tf_op jit(solution)/shard_map/pmax | solution.py:167
  276.9 60.2 %all-reduce = bf16[128,16]{1,0:T(8,128)(2,1)S(1)} all-reduce(bf16[128,16]{1,0:T(8,128)(2,1)S(1)} %copy.96), channel_id=3, replica_groups=mesh['dp'=32,'mp'=16] {'mp'}, use_global_device_ids=true, to_apply=%region_12.13.clone | all-reduce | flops 2048 | bytes 8192
  337.1 2.4 fusion.98
  339.8 3.8 fusion.7
  343.6 1.5 fusion.5
  345.1 2.4 pad_maximum_fusion
  347.4 53.5 %all-gather.7.cloned.1.call-done = bf16[512,16,128]{2,0,1:T(8,128)(2,1)} async-done(((bf16[512,1,128]{2,0,1:T(8,128)(2,1)}), bf16[512,16,128]{2,0,1:T(8,128)(2,1)}) %all-gather.7.cloned.1.call-update) | async-done | bytes 2097168 | tf_op jit(solution)/shard_map/all_gather | solution.py:133
  400.9 7.9 fusion.20
  412.2 198.6 %reduce-scatter.4.cloned.1.call-done = bf16[128,1,128]{2,0,1:T(8,128)(2,1)} async-done(((bf16[128,16,128]{2,0,1:T(8,128)(2,1)}), bf16[128,1,128]{2,0,1:T(8,128)(2,1)}) %reduce-scatter.4.cloned.1.call-update) | async-done | bytes 32784 | tf_op jit(solution)/shard_map/reduce_scatter | solution.py:178
  613.3 1.6 fusion.18
  616.3 204.1 %reduce-scatter.6.cloned.1.call-done = bf16[8,2048]{1,0:T(8,128)(2,1)} async-done(((bf16[128,2048]{1,0:T(8,128)(2,1)}), bf16[8,2048]{1,0:T(8,128)(2,1)}) %reduce-scatter.6.cloned.1.call-update) | async-done | bytes 32784 | tf_op jit(solution)/shard_map/reduce_scatter | solution.py:195
  (119 shorter events, 21.6 us)
Async XLA Ops:
  7.2 159.1 %copy-start.10 = (s32[2]{0:T(128)S(1)}, s32[2]{0:T(128)}, u32[]{:S(2)}) copy-start(s32[2]{0:T(128)} %param.19) | copy-start | bytes 28
  7.2 92.4 %copy-start.8 = (bf16[16,1,256]{2,0,1:T(8,128)(2,1)S(1)}, bf16[16,1,256]{2,0,1:T(8,128)(2,1)}, u32[]{:S(2)}) copy-start(bf16[16,1,256]{2,0,1:T(8,128)(2,1)} %param.16) | copy-start | bytes 24580
  7.2 125.0 %copy-start.9 = (bf16[128,18]{0,1:T(8,128)(2,1)S(1)}, bf16[128,18]{0,1:T(8,128)(2,1)}, u32[]{:S(2)}) copy-start(bf16[128,18]{0,1:T(8,128)(2,1)} %param.14) | copy-start | bytes 13828
  7.2 159.8 %copy-start.12 = (s32[2,128]{1,0:T(2,128)S(1)}, s32[2,128]{1,0:T(2,128)}, u32[]{:S(2)}) copy-start(s32[2,128]{1,0:T(2,128)} %param.23) | copy-start | bytes 3076
  7.2 160.1 %copy-start.13 = (s32[2]{0:T(128)S(1)}, s32[2]{0:T(128)}, u32[]{:S(2)}) copy-start(s32[2]{0:T(128)} %param.22) | copy-start | bytes 28
  7.2 160.8 %copy-start.7 = (bf16[128,64]{0,1:T(8,128)(2,1)S(1)}, bf16[128,64]{0,1:T(8,128)(2,1)}, u32[]{:S(2)}) copy-start(bf16[128,64]{0,1:T(8,128)(2,1)} %param.17) | copy-start | bytes 49156
  7.2 193.3 %copy-start.2 = (bf16[16,64,576]{2,1,0:T(8,128)(2,1)S(1)}, bf16[16,64,576]{2,1,0:T(8,128)(2,1)}, u32[]{:S(2)}) copy-start(bf16[16,64,576]{2,1,0:T(8,128)(2,1)} %param.18) | copy-start | bytes 3538948
  7.2 208.6 %all-gather.5.cloned.1.call-start = ((), (), s32[]{:S(2)}) async-start(), calls=%async_computation.2 | async-start | bytes 2506752 | tf_op jit(solution)/shard_map/all_gather | solution.py:132
  54.3 149.0 %copy-start.14 = (s32[2]{0:T(128)S(1)}, s32[2]{0:T(128)}, u32[]{:S(2)}) copy-start(s32[2]{0:T(128)} %param.20) | copy-start | bytes 28
  131.0 74.7 %copy-start.5 = (bf16[512,1,256]{2,0,1:T(8,128)(2,1)}, bf16[512,1,256]{2,0,1:T(8,128)(2,1)S(1)}, u32[]{:S(2)}) copy-start(bf16[512,1,256]{2,0,1:T(8,128)(2,1)S(1)} %all_gather.26) | copy-start | bytes 786436
  132.1 204.9 %all-gather.9.cloned.1.call-start = ((), (), s32[]{:S(2)}) async-start(), calls=%async_computation.5 | async-start | bytes 2506752 | tf_op jit(solution)/shard_map/all_gather | solution.py:116
  165.5 235.4 %all-gather.7.cloned.1.call-start = ((), (), s32[]{:S(2)}) async-start(), calls=%async_computation.3 | async-start | bytes 2228224 | tf_op jit(solution)/shard_map/all_gather | solution.py:133
  166.2 444.6 %reduce-scatter.4.cloned.1.call-start = ((), (), s32[]{:S(2)}) async-start(), calls=%async_computation.4 | async-start | bytes 557056 | tf_op jit(solution)/shard_map/reduce_scatter | solution.py:178
  228.5 5.7 copy-start.1
  239.4 100.4 %copy-start.3 = (bf16[16,64,576]{2,1,0:T(8,128)(2,1)S(1)}, bf16[16,64,576]{2,1,0:T(8,128)(2,1)}, u32[]{:S(2)}) copy-start(bf16[16,64,576]{2,1,0:T(8,128)(2,1)} %param.18) | copy-start | bytes 3538948
  339.8 3.8 copy-start
  347.4 63.6 %copy-start.11 = (f32[512]{0:T(512)S(1)}, f32[512]{0:T(512)}, u32[]{:S(2)}) copy-start(f32[512]{0:T(512)} %param.15) | copy-start | bytes 6148
  400.9 209.9 %copy-start.6 = (bf16[512,1,256]{2,0,1:T(8,128)(2,1)S(1)}, bf16[512,1,256]{2,0,1:T(8,128)(2,1)}, u32[]{:S(2)}) copy-start(bf16[512,1,256]{2,0,1:T(8,128)(2,1)} %copy-done.5) | copy-start | bytes 786436
  408.8 204.5 %copy-start.4 = (bf16[1024,576]{0,1:T(8,128)(2,1)S(1)}, bf16[1024,576]{0,1:T(8,128)(2,1)}, u32[]{:S(2)}) copy-start(bf16[1024,576]{0,1:T(8,128)(2,1)} %copy.98) | copy-start | bytes 3538948
  408.8 411.6 %reduce-scatter.6.cloned.1.call-start = ((), (), s32[]{:S(2)}) async-start(), calls=%async_computation.6 | async-start | bytes 557056 | tf_op jit(solution)/shard_map/reduce_scatter | solution.py:195
Sparse Core Ops, SparseCore 0:
  132.3 83.5 all-gather.4
  218.9 91.5 all-gather.8
  313.7 87.1 all-gather.6
  409.0 201.8 reduce-scatter.3
  615.7 204.7 reduce-scatter.5
where the time goes:
time: 833 us; the launch traced here: 828 us
  waiting for transfers between devices  466 us (56%)
  blocking collectives  277 us (33%)
  matrix products  33.8 us (4%)
  local copies, waits for them, and re-layouts  23.3 us (3%)
  between operations  14.2 us (2%)
  other arithmetic  13.2 us (2%)
    reduce_scatter x1, waiting for transfers between devices, per_device(): lax.psum_scatter(jnp.dot(head_out, out_full, preferred_element_type=jnp.f...  204 us
    reduce_scatter x1, waiting for transfers between devices, per_device(): lax.psum_scatter(partial_v.astype(jnp.bfloat16), 'mp', scatter_dimension=...  199 us
    unnamed x1, blocking collectives  60.2 us
    all_gather x1, waiting for transfers between devices, per_device(): value_all = lax.all_gather(up_maps[:, :, NOPE:], 'mp', axis=1, tiled=True)  53.5 us
    all_gather x1, blocking collectives, per_device(): lax.all_gather(q_weight, 'dp', axis=0, tiled=True)  44.4 us
    all_gather x1, blocking collectives, per_device(): full_x = lax.all_gather(hidden, 'mp', axis=1, tiled=True)  44 us
    all_gather x1, blocking collectives, per_device(): down_cols = lax.all_gather(dkv_weight, 'dp', axis=1, tiled=True)  32.6 us
    all_gather x1, blocking collectives, per_device(): out_full = lax.all_gather(out_weight, 'dp', axis=1, tiled=True)  32.5 us
  transfers between devices with their start and end apart: 5, of which 4 were waited for; matrix products, arithmetic and copies ran while one was open for 7% of the time, Pallas kernels for 0%

commit v1 on v0

v1 whole, which is shorter than its diff:
```python
import jax
import jax.numpy as jnp
from jax import lax
from jax.experimental import pallas as pl
from jax.experimental.pallas import tpu as pltpu
from jax.sharding import Mesh, PartitionSpec as P

NOPE = 128
ROPE = 64
LAT = 512
WIDTH = LAT + ROPE
AXES = ("y", "xl", "c", "zh", "zl", "xh")
DP = ("y", "xl", "c")
MP = ("zh", "zl", "xh")
Z = ("zh", "zl")
SCALE2 = (NOPE + ROPE) ** (-0.5) * 1.4426950408889634
NEG = -1e30
BF = jnp.bfloat16
F32 = jnp.float32


def tree_reach(parent_row):
    count = parent_row.shape[0]
    index = jnp.arange(count, dtype=jnp.int32)
    linked = jnp.logical_or(
        parent_row[:, None] == index[None, :], index[:, None] == index[None, :]
    ).astype(F32)
    for _ in range(max(1, (count - 1).bit_length())):
        linked = jnp.minimum(
            jnp.dot(linked.astype(BF), linked.astype(BF), preferred_element_type=F32), 1.0
        )
    return linked


def swap(x, axis):
    return lax.ppermute(x, axis, [(0, 1), (1, 0)])


def both(x, axis):
    other = swap(x, axis)
    first = lax.axis_index(axis) == 0
    return jnp.stack([jnp.where(first, x, other), jnp.where(first, other, x)])


def split3(v):
    hi = v.astype(BF)
    rest = v - hi.astype(F32)
    mid = rest.astype(BF)
    low = (rest - mid.astype(F32)).astype(BF)
    return [hi.astype(F32), mid.astype(F32), low.astype(F32)]


def attn_kernel(q_ref, k1_ref, k2_ref, bias_ref, o_ref, vt_ref):
    half = k1_ref.shape[0]

    @pl.when(pl.program_id(0) == 0)
    def _():
        vt_ref[:, :half] = k1_ref[:, :LAT].T
        vt_ref[:, half:] = k2_ref[:, :LAT].T

    q = jnp.concatenate([q_ref[0, :WIDTH, :], q_ref[1, :WIDTH, :]], axis=1)
    b1 = bias_ref[:half, :]
    b2 = bias_ref[half:, :]
    s1 = jnp.dot(k1_ref[...], q, preferred_element_type=F32) * SCALE2
    s2 = jnp.dot(k2_ref[...], q, preferred_element_type=F32) * SCALE2
    s1 = s1 + jnp.concatenate([b1, b1], axis=1)
    s2 = s2 + jnp.concatenate([b2, b2], axis=1)
    top = jnp.maximum(jnp.max(s1, axis=0, keepdims=True), jnp.max(s2, axis=0, keepdims=True))
    p1 = jnp.exp2(s1 - top)
    p2 = jnp.exp2(s2 - top)
    total = jnp.sum(p1, axis=0, keepdims=True) + jnp.sum(p2, axis=0, keepdims=True)
    out = jnp.dot(vt_ref[:, :half], p1.astype(BF), preferred_element_type=F32)
    out = out + jnp.dot(vt_ref[:, half:], p2.astype(BF), preferred_element_type=F32)
    stats = jnp.concatenate(
        split3(top) + split3(total) + [jnp.zeros((10, top.shape[1]), F32)], axis=0
    ).astype(BF)
    out = out.astype(BF)
    for h in range(2):
        o_ref[h, :LAT, :] = out[:, h * 128 : (h + 1) * 128]
        o_ref[h, LAT:, :] = stats[:, h * 128 : (h + 1) * 128]


def attend(queries, keys1, keys2, bias):
    heads, rows, lanes = queries.shape
    n1 = keys1.shape[0]
    return pl.pallas_call(
        attn_kernel,
        grid=(heads // 2,),
        in_specs=[
            pl.BlockSpec((2, rows, lanes), lambda i: (i, 0, 0)),
            pl.BlockSpec((n1, WIDTH), lambda i: (0, 0)),
            pl.BlockSpec((n1, WIDTH), lambda i: (0, 0)),
            pl.BlockSpec((2 * n1, lanes), lambda i: (0, 0)),
        ],
        out_specs=pl.BlockSpec((2, LAT + 16, lanes), lambda i: (i, 0, 0)),
        out_shape=jax.ShapeDtypeStruct((heads, LAT + 16, lanes), BF),
        scratch_shapes=[pltpu.VMEM((LAT, 2 * n1), BF)],
        compiler_params=pltpu.CompilerParams(vmem_limit_bytes=48 * 1024 * 1024),
        name="cache_attention",
    )(queries, keys1, keys2, bias)


def merge_kernel(part_ref, q_ref, comp_ref, gain_ref, cos_ref, sin_ref, tb_ref, vt_ref, ow_ref, o_ref, f_ref):
    lat = comp_ref[:LAT, :]
    mean = jnp.mean(lat * lat, axis=0, keepdims=True)
    normed = lat * lax.rsqrt(mean + 1e-06) * gain_ref[...]
    first = comp_ref[LAT : LAT + ROPE // 2, :]
    second = comp_ref[LAT + ROPE // 2 :, :]
    cosine = cos_ref[...]
    sine = sin_ref[...]
    fresh32 = jnp.concatenate(
        [normed, first * cosine - second * sine, second * cosine + first * sine], axis=0
    )
    fresh_t = fresh32.astype(BF)
    fresh = fresh32.T.astype(BF)
    f_ref[...] = fresh
    scores = jnp.dot(fresh, q_ref[...], preferred_element_type=F32) * SCALE2 + tb_ref[...]
    top = jnp.max(scores, axis=0, keepdims=True)
    parts = part_ref.shape[0]
    tops = []
    sums = []
    for i in range(parts):
        stats = part_ref[i, LAT:, :].astype(F32)
        tops.append(stats[0:1] + stats[1:2] + stats[2:3])
        sums.append(stats[3:4] + stats[4:5] + stats[5:6])
        top = jnp.maximum(top, tops[i])
    weights = jnp.exp2(scores - top)
    total = jnp.sum(weights, axis=0, keepdims=True)
    acc = jnp.dot(fresh_t[:LAT], weights.astype(BF), preferred_element_type=F32)
    for i in range(parts):
        factor = jnp.exp2(tops[i] - top)
        total = total + sums[i] * factor
        acc = acc + part_ref[i, :LAT, :].astype(F32) * factor
    acc = (acc / total).astype(BF)
    head = jnp.dot(vt_ref[...], acc, preferred_element_type=F32)
    head = head.T.astype(BF)
    o_ref[...] = lax.dot_general(
        head, ow_ref[...], (((1,), (1,)), ((), ())), preferred_element_type=F32
    ).astype(BF)


def merge(parts, q_own, comp, gain, cosine, sine, tree_bias, value_t, out_t):
    tokens = q_own.shape[1]
    return pl.pallas_call(
        merge_kernel,
        out_shape=(
            jax.ShapeDtypeStruct((tokens, out_t.shape[0]), BF),
            jax.ShapeDtypeStruct((tokens, WIDTH), BF),
        ),
        compiler_params=pltpu.CompilerParams(vmem_limit_bytes=48 * 1024 * 1024),
        name="merge_project",
    )(parts, q_own, comp, gain, cosine, sine, tree_bias, value_t, out_t)


def per_device(
    hidden,
    q_weight,
    dkv_weight,
    latent_gain,
    kvb_weight,
    out_weight,
    cache,
    cache_len,
    draft_count,
    parents,
    accept_node,
    page_table,
):
    reqs, draft = parents.shape
    tokens = reqs * draft
    slots, page_len, width = cache.shape
    z_rank = lax.axis_index(Z)
    mp_rank = lax.axis_index(MP)
    keys = cache.reshape(slots * page_len, width)
    rows = jnp.concatenate([hidden, dkv_weight.T], axis=0)
    pair = both(rows, "xh")
    keys_other = swap(keys, "xh")
    hid = jnp.concatenate([pair[0, :tokens], pair[1, :tokens]], axis=1)
    cols = dkv_weight.shape[1]
    pack = jnp.concatenate(
        [
            q_weight[:, :NOPE],
            jnp.concatenate([q_weight[:32, NOPE:], q_weight[32:, NOPE:]], axis=1),
            kvb_weight[:, 0, :NOPE],
            kvb_weight[:, 0, NOPE:],
            out_weight.T,
            pair[0, tokens:],
            pair[1, tokens:],
            jnp.zeros((12, 128), BF),
        ],
        axis=0,
    )
    wide = lax.all_to_all(jnp.broadcast_to(pack[None], (8,) + pack.shape), "y", 0, 0, tiled=True)
    wide = both(both(wide, "xl"), "c")
    wide = wide.transpose(2, 1, 0, 3, 4)
    w_plain = wide[..., :64, :].reshape(2048, 128)
    w_rot = wide[..., 64:96, :]
    w_rot = jnp.concatenate([w_rot, w_rot], axis=3).reshape(2048, 128)
    key_map = wide[..., 96:112, :].reshape(LAT, NOPE)
    value_t = wide[..., 112:128, :].reshape(LAT, 128).T
    out_t = wide[..., 128:192, :].reshape(2048, 128)
    down = jnp.concatenate(
        [wide[..., 192 : 192 + cols, :], wide[..., 192 + cols : 192 + 2 * cols, :]], axis=4
    ).reshape(8, 4 * cols, 256)
    sent = jnp.concatenate([jnp.broadcast_to(hid[None], (8,) + hid.shape), down], axis=1)
    got = lax.all_to_all(sent, Z, 0, 0, tiled=True)
    full_x = got[:, :tokens].transpose(1, 0, 2).reshape(tokens, 2048)
    down_t = got[:, tokens:].transpose(1, 0, 2).reshape(4 * cols, 2048)
    linked = jax.vmap(tree_reach)(parents)
    depth = jnp.sum(linked, axis=2) - 1.0
    positions = (cache_len.astype(F32)[:, None] + depth).reshape(1, tokens)
    inverse = 10000.0 ** (-(jnp.arange(ROPE // 2, dtype=F32) * 2.0) / ROPE)
    phase = positions * inverse[:, None]
    cosine = jnp.cos(phase)
    sine = jnp.sin(phase)
    q_plain = jnp.dot(full_x, w_plain, preferred_element_type=F32).astype(BF)
    early = (jnp.arange(2048) % 64 < 32)[None, :]
    zero = jnp.zeros((), BF)
    rot_a = jnp.dot(jnp.where(early, full_x, zero), w_rot, preferred_element_type=F32)
    rot_b = jnp.dot(jnp.where(early, zero, full_x), w_rot, preferred_element_type=F32)
    q_rot = (rot_a[:, :ROPE] + rot_b[:, ROPE:]).T.astype(BF).astype(F32)
    q_lat = lax.dot_general(
        key_map, q_plain, (((1,), (1,)), ((), ())), preferred_element_type=F32
    )
    r1 = q_rot[: ROPE // 2]
    r2 = q_rot[ROPE // 2 :]
    q_own = jnp.concatenate(
        [q_lat, r1 * cosine - r2 * sine, r2 * cosine + r1 * sine], axis=0
    ).astype(BF)
    comp = lax.dot_general(
        down_t, full_x, (((1,), (1,)), ((), ())), preferred_element_type=F32
    ).astype(BF)
    packed = jnp.concatenate([q_own, comp, jnp.zeros((8, tokens), BF)], axis=0)
    queries = lax.all_to_all(
        jnp.broadcast_to(packed[None], (8,) + packed.shape), Z, 0, 0, tiled=True
    )
    slot_base = jnp.stack([mp_rank, mp_rank ^ 1]) * slots
    slot_ids = (slot_base[:, None] + jnp.arange(slots, dtype=jnp.int32)[None, :]).reshape(-1)
    page_ids = jnp.arange(reqs * page_table.shape[1], dtype=jnp.int32)
    place = jnp.sum(
        jnp.where(page_table.reshape(-1)[:, None] == slot_ids[None, :], page_ids[:, None], 0), axis=0
    )
    slot_req = place // page_table.shape[1]
    slot_page = place % page_table.shape[1]
    token_req = jnp.arange(tokens, dtype=jnp.int32) // draft
    token_len = jnp.repeat(cache_len, draft)
    key_pos = slot_page[:, None] * page_len + jnp.arange(page_len, dtype=jnp.int32)[None, :]
    same = slot_req[:, None, None] == token_req[None, None, :]
    offset = key_pos[:, :, None] - token_len[None, None, :]
    bias = jnp.where(jnp.logical_and(same, offset < 0), 0.0, NEG).astype(F32)
    bias = bias.reshape(2 * slots * page_len, tokens)
    accept_hot = (accept_node[:, None] == jnp.arange(draft, dtype=jnp.int32)[None, :]).astype(F32)
    path = jnp.sum(accept_hot[:, :, None] * linked, axis=1).reshape(tokens)
    write_at = jnp.where(path > 0.5, depth.reshape(tokens).astype(jnp.int32), -1)
    chosen = jnp.logical_and(
        same[:slots],
        jnp.logical_and(write_at[None, None, :] >= 0, offset[:slots] == write_at[None, None, :]),
    )
    chosen = chosen.reshape(slots * page_len, tokens).astype(BF)
    partial = attend(queries, keys, keys_other, bias)
    partial = lax.all_to_all(partial, Z, 0, 0, tiled=True)
    comp_all = queries[:, WIDTH : WIDTH + 4 * cols].reshape(WIDTH, tokens).astype(F32)
    linked_t = linked.transpose(0, 2, 1)
    blank = jnp.zeros((draft, draft), F32)
    tree_live = jnp.concatenate(
        [
            jnp.concatenate([linked_t[0], blank], axis=1),
            jnp.concatenate([blank, linked_t[1]], axis=1),
        ],
        axis=0,
    )
    tree_bias = jnp.where(tree_live > 0.5, 0.0, NEG).astype(F32)
    gain = jnp.broadcast_to(latent_gain[:, None], (LAT, tokens))
    projected, fresh = merge(
        partial, q_own, comp_all, gain, cosine, sine, tree_bias, value_t, out_t
    )
    shares = lax.all_to_all(projected.reshape(16, tokens // 16, 2048), MP, 0, 0, tiled=True)
    mine_rows = jnp.sum(shares.astype(F32), axis=0)
    row_index = mp_rank * (tokens // 16) + jnp.arange(tokens // 16, dtype=jnp.int32)
    row_count = jnp.sum(
        jnp.where(
            (row_index // draft)[:, None] == jnp.arange(reqs, dtype=jnp.int32)[None, :],
            draft_count[None, :],
            0,
        ),
        axis=1,
    )
    attended = jnp.where((row_index % draft < row_count)[:, None], mine_rows, 0.0).astype(BF)
    placed = jnp.dot(chosen, fresh, preferred_element_type=F32).astype(BF)
    written = jnp.sum(chosen.astype(F32), axis=1, keepdims=True) > 0.5
    new_cache = jnp.where(written, placed, keys).reshape(cache.shape)
    return (attended, new_cache)


def solution(mesh):
    grid = Mesh(mesh.devices.reshape(8, 2, 2, 2, 4, 2), AXES)
    return jax.shard_map(
        per_device,
        mesh=grid,
        in_specs=(
            P(DP, MP),
            P(DP, MP),
            P(MP, DP),
            P(),
            P(DP, MP, None),
            P(MP, DP),
            P(DP + MP, None, None),
            P(DP),
            P(DP),
            P(DP, None),
            P(DP),
            P(DP, None),
        ),
        out_specs=(P(DP + MP, None), P(DP + MP, None, None)),
        check_vma=False,
    )
```

time: 833 us -> 220 us (0.26)
  waiting for transfers between devices: 466 us -> 99 us
  blocking collectives: 277 us -> 20 us
  starting transfers between devices: 0.21 us -> 42.9 us
  matrix products: 33.8 us -> 7.77 us
  Pallas kernels: 0 us -> 15.7 us
  between operations: 14.2 us -> 1.12 us
    reduce_scatter x2 -> x0, waiting for transfers between devices: 403 us -> none  [the longest x1 204 us: per_device(): lax.psum_scatter(jnp.dot(head_out, out_full, preferred_element_type=jnp.f...]
    all_gather x5 -> x0, blocking collectives: 185 us -> none  [the longest x1 44.4 us: per_device(): lax.all_gather(q_weight, 'dp', axis=0, tiled=True)]
    all_to_all x0 -> x4, waiting for transfers between devices: none -> 64.9 us  [the longest x1 26 us: per_device(): partial = lax.all_to_all(partial, Z, 0, 0, tiled=True)]
    all_gather x3 -> x0, waiting for transfers between devices: 63.7 us -> none  [the longest x1 53.5 us: per_device(): value_all = lax.all_gather(up_maps[:, :, NOPE:], 'mp', axis=1, tiled=True)]
    unnamed x1 -> x0, blocking collectives: 60.2 us -> none
    ppermute x0 -> x4, waiting for transfers between devices: none -> 34 us  [swap(): return lax.ppermute(x, axis, [(0, 1), (1, 0)])]
    pmax x1 -> x0, blocking collectives: 32.2 us -> none  [per_device(): global_top = lax.pmax(local_top, 'mp')]
    dot_general x21 -> x8, matrix products: 33.8 us -> 7.77 us  [the longest x1 1.62 us: per_device(): jnp.dot(jnp.where(early, zero, full_x), w_rot, preferred_element_type=F32)]
  transfers between devices with their start and end apart: 5 -> 8, of which waited for: 4 -> 7; matrix products, arithmetic and copies ran while one was open for 7% -> 8% of each run, Pallas kernels for 0% -> 0%
where the time goes in v1:
time: 220 us; the launch traced here: 218 us
  waiting for transfers between devices  99 us (45%)
  starting transfers between devices  42.9 us (20%)
  blocking collectives  20 us (9%)
  local copies, waits for them, and re-layouts  19 us (9%)
  Pallas kernels  15.7 us (7%)
  other arithmetic  13 us (6%)
  matrix products  7.77 us (4%)
    ppermute x4, waiting for transfers between devices, swap(): return lax.ppermute(x, axis, [(0, 1), (1, 0)])  34 us
    all_to_all x1, waiting for transfers between devices, per_device(): partial = lax.all_to_all(partial, Z, 0, 0, tiled=True)  26 us
    all_to_all x1, waiting for transfers between devices, per_device(): got = lax.all_to_all(sent, Z, 0, 0, tiled=True)  22.7 us
    all_to_all x1, blocking collectives, per_device(): lax.all_to_all(jnp.broadcast_to(pack[None], (8,) + pack.shape), 'y', 0, 0...  20 us
    ppermute x4, starting transfers between devices, swap(): return lax.ppermute(x, axis, [(0, 1), (1, 0)])  18.8 us
    all_to_all x1, waiting for transfers between devices, per_device(): lax.all_to_all(projected.reshape(16, tokens // 16, 2048), MP, 0, 0, tiled...  15.4 us
    pallas_call x1, Pallas kernels, attend(): pl.pallas_call(attn_kernel, grid=(heads // 2,), in_specs=[pl.BlockSpec((2...  12.5 us
    all_to_all x1, starting transfers between devices, per_device(): got = lax.all_to_all(sent, Z, 0, 0, tiled=True)  11.3 us
  transfers between devices with their start and end apart: 8, of which 7 were waited for; matrix products, arithmetic and copies ran while one was open for 8% of the time, Pallas kernels for 0%

profile of v1, /device:TPU:1, one launch (start us, length us, event | category | flops | bytes accessed | tf_op | source)
XLA Modules:
  0.0 218.4 jit_solution(446723589818400713)
XLA Ops:
  1.4 5.5 %collective-permute-start = (bf16[146,128]{1,0:T(8,128)(2,1)S(1)}, bf16[146,128]{1,0:T(8,128)(2,1)S(1)}, u32[]{:S(2)}, u32[]{:S(2)}) collective-permute-start(bf16[146,128]{1,0:T(8,128)(2,1)S(1)} %pad_maximum_fusion.6), channel_id=1, source_target_pairs={{0,1},{1,0},{2,3},{3,2},{4,5},{5,4},{6,7},{7,6},{8,9},{9,8},{10,11... | collective-permute-start | bytes 112136 | tf_op jit(solution)/shard_map/ppermute | solution.py:36
  11.0 20.0 %all_to_all.25 = bf16[8,240,128]{2,1,0:T(8,128)(2,1)S(1)} all-to-all(bf16[8,240,128]{2,1,0:T(8,128)(2,1)S(1)} %broadcast_in_dim.148), channel_id=1, replica_groups=mesh['y'=8,'xl'=2,'c'=2,'zh'=2,'zl'=4,'xh'=2] {'y'}, dimensions={0} | all-to-all | bytes 983040 | tf_op jit(solution)/shard_map/all_to_all | solution.py:193
  31.0 3.0 %collective-permute-start.1 = (bf16[8,240,128]{2,1,0:T(8,128)(2,1)S(1)}, bf16[8,240,128]{2,1,0:T(8,128)(2,1)S(1)}, u32[]{:S(2)}, u32[]{:S(2)}) collective-permute-start(bf16[8,240,128]{2,1,0:T(8,128)(2,1)S(1)} %all_to_all.25), channel_id=1, source_target_pairs={{0,32},{32,0},{1,33},{33,1},{2,34},{34,2},{3,35},{35,3},{4,36},{36... | collective-permute-start | bytes 1474568 | tf_op jit(solution)/shard_map/ppermute | solution.py:36
  34.0 7.2 %collective-permute-done.1 = bf16[8,240,128]{2,1,0:T(8,128)(2,1)S(1)} collective-permute-done((bf16[8,240,128]{2,1,0:T(8,128)(2,1)S(1)}, bf16[8,240,128]{2,1,0:T(8,128)(2,1)S(1)}, u32[]{:S(2)}, u32[]{:S(2)}) %collective-permute-start.1) | collective-permute-done | bytes 491552 | tf_op jit(solution)/shard_map/ppermute | solution.py:36
  41.4 7.2 %collective-permute-start.2 = (bf16[2,8,240,128]{3,2,0,1:T(8,128)(2,1)S(1)}, bf16[2,8,240,128]{3,2,0,1:T(8,128)(2,1)S(1)}, u32[]{:S(2)}, u32[]{:S(2)}) collective-permute-start(bf16[2,8,240,128]{3,2,0,1:T(8,128)(2,1)S(1)} %pad_maximum_fusion), channel_id=1, source_target_pairs={{0,16},{16,0},{1,17},{17,1},{2,18},{18,2},{3,19},{19,3},{4,20},{20... | collective-permute-start | bytes 2949128 | tf_op jit(solution)/shard_map/ppermute | solution.py:36
  49.4 1.4 collective-permute-done.2
  52.5 11.3 %all-to-all-start.1 = ((bf16[8,200,256]{2,1,0:T(8,128)(2,1)}), bf16[8,200,256]{2,1,0:T(8,128)(2,1)}, u32[]{:S(2)}, u32[]{:S(2)}) async-start(bf16[8,200,256]{2,1,0:T(8,128)(2,1)} %pad_maximum_fusion.1), calls=%async_computation.1 | async-start | bytes 1638400 | tf_op jit(solution)/shard_map/all_to_all | solution.py:206
  65.6 22.7 %all-to-all-done.1 = bf16[8,200,256]{2,1,0:T(8,128)(2,1)} async-done(((bf16[8,200,256]{2,1,0:T(8,128)(2,1)}), bf16[8,200,256]{2,1,0:T(8,128)(2,1)}, u32[]{:S(2)}, u32[]{:S(2)}) %all-to-all-start.1) | async-done | bytes 819232 | tf_op jit(solution)/shard_map/all_to_all | solution.py:206
  92.8 1.5 fusion.14
  94.3 1.6 fusion.10
  98.0 1.4 fusion.7
  100.7 3.7 %all-to-all-start.2 = ((bf16[8,656,128]{2,1,0:T(8,128)(2,1)}), bf16[8,656,128]{2,1,0:T(8,128)(2,1)S(1)}, u32[]{:S(2)}, u32[]{:S(2)}) async-start(bf16[8,656,128]{2,1,0:T(8,128)(2,1)} %broadcast_in_dim.153), calls=%async_computation.2 | async-start | bytes 2686976 | tf_op jit(solution)/shard_map/all_to_all | solution.py:234
  104.5 1.4 copy.98
  105.9 3.2 %collective-permute-start.3 = (bf16[1024,576]{0,1:T(8,128)(2,1)}, bf16[1024,576]{0,1:T(8,128)(2,1)}, u32[]{:S(2)}, u32[]{:S(2)}) collective-permute-start(bf16[1024,576]{0,1:T(8,128)(2,1)} %copy.98), channel_id=1, source_target_pairs={{0,1},{1,0},{2,3},{3,2},{4,5},{5,4},{6,7},{7,6},{8,9},{9,8},{10,11... | collective-permute-start | bytes 3538952 | tf_op jit(solution)/shard_map/ppermute | solution.py:36
  111.2 25.4 %collective-permute-done.3 = bf16[1024,576]{0,1:T(8,128)(2,1)} collective-permute-done((bf16[1024,576]{0,1:T(8,128)(2,1)}, bf16[1024,576]{0,1:T(8,128)(2,1)}, u32[]{:S(2)}, u32[]{:S(2)}) %collective-permute-start.3) | collective-permute-done | bytes 1179680 | tf_op jit(solution)/shard_map/ppermute | solution.py:36
  136.6 2.4 %copy.99.k2_ref = bf16[1024,576]{1,0:T(8,128)(2,1)} copy(bf16[1024,576]{0,1:T(8,128)(2,1)} %collective-permute-done.3) | data formatting | bytes 2359296 | tf_op jit(solution)/shard_map/ppermute | solution.py:36
  142.4 12.5 %cache_attention.1 = bf16[8,528,128]{2,1,0:T(8,128)(2,1)S(1)} custom-call(bf16[8,656,128]{2,1,0:T(8,128)(2,1)S(1)} %all-to-all-done.2.q_ref, bf16[1024,576]{1,0:T(8,128)(2,1)S(1)} %bitcast.92, bf16[1024,576]{1,0:T(8,128)(2,1)S(1)} %copy-done.1, f32[2048,128]{1,0:T(8,128)S(1)} %copy-done.3), custom_call_target="tpu_custom_call" | custom-call | tf_op jit(solution)/shard_map/cache_attention/pallas_call | solution.py:86
  155.9 5.4 %all-to-all-start.3 = ((bf16[8,528,128]{2,1,0:T(8,128)(2,1)}), bf16[8,528,128]{2,1,0:T(8,128)(2,1)}, u32[]{:S(2)}, u32[]{:S(2)}) async-start(bf16[8,528,128]{2,1,0:T(8,128)(2,1)} %copy-done.2), calls=%async_computation.3 | async-start | bytes 2162688 | tf_op jit(solution)/shard_map/all_to_all | solution.py:261
  163.8 1.4 pad_maximum_fusion.4.q_ref
  165.2 26.0 %all-to-all-done.3.part_ref = bf16[8,528,128]{2,1,0:T(8,128)(2,1)} async-done(((bf16[8,528,128]{2,1,0:T(8,128)(2,1)}), bf16[8,528,128]{2,1,0:T(8,128)(2,1)}, u32[]{:S(2)}, u32[]{:S(2)}) %all-to-all-start.3) | async-done | bytes 1081376 | tf_op jit(solution)/shard_map/all_to_all | solution.py:261
  193.2 3.2 %merge_project.1 = (bf16[128,2048]{1,0:T(8,128)(2,1)}, bf16[128,576]{1,0:T(8,128)(2,1)S(1)}) custom-call(bf16[8,528,128]{2,1,0:T(8,128)(2,1)} %all-to-all-done.3.part_ref, bf16[576,128]{1,0:T(8,128)(2,1)S(1)} %copy-done.4, f32[576,128]{1,0:T(8,128)S(1)} %bitcast_convert_fusion.comp_ref, f32[512,128]{1,0:T(8,128)S(1)} %broadcast_in_dim.159.gain_ref, ...), custom_call_target="tpu_custom_call" | custom-call | tf_op jit(solution)/shard_map/merge_project/pallas_call | solution.py:144
  196.5 3.6 %all-to-all-start.4 = ((bf16[16,8,2048]{2,1,0:T(8,128)(2,1)}), bf16[16,8,2048]{2,1,0:T(8,128)(2,1)S(1)}, u32[]{:S(2)}, u32[]{:S(2)}) async-start(bf16[16,8,2048]{2,1,0:T(8,128)(2,1)} %bitcast.40), calls=%async_computation.4 | async-start | bytes 1048576 | tf_op jit(solution)/shard_map/all_to_all | solution.py:277
  200.7 1.6 fusion
  202.3 15.4 %all-to-all-done.4 = bf16[16,8,2048]{2,1,0:T(8,128)(2,1)S(1)} async-done(((bf16[16,8,2048]{2,1,0:T(8,128)(2,1)}), bf16[16,8,2048]{2,1,0:T(8,128)(2,1)S(1)}, u32[]{:S(2)}, u32[]{:S(2)}) %all-to-all-start.4) | async-done | bytes 524320 | tf_op jit(solution)/shard_map/all_to_all | solution.py:277
  (121 shorter events, 29.2 us)
Async XLA Ops:
  1.4 7.7 %collective-permute-start = (bf16[146,128]{1,0:T(8,128)(2,1)S(1)}, bf16[146,128]{1,0:T(8,128)(2,1)S(1)}, u32[]{:S(2)}, u32[]{:S(2)}) collective-permute-start(bf16[146,128]{1,0:T(8,128)(2,1)S(1)} %pad_maximum_fusion.6), channel_id=1, source_target_pairs={{0,1},{1,0},{2,3},{3,2},{4,5},{5,4},{6,7},{7,6},{8,9},{9,8},{10,11... | collective-permute-start | bytes 112136 | tf_op jit(solution)/shard_map/ppermute | solution.py:36
  31.0 10.2 %collective-permute-start.1 = (bf16[8,240,128]{2,1,0:T(8,128)(2,1)S(1)}, bf16[8,240,128]{2,1,0:T(8,128)(2,1)S(1)}, u32[]{:S(2)}, u32[]{:S(2)}) collective-permute-start(bf16[8,240,128]{2,1,0:T(8,128)(2,1)S(1)} %all_to_all.25), channel_id=1, source_target_pairs={{0,32},{32,0},{1,33},{33,1},{2,34},{34,2},{3,35},{35,3},{4,36},{36... | collective-permute-start | bytes 1474568 | tf_op jit(solution)/shard_map/ppermute | solution.py:36
  41.3 7.3 %copy-start.18 = (s32[2]{0:T(128)S(1)}, s32[2]{0:T(128)}, u32[]{:S(2)}) copy-start(s32[2]{0:T(128)} %param.19) | copy-start | bytes 28
  41.3 7.4 %copy-start.16 = (s32[2,64]{1,0:T(2,128)S(1)}, s32[2,64]{1,0:T(2,128)}, u32[]{:S(2)}) copy-start(s32[2,64]{1,0:T(2,128)} %param.21) | copy-start | bytes 1540
  41.4 9.4 %collective-permute-start.2 = (bf16[2,8,240,128]{3,2,0,1:T(8,128)(2,1)S(1)}, bf16[2,8,240,128]{3,2,0,1:T(8,128)(2,1)S(1)}, u32[]{:S(2)}, u32[]{:S(2)}) collective-permute-start(bf16[2,8,240,128]{3,2,0,1:T(8,128)(2,1)S(1)} %pad_maximum_fusion), channel_id=1, source_target_pairs={{0,16},{16,0},{1,17},{17,1},{2,18},{18,2},{3,19},{19,3},{4,20},{20... | collective-permute-start | bytes 2949128 | tf_op jit(solution)/shard_map/ppermute | solution.py:36
  51.6 12.3 %copy-start.17 = (s32[2]{0:T(128)S(1)}, s32[2]{0:T(128)}, u32[]{:S(2)}) copy-start(s32[2]{0:T(128)} %param.22) | copy-start | bytes 28
  52.5 35.8 %all-to-all-start.1 = ((bf16[8,200,256]{2,1,0:T(8,128)(2,1)}), bf16[8,200,256]{2,1,0:T(8,128)(2,1)}, u32[]{:S(2)}, u32[]{:S(2)}) async-start(bf16[8,200,256]{2,1,0:T(8,128)(2,1)} %pad_maximum_fusion.1), calls=%async_computation.1 | async-start | bytes 1638400 | tf_op jit(solution)/shard_map/all_to_all | solution.py:206
  64.5 32.8 %copy-start.8 = (f32[128]{0:T(128)}, f32[128]{0:T(128)S(1)}, u32[]{:S(2)}) copy-start(f32[128]{0:T(128)S(1)} %add.156) | copy-start | bytes 1540
  64.5 32.8 %copy-start.9 = (f32[32]{0:T(128)}, f32[32]{0:T(128)S(1)}, u32[]{:S(2)}) copy-start(f32[32]{0:T(128)S(1)} %multiply_power_fusion) | copy-start | bytes 388
  91.8 2.5 %copy-start.6 = (bf16[8,2,2,64,128]{4,3,2,1,0:T(8,128)(2,1)S(1)}, bf16[8,2,2,64,128]{4,3,2,1,0:T(8,128)(2,1)}, u32[]{:S(2)}) copy-start(bf16[8,2,2,64,128]{4,3,2,1,0:T(8,128)(2,1)} %pad_maximum_fusion.2) | copy-start | bytes 1572868
  100.7 3.7 %copy-start = (bf16[16,64,576]{2,1,0:T(8,128)(2,1)S(1)}, bf16[16,64,576]{2,1,0:T(8,128)(2,1)}, u32[]{:S(2)}) copy-start(bf16[16,64,576]{2,1,0:T(8,128)(2,1)} %param.18) | copy-start | bytes 3538948
  100.7 39.1 %all-to-all-start.2 = ((bf16[8,656,128]{2,1,0:T(8,128)(2,1)}), bf16[8,656,128]{2,1,0:T(8,128)(2,1)S(1)}, u32[]{:S(2)}, u32[]{:S(2)}) async-start(bf16[8,656,128]{2,1,0:T(8,128)(2,1)} %broadcast_in_dim.153), calls=%async_computation.2 | async-start | bytes 2686976 | tf_op jit(solution)/shard_map/all_to_all | solution.py:234
  104.4 5.0 %copy-start.15 = (s32[2,128]{1,0:T(2,128)S(1)}, s32[2,128]{1,0:T(2,128)}, u32[]{:S(2)}) copy-start(s32[2,128]{1,0:T(2,128)} %param.23) | copy-start | bytes 3076
  105.9 30.7 %collective-permute-start.3 = (bf16[1024,576]{0,1:T(8,128)(2,1)}, bf16[1024,576]{0,1:T(8,128)(2,1)}, u32[]{:S(2)}, u32[]{:S(2)}) collective-permute-start(bf16[1024,576]{0,1:T(8,128)(2,1)} %copy.98), channel_id=1, source_target_pairs={{0,1},{1,0},{2,3},{3,2},{4,5},{5,4},{6,7},{7,6},{8,9},{9,8},{10,11... | collective-permute-start | bytes 3538952 | tf_op jit(solution)/shard_map/ppermute | solution.py:36
  109.2 29.8 %copy-start.11 = (s32[128]{0:T(128)}, s32[128]{0:T(128)S(1)}, u32[]{:S(2)}) copy-start(s32[128]{0:T(128)S(1)} %sub.53) | copy-start | bytes 1540
  109.7 29.4 %copy-start.13 = (s32[32]{0:T(128)}, s32[32]{0:T(128)S(1)}, u32[]{:S(2)}) copy-start(s32[32]{0:T(128)S(1)} %get-tuple-element.36) | copy-start | bytes 388
  109.7 51.5 %copy-start.7 = (s32[32,64]{1,0:T(8,128)}, s32[32,64]{1,0:T(8,128)S(1)}, u32[]{:S(2)}) copy-start(s32[32,64]{1,0:T(8,128)S(1)} %iota_add_fusion) | copy-start | bytes 24580
  109.8 29.2 %copy-start.14 = (s32[128]{0:T(128)}, s32[128]{0:T(128)S(1)}, u32[]{:S(2)}) copy-start(s32[128]{0:T(128)S(1)} %and_select_fusion.1) | copy-start | bytes 1540
  155.9 35.4 %all-to-all-start.3 = ((bf16[8,528,128]{2,1,0:T(8,128)(2,1)}), bf16[8,528,128]{2,1,0:T(8,128)(2,1)}, u32[]{:S(2)}, u32[]{:S(2)}) async-start(bf16[8,528,128]{2,1,0:T(8,128)(2,1)} %copy-done.2), calls=%async_computation.3 | async-start | bytes 2162688 | tf_op jit(solution)/shard_map/all_to_all | solution.py:261
  161.3 30.0 %copy-start.10 = (f32[512]{0:T(512)S(1)}, f32[512]{0:T(512)}, u32[]{:S(2)}) copy-start(f32[512]{0:T(512)} %param.15) | copy-start | bytes 6148
  193.2 6.8 %slice-start = ((s32[32,64]{1,0:T(8,128)}), s32[16,64]{1,0:T(8,128)S(1)}, s32[]{:S(2)}) async-start(s32[32,64]{1,0:T(8,128)} %copy-done.7), calls=%async_computation.5 | async-start | bytes 16384 | tf_op jit(solution)/shard_map/slice | solution.py:257
  193.2 6.8 %copy-start.12 = (s32[128]{0:T(128)S(1)}, s32[128]{0:T(128)}, u32[]{:S(2)}) copy-start(s32[128]{0:T(128)} %copy-done.11) | copy-start | bytes 1540
  193.2 7.3 %copy-start.19 = (s32[2]{0:T(128)S(1)}, s32[2]{0:T(128)}, u32[]{:S(2)}) copy-start(s32[2]{0:T(128)} %param.20) | copy-start | bytes 28
  196.5 21.2 %all-to-all-start.4 = ((bf16[16,8,2048]{2,1,0:T(8,128)(2,1)}), bf16[16,8,2048]{2,1,0:T(8,128)(2,1)S(1)}, u32[]{:S(2)}, u32[]{:S(2)}) async-start(bf16[16,8,2048]{2,1,0:T(8,128)(2,1)} %bitcast.40), calls=%async_computation.4 | async-start | bytes 1048576 | tf_op jit(solution)/shard_map/all_to_all | solution.py:277
  (5 other events, 5.3 us)

commit v2 on v1

v2 whole, which is shorter than its diff:
```python
import jax
import jax.numpy as jnp
from jax import lax
from jax.experimental import pallas as pl
from jax.experimental.pallas import tpu as pltpu
from jax.sharding import Mesh, PartitionSpec as P

NOPE = 128
ROPE = 64
LAT = 512
WIDTH = LAT + ROPE
AXES = ("y", "xl", "c", "zh", "zl", "xh")
DP = ("y", "xl", "c")
MP = ("zh", "zl", "xh")
Z = ("zh", "zl")
SIDE = 80
SCALE2 = (NOPE + ROPE) ** (-0.5) * 1.4426950408889634
NEG = -1e30
BF = jnp.bfloat16
F32 = jnp.float32


def tree_reach(parent_row):
    count = parent_row.shape[0]
    index = jnp.arange(count, dtype=jnp.int32)
    linked = jnp.logical_or(
        parent_row[:, None] == index[None, :], index[:, None] == index[None, :]
    ).astype(F32)
    for _ in range(max(1, (count - 1).bit_length())):
        linked = jnp.minimum(
            jnp.dot(linked.astype(BF), linked.astype(BF), preferred_element_type=F32), 1.0
        )
    return linked


def swap(x, axis):
    return lax.ppermute(x, axis, [(0, 1), (1, 0)])


def both(x, axis):
    other = swap(x, axis)
    first = lax.axis_index(axis) == 0
    return jnp.stack([jnp.where(first, x, other), jnp.where(first, other, x)])


def split3(v):
    hi = v.astype(BF)
    rest = v - hi.astype(F32)
    mid = rest.astype(BF)
    low = (rest - mid.astype(F32)).astype(BF)
    return [hi.astype(F32), mid.astype(F32), low.astype(F32)]


def prep_kernel(k1_ref, k2t_ref, mask_ref, k_ref, v_ref):
    half = k1_ref.shape[0]
    k_ref[:half, :WIDTH] = k1_ref[...]
    k_ref[half:, :WIDTH] = k2t_ref[...].T
    k_ref[:, WIDTH:] = mask_ref[...]
    v_ref[:, :half] = k1_ref[:, :LAT].T
    v_ref[:, half:] = k2t_ref[:LAT, :]


def prepare(keys, other_t, mask):
    n1 = keys.shape[0]
    return pl.pallas_call(
        prep_kernel,
        out_shape=(
            jax.ShapeDtypeStruct((2 * n1, WIDTH + 16), BF),
            jax.ShapeDtypeStruct((LAT, 2 * n1), BF),
        ),
        compiler_params=pltpu.CompilerParams(vmem_limit_bytes=48 * 1024 * 1024),
        name="prepare_keys",
    )(keys, other_t, mask)


def maps_kernel(w_ref, km_ref, vm_ref):
    order = [(y, xl, c) for y in range(8) for xl in range(2) for c in range(2)]
    for h in range(8):
        for n, (y, xl, c) in enumerate(order):
            km_ref[h, 16 * n : 16 * n + 16, :] = w_ref[c, xl, y, 16 * h : 16 * h + 16, :]
        value = [w_ref[c, xl, y, 128 + 16 * h : 144 + 16 * h, :] for y, xl, c in order]
        vm_ref[h] = jnp.concatenate(value, axis=0).T


def arrange(wide):
    return pl.pallas_call(
        maps_kernel,
        out_shape=(
            jax.ShapeDtypeStruct((8, LAT, 128), BF),
            jax.ShapeDtypeStruct((8, 128, LAT), BF),
        ),
        compiler_params=pltpu.CompilerParams(vmem_limit_bytes=48 * 1024 * 1024),
        name="arrange_maps",
    )(wide)


def project_kernel(x_ref, w_ref, h_ref, d_ref, cos_ref, sin_ref, o_ref):
    tokens = h_ref.shape[0]
    nt = (((1,), (1,)), ((), ()))
    part = lax.dot_general(h_ref[...], d_ref[...], nt, preferred_element_type=F32)
    part = jnp.concatenate([part, jnp.zeros((tokens, ROPE), F32)], axis=1).astype(BF)
    order = [(0, 0), (1, 0), (0, 1), (1, 1)]
    zero = jnp.zeros((32, 128), BF)
    acc = jnp.zeros((tokens, 3 * 128), F32)
    for y in range(8):
        plain = []
        rot_a = []
        rot_b = []
        for c, xl in order:
            plain.append(w_ref[c, xl, y, 0:64, :])
            rot = w_ref[c, xl, y, 64:96, :]
            rot_a += [rot, zero]
            rot_b += [zero, rot]
        weights = jnp.concatenate(
            [
                jnp.concatenate(plain, axis=0),
                jnp.concatenate(rot_a, axis=0),
                jnp.concatenate(rot_b, axis=0),
            ],
            axis=1,
        )
        acc = acc + jnp.dot(x_ref[y, :tokens], weights, preferred_element_type=F32)
    q_plain = acc[:, :128].T
    rot = acc[:, 128:256].T[:ROPE] + acc[:, 256:384].T[ROPE:]
    rot = rot.astype(BF).astype(F32)
    r1 = rot[: ROPE // 2]
    r2 = rot[ROPE // 2 :]
    cosine = cos_ref[...]
    sine = sin_ref[...]
    q_rot = jnp.concatenate([r1 * cosine - r2 * sine, r2 * cosine + r1 * sine], axis=0)
    lane = lax.broadcasted_iota(jnp.int32, (16, tokens), 1) // (tokens // 2)
    row = lax.broadcasted_iota(jnp.int32, (16, tokens), 0)
    which = jnp.where(lane == row, 1.0, 0.0)
    tail = jnp.concatenate([q_plain, q_rot, which], axis=0).astype(BF)
    for i in range(o_ref.shape[0]):
        for k in range(5):
            o_ref[i, 16 * k : 16 * k + 16, :] = part[16 * i : 16 * i + 16, 128 * k : 128 * k + 128]
        o_ref[i, SIDE:, :] = tail


def project(x, wide, own, down, cosine, sine):
    tokens = own.shape[0]
    return pl.pallas_call(
        project_kernel,
        out_shape=jax.ShapeDtypeStruct((8, SIDE + NOPE + ROPE + 16, tokens), BF),
        compiler_params=pltpu.CompilerParams(vmem_limit_bytes=48 * 1024 * 1024),
        name="project_queries",
    )(x, wide, own, down, cosine, sine)


def attn_kernel(q_ref, k_ref, v_ref, km_ref, vm_ref, part_ref, gain_ref, cos_ref, sin_ref, o_ref):
    comp = jnp.zeros((SIDE, 128), F32)
    for i in range(part_ref.shape[0]):
        for j in range(part_ref.shape[1]):
            comp = comp + part_ref[i, j].astype(F32)
    squares = jnp.zeros((16, 128), F32)
    for k in range(4):
        lat = comp[16 * k : 16 * k + 16]
        squares = squares + lat * lat
    scale = lax.rsqrt(jnp.sum(squares, axis=1, keepdims=True) * (1.0 / LAT) + 1e-06)
    fresh = [
        comp[16 * k : 16 * k + 16] * scale * gain_ref[:, 128 * k : 128 * k + 128] for k in range(4)
    ]
    rot = comp[64:80]
    lane = lax.broadcasted_iota(jnp.int32, rot.shape, 1)
    across = jnp.where(lane < 32, pltpu.roll(rot, 96, 1), pltpu.roll(rot, 32, 1))
    fresh.append(rot * cos_ref[...] + across * sin_ref[...])
    fresh = jnp.concatenate(fresh, axis=0).astype(BF)
    q = []
    for h in range(2):
        lat = jnp.dot(
            km_ref[h, 0], q_ref[h, 0, SIDE : SIDE + NOPE, :], preferred_element_type=F32
        ).astype(BF)
        q.append(jnp.concatenate([lat, q_ref[h, 0, SIDE + NOPE :, :]], axis=0))
    q = jnp.concatenate(q, axis=1)
    scores = jnp.dot(k_ref[...], q, preferred_element_type=F32)
    top = jnp.max(scores, axis=0, keepdims=True) * SCALE2
    weights = jnp.exp2(scores * SCALE2 - top)
    total = jnp.sum(weights, axis=0, keepdims=True)
    out = jnp.dot(v_ref[...], weights.astype(BF), preferred_element_type=F32).astype(BF)
    a = jnp.dot(vm_ref[0, 0], out[:, :128], preferred_element_type=F32)
    b = jnp.dot(vm_ref[1, 0], out[:, 128:], preferred_element_type=F32)
    stats = jnp.concatenate(
        split3(top) + split3(total) + [jnp.zeros((10, top.shape[1]), F32)], axis=0
    )
    a = jnp.concatenate([a, stats[:, :128]], axis=0)
    b = jnp.concatenate([b, stats[:, 128:]], axis=0)
    low = lax.broadcasted_iota(jnp.int32, a.shape, 1) < 64
    rows = a.shape[0]
    o_ref[0, 0, :rows, :] = jnp.where(low, a, pltpu.roll(b, 64, 1)).astype(BF)
    o_ref[1, 0, :rows, :] = jnp.where(low, pltpu.roll(a, 64, 1), b).astype(BF)
    o_ref[0, 0, rows:, :] = fresh
    o_ref[1, 0, rows:, :] = fresh


def attend(queries, keys, values_t, key_maps, value_maps, gain, cosine, sine):
    groups, pairs, rows, lanes = queries.shape
    n = keys.shape[0]
    out_rows = 128 + 16 + SIDE
    return pl.pallas_call(
        attn_kernel,
        grid=(pairs,),
        in_specs=[
            pl.BlockSpec((2, 1, rows, lanes), lambda i: (0, i, 0, 0)),
            pl.BlockSpec((n, WIDTH + 16), lambda i: (0, 0)),
            pl.BlockSpec((LAT, n), lambda i: (0, 0)),
            pl.BlockSpec((2, 1, LAT, 128), lambda i: (0, i, 0, 0)),
            pl.BlockSpec((2, 1, 128, LAT), lambda i: (0, i, 0, 0)),
            pl.BlockSpec((groups, pairs, SIDE, lanes), lambda i: (0, 0, 0, 0)),
            pl.BlockSpec((1, LAT), lambda i: (0, 0)),
            pl.BlockSpec((16, 128), lambda i: (0, 0)),
            pl.BlockSpec((16, 128), lambda i: (0, 0)),
        ],
        out_specs=pl.BlockSpec((2, 1, out_rows, lanes), lambda i: (0, i, 0, 0)),
        out_shape=jax.ShapeDtypeStruct((2, pairs, out_rows, lanes), BF),
        compiler_params=pltpu.CompilerParams(vmem_limit_bytes=48 * 1024 * 1024),
        name="cache_attention",
    )(queries, keys, values_t, key_maps, value_maps, queries, gain, cosine, sine)


def merge_kernel(part_ref, q_ref, km_ref, vm_ref, tb_ref, w_ref, o_ref, f_ref):
    parts = part_ref.shape[0]
    base = 128 + 16
    fresh = jnp.concatenate(
        [
            jnp.concatenate(
                [part_ref[i, base + 16 * k : base + 16 * k + 16, :] for k in range(5)], axis=1
            )
            for i in range(parts)
        ],
        axis=0,
    )
    fresh_t = fresh[:, :LAT].astype(F32).T.astype(BF)
    fresh = fresh[:, :WIDTH]
    f_ref[...] = fresh
    low = lax.broadcasted_iota(jnp.int32, (1, q_ref.shape[1]), 1) < 64
    plain = q_ref[:NOPE]
    lat = [jnp.dot(km_ref[h], plain, preferred_element_type=F32) for h in range(2)]
    lat = jnp.where(low, lat[0], lat[1]).astype(BF)
    q = jnp.concatenate([lat, q_ref[NOPE:]], axis=0)
    scores = jnp.dot(fresh, q, preferred_element_type=F32) * SCALE2 + tb_ref[...]
    top = jnp.max(scores, axis=0, keepdims=True)
    tops = []
    sums = []
    for i in range(parts):
        stats = part_ref[i, 128 : 128 + 16, :].astype(F32)
        tops.append(stats[0:1] + stats[1:2] + stats[2:3])
        sums.append(stats[3:4] + stats[4:5] + stats[5:6])
        top = jnp.maximum(top, tops[i])
    weights = jnp.exp2(scores - top)
    total = jnp.sum(weights, axis=0, keepdims=True)
    tree = jnp.dot(fresh_t, weights.astype(BF), preferred_element_type=F32).astype(BF)
    tree = [jnp.dot(vm_ref[h], tree, preferred_element_type=F32) for h in range(2)]
    acc = jnp.where(low, tree[0], tree[1])
    for i in range(parts):
        factor = jnp.exp2(tops[i] - top)
        total = total + sums[i] * factor
        acc = acc + part_ref[i, :128, :].astype(F32) * factor
    head = (acc / total).T.astype(BF)
    n = head.shape[0] // 2
    blocks = w_ref.shape[0]
    result = jnp.zeros((n, blocks * 64), F32)
    for h in range(2):
        project = w_ref[:, 64 * h : 64 * (h + 1), :].reshape(blocks * 64, 128)
        result = result + lax.dot_general(
            head[h * n : (h + 1) * n],
            project,
            (((1,), (1,)), ((), ())),
            preferred_element_type=F32,
        )
    o_ref[...] = result.astype(BF)


def merge(parts, q_pair, key_maps, value_maps, tree_bias, late):
    lanes = q_pair.shape[1]
    return pl.pallas_call(
        merge_kernel,
        out_shape=(
            jax.ShapeDtypeStruct((lanes // 2, late.shape[0] * 64), BF),
            jax.ShapeDtypeStruct((tree_bias.shape[0], WIDTH), BF),
        ),
        compiler_params=pltpu.CompilerParams(vmem_limit_bytes=48 * 1024 * 1024),
        name="merge_project",
    )(parts, q_pair, key_maps, value_maps, tree_bias, late)


def per_device(
    hidden,
    q_weight,
    dkv_weight,
    latent_gain,
    kvb_weight,
    out_weight,
    cache,
    cache_len,
    draft_count,
    parents,
    accept_node,
    page_table,
):
    reqs, draft = parents.shape
    tokens = reqs * draft
    slots, page_len, width = cache.shape
    mp_rank = lax.axis_index(MP)
    zh = lax.axis_index("zh")
    zl = lax.axis_index("zl")
    cols = dkv_weight.shape[1]
    keys = cache.reshape(slots * page_len, width)
    pair = both(jnp.concatenate([hidden, dkv_weight.T], axis=0), "xh")
    hid = jnp.concatenate([pair[0, :tokens], pair[1, :tokens]], axis=1)
    pack = jnp.concatenate(
        [
            q_weight[:, :NOPE],
            jnp.concatenate([q_weight[:32, NOPE:], q_weight[32:, NOPE:]], axis=1),
            pair[0, tokens:],
            pair[1, tokens:],
            jnp.zeros((12, 128), BF),
        ],
        axis=0,
    )
    wide = lax.all_to_all(jnp.broadcast_to(pack[None], (8,) + pack.shape), "y", 0, 0, tiled=True)
    keys_t, late, hid = lax.optimization_barrier((keys.T, out_weight.T, hid))
    other_t = swap(keys_t, "xh")
    late = both(late, "zh").reshape(128, 128)
    sent = jnp.concatenate([hid, kvb_weight[:, 0, :]], axis=0)
    sent = jnp.broadcast_to(sent[None], (8,) + sent.shape)
    wide, sent, late = lax.optimization_barrier((wide, sent, late))
    full_x = lax.all_to_all(sent, Z, 0, 0, tiled=True)
    late = lax.all_gather(late, DP)
    wide = both(both(wide, "xl"), "c")
    wide, other_t = lax.optimization_barrier((wide, other_t))
    down = wide[..., 96 : 96 + 2 * cols, :].transpose(2, 1, 0, 3, 4).reshape(32, 2, cols, 128)
    down = jnp.concatenate([down[:, 0], down[:, 1]], axis=2).reshape(WIDTH, 256)
    maps = full_x[:, tokens:]
    maps = jnp.concatenate(
        [maps[..., :NOPE].reshape(128, 128), maps[..., NOPE:].reshape(128, 128)], axis=0
    )
    maps = lax.all_to_all(jnp.broadcast_to(maps[None], (8,) + maps.shape), "y", 0, 0, tiled=True)
    linked = jax.vmap(tree_reach)(parents)
    depth = jnp.sum(linked, axis=2) - 1.0
    positions = (cache_len.astype(F32)[:, None] + depth).reshape(1, tokens)
    inverse = 10000.0 ** (-(jnp.arange(ROPE // 2, dtype=F32) * 2.0) / ROPE)
    phase = positions * inverse[:, None]
    cosine = jnp.cos(phase)
    sine = jnp.sin(phase)
    mine = lax.dynamic_slice_in_dim(positions.reshape(tokens), 16 * (zh * 4 + zl), 16)
    mine = mine[:, None] * jnp.concatenate([inverse, inverse])[None, :]
    sign = jnp.where(jnp.arange(ROPE) < ROPE // 2, -1.0, 1.0)[None, :]
    mine_cos = jnp.pad(jnp.cos(mine), ((0, 0), (0, 128 - ROPE)))
    mine_sin = jnp.pad(jnp.sin(mine) * sign, ((0, 0), (0, 128 - ROPE)))
    queries = project(full_x, wide, hid, down, cosine, sine)
    queries, maps, other_t = lax.optimization_barrier((queries, maps, other_t))
    queries = lax.all_to_all(queries, Z, 0, 0, tiled=True)
    queries, late = lax.optimization_barrier((queries, late))
    maps = both(both(maps, "xl"), "c")
    slot_base = jnp.stack([mp_rank, mp_rank ^ 1]) * slots
    slot_ids = (slot_base[:, None] + jnp.arange(slots, dtype=jnp.int32)[None, :]).reshape(-1)
    page_ids = jnp.arange(reqs * page_table.shape[1], dtype=jnp.int32)
    place = jnp.sum(
        jnp.where(page_table.reshape(-1)[:, None] == slot_ids[None, :], page_ids[:, None], 0), axis=0
    )
    slot_req = place // page_table.shape[1]
    slot_page = place % page_table.shape[1]
    key_pos = slot_page[:, None] * page_len + jnp.arange(page_len, dtype=jnp.int32)[None, :]
    column = jnp.arange(16, dtype=jnp.int32)
    column_len = jnp.pad(cache_len, (0, 16 - reqs))
    hidden_key = jnp.logical_or(
        slot_req[:, None, None] != column, key_pos[:, :, None] >= column_len
    )
    mask = jnp.where(jnp.logical_and(hidden_key, column < reqs), NEG, 0.0).astype(BF)
    mask = mask.reshape(2 * slots * page_len, 16)
    token_req = jnp.arange(tokens, dtype=jnp.int32) // draft
    accept_hot = (accept_node[:, None] == jnp.arange(draft, dtype=jnp.int32)[None, :]).astype(F32)
    path = jnp.sum(accept_hot[:, :, None] * linked, axis=1)
    write_at = jnp.where(
        path > 0.5, cache_len[:, None] + depth.astype(jnp.int32), -1
    ).reshape(tokens)
    chosen = jnp.logical_and(
        slot_req[:slots, None, None] == token_req, key_pos[:slots, :, None] == write_at
    )
    chosen = chosen.reshape(slots * page_len, tokens).astype(BF)
    all_keys, values_t = prepare(keys, other_t, mask)
    key_maps, value_maps = arrange(maps)
    queries = queries.reshape((2, 4) + queries.shape[1:])
    key_maps = key_maps.reshape((2, 4) + key_maps.shape[1:])
    value_maps = value_maps.reshape((2, 4) + value_maps.shape[1:])
    partial = attend(
        queries, all_keys, values_t, key_maps, value_maps, latent_gain[None, :], mine_cos, mine_sin
    )
    partial = lax.all_to_all(
        partial.reshape((8,) + partial.shape[2:]), Z, 0, 0, tiled=True
    )
    q_pair = lax.dynamic_index_in_dim(queries, zl, 1, keepdims=False)
    q_pair = q_pair[:, SIDE : SIDE + NOPE + ROPE]
    q_pair = jnp.where(zh == 0, q_pair[..., :draft], q_pair[..., draft:])
    q_pair = jnp.concatenate([q_pair[0], q_pair[1]], axis=1)
    linked_t = jnp.where(zh == 0, linked[0], linked[1]).T
    blank = jnp.zeros((draft, draft), F32)
    live = jnp.concatenate(
        [jnp.where(zh == 0, linked_t, blank), jnp.where(zh == 0, blank, linked_t)], axis=0
    )
    tree_bias = jnp.where(jnp.concatenate([live, live], axis=1) > 0.5, 0.0, NEG).astype(F32)
    key_pair = lax.dynamic_index_in_dim(key_maps, zl, 1, keepdims=False)
    value_pair = lax.dynamic_index_in_dim(value_maps, zl, 1, keepdims=False)
    projected, fresh = merge(partial, q_pair, key_pair, value_pair, tree_bias, late)
    rows = tokens // 16
    shares = lax.all_to_all(projected.reshape(8, rows, 2048), ("zl", "xh"), 0, 0, tiled=True)
    mine_rows = jnp.sum(shares.astype(F32), axis=0)
    row_index = (mp_rank * rows) % draft + jnp.arange(rows, dtype=jnp.int32)
    row_count = jnp.where(zh == 0, draft_count[0], draft_count[1])
    attended = jnp.where((row_index < row_count)[:, None], mine_rows, 0.0).astype(BF)
    placed = jnp.dot(chosen, fresh, preferred_element_type=F32).astype(BF)
    written = jnp.sum(chosen.astype(F32), axis=1, keepdims=True) > 0.5
    new_cache = jnp.where(written, placed, keys).reshape(cache.shape)
    return (attended, new_cache)


def solution(mesh):
    grid = Mesh(mesh.devices.reshape(8, 2, 2, 2, 4, 2), AXES)
    return jax.shard_map(
        per_device,
        mesh=grid,
        in_specs=(
            P(DP, MP),
            P(DP, MP),
            P(MP, DP),
            P(),
            P(DP, MP, None),
            P(MP, DP),
            P(DP + MP, None, None),
            P(DP),
            P(DP),
            P(DP, None),
            P(DP),
            P(DP, None),
        ),
        out_specs=(P(DP + MP, None), P(DP + MP, None, None)),
        check_vma=False,
    )
```

time: 220 us -> 202 us (0.918)
  waiting for transfers between devices: 99 us -> 56.3 us
  starting transfers between devices: 42.9 us -> 72.7 us
  blocking collectives: 20 us -> 0 us
  between operations: 1.12 us -> 15.9 us
  Pallas kernels: 15.7 us -> 22.8 us
  matrix products: 7.77 us -> 4.19 us
  local copies, waits for them, and re-layouts: 19 us -> 15.5 us
    all_to_all x4 -> x6, waiting for transfers between devices: 64.9 us -> 31.1 us  [the longest x1 16.3 us: per_device(): lax.all_to_all(partial.reshape((8,) + partial.shape[2:]), Z, 0, 0, tiled=...]
    ppermute x4 -> x7, waiting for transfers between devices: 34 us -> 11.8 us  [swap(): return lax.ppermute(x, axis, [(0, 1), (1, 0)])]
    all_to_all x1 -> x0, blocking collectives: 20 us -> none  [per_device(): lax.all_to_all(jnp.broadcast_to(pack[None], (8,) + pack.shape), 'y', 0, 0...]
    ppermute x4 -> x7, starting transfers between devices: 18.8 us -> 38 us  [swap(): return lax.ppermute(x, axis, [(0, 1), (1, 0)])]
    all_gather x0 -> x1, waiting for transfers between devices: none -> 13.4 us  [per_device(): late = lax.all_gather(late, DP)]
    all_to_all x4 -> x6, starting transfers between devices: 24 us -> 34.6 us  [the longest x1 8.3 us: per_device(): full_x = lax.all_to_all(sent, Z, 0, 0, tiled=True)]
    pallas_call x2 -> x5, Pallas kernels: 15.7 us -> 22.8 us  [the longest x1 16.3 us: attend(): pl.pallas_call(attn_kernel, grid=(pairs,), in_specs=[pl.BlockSpec((2, 1,...]
    dot_general x4 -> x0, matrix products: 5.12 us -> none  [the longest x1 1.62 us: per_device(): jnp.dot(jnp.where(early, zero, full_x), w_rot, preferred_element_type=F32)]
  transfers between devices with their start and end apart: 8 -> 14, of which waited for: 7 -> 8; matrix products, arithmetic and copies ran while one was open for 8% -> 12% of each run, Pallas kernels for 0% -> 2%
where the time goes in v2:
time: 202 us; the launch traced here: 201 us
  starting transfers between devices  72.7 us (36%)
  waiting for transfers between devices  56.3 us (28%)
  Pallas kernels  22.8 us (11%)
  between operations  15.9 us (8%)
  local copies, waits for them, and re-layouts  15.5 us (8%)
  other arithmetic  13.6 us (7%)
  matrix products  4.19 us (2%)
    ppermute x7, starting transfers between devices, swap(): return lax.ppermute(x, axis, [(0, 1), (1, 0)])  38 us
    pallas_call x1, Pallas kernels, attend(): pl.pallas_call(attn_kernel, grid=(pairs,), in_specs=[pl.BlockSpec((2, 1,...  16.3 us
    all_to_all x1, waiting for transfers between devices, per_device(): lax.all_to_all(partial.reshape((8,) + partial.shape[2:]), Z, 0, 0, tiled=...  16.3 us
    all_gather x1, waiting for transfers between devices, per_device(): late = lax.all_gather(late, DP)  13.4 us
    ppermute x7, waiting for transfers between devices, swap(): return lax.ppermute(x, axis, [(0, 1), (1, 0)])  11.8 us
    all_to_all x1, starting transfers between devices, per_device(): full_x = lax.all_to_all(sent, Z, 0, 0, tiled=True)  8.3 us
    all_to_all x1, waiting for transfers between devices, per_device(): lax.all_to_all(jnp.broadcast_to(maps[None], (8,) + maps.shape), 'y', 0, 0...  7.31 us
    all_to_all x1, starting transfers between devices, per_device(): lax.all_to_all(partial.reshape((8,) + partial.shape[2:]), Z, 0, 0, tiled=...  7.17 us
  transfers between devices with their start and end apart: 14, of which 8 were waited for; matrix products, arithmetic and copies ran while one was open for 12% of the time, Pallas kernels for 2%

profile of v2, /device:TPU:1, one launch (start us, length us, event | category | flops | bytes accessed | tf_op | source)
XLA Modules:
  0.0 200.8 jit_solution(18077956969852129838)
XLA Ops:
  7.9 5.5 %collective-permute-start = (bf16[146,128]{1,0:T(8,128)(2,1)S(1)}, bf16[146,128]{1,0:T(8,128)(2,1)S(1)}, u32[]{:S(2)}, u32[]{:S(2)}) collective-permute-start(bf16[146,128]{1,0:T(8,128)(2,1)S(1)} %pad_maximum_fusion.9), channel_id=1, source_target_pairs={{0,1},{1,0},{2,3},{3,2},{4,5},{5,4},{6,7},{7,6},{8,9},{9,8},{10,11... | collective-permute-start | bytes 112136 | tf_op jit(solution)/shard_map/ppermute | solution.py:37
  20.5 2.4 %copy.29 = bf16[1024,576]{0,1:T(8,128)(2,1)} copy(bf16[1024,576]{1,0:T(8,128)(2,1)} %bitcast.96) | data formatting | bytes 2359296 | tf_op jit(solution)/shard_map/reshape | solution.py:308
  24.1 6.8 %all-to-all-start = ((bf16[8,144,128]{2,1,0:T(8,128)(2,1)}), bf16[8,144,128]{2,1,0:T(8,128)(2,1)S(1)}, u32[]{:S(2)}, u32[]{:S(2)}) async-start(bf16[8,144,128]{2,1,0:T(8,128)(2,1)} %broadcast_in_dim.65), calls=%async_computation | async-start | bytes 589824 | tf_op jit(solution)/shard_map/all_to_all | solution.py:321
  30.9 10.6 %collective-permute-start.1 = (bf16[64,128]{1,0:T(8,128)(2,1)S(1)}, bf16[64,128]{1,0:T(8,128)(2,1)S(1)}, u32[]{:S(2)}, u32[]{:S(2)}) collective-permute-start(bf16[64,128]{1,0:T(8,128)(2,1)S(1)} %bitcast.111), channel_id=1, source_target_pairs={{0,8},{8,0},{1,9},{9,1},{2,10},{10,2},{3,11},{11,3},{4,12},{12,4},... | collective-permute-start | bytes 49160 | tf_op jit(solution)/shard_map/ppermute | solution.py:37
  44.2 2.2 %collective-permute-start.2 = (bf16[8,144,128]{2,1,0:T(8,128)(2,1)S(1)}, bf16[8,144,128]{2,1,0:T(8,128)(2,1)S(1)}, u32[]{:S(2)}, u32[]{:S(2)}) collective-permute-start(bf16[8,144,128]{2,1,0:T(8,128)(2,1)S(1)} %all-to-all-done), channel_id=1, source_target_pairs={{0,32},{32,0},{1,33},{33,1},{2,34},{34,2},{3,35},{35,3},{4,36},{36... | collective-permute-start | bytes 884744 | tf_op jit(solution)/shard_map/ppermute | solution.py:37
  46.4 8.3 %all-to-all-start.1 = ((bf16[8,144,256]{2,1,0:T(8,128)(2,1)}), bf16[8,144,256]{2,1,0:T(8,128)(2,1)S(1)}, u32[]{:S(2)}, u32[]{:S(2)}) async-start(bf16[8,144,256]{2,1,0:T(8,128)(2,1)} %broadcast_in_dim.66), calls=%async_computation.1 | async-start | bytes 1179648 | tf_op jit(solution)/shard_map/all_to_all | solution.py:328
  54.9 3.6 %collective-permute-start.4 = (bf16[576,1024]{1,0:T(8,128)(2,1)}, bf16[576,1024]{1,0:T(8,128)(2,1)S(1)}, u32[]{:S(2)}, u32[]{:S(2)}) collective-permute-start(bf16[576,1024]{1,0:T(8,128)(2,1)} %bitcast.8), channel_id=1, source_target_pairs={{0,1},{1,0},{2,3},{3,2},{4,5},{5,4},{6,7},{7,6},{8,9},{9,8},{10,11... | collective-permute-start | bytes 3538952 | tf_op jit(solution)/shard_map/ppermute | solution.py:37
  59.4 5.6 %collective-permute-start.3 = (bf16[2,8,144,128]{3,2,1,0:T(8,128)(2,1)}, bf16[2,8,144,128]{3,2,1,0:T(8,128)(2,1)S(1)}, u32[]{:S(2)}, u32[]{:S(2)}) collective-permute-start(bf16[2,8,144,128]{3,2,1,0:T(8,128)(2,1)} %pad_maximum_fusion.3), channel_id=1, source_target_pairs={{0,16},{16,0},{1,17},{17,1},{2,18},{18,2},{3,19},{19,3},{4,20},{20... | collective-permute-start | bytes 1769480 | tf_op jit(solution)/shard_map/ppermute | solution.py:37
  67.7 3.2 %all-to-all-done.1.x_ref = bf16[8,144,256]{2,1,0:T(8,128)(2,1)S(1)} async-done(((bf16[8,144,256]{2,1,0:T(8,128)(2,1)}), bf16[8,144,256]{2,1,0:T(8,128)(2,1)S(1)}, u32[]{:S(2)}, u32[]{:S(2)}) %all-to-all-start.1) | async-done | bytes 589856 | tf_op jit(solution)/shard_map/all_to_all | solution.py:328
  71.8 5.2 %all-to-all-start.2 = ((bf16[8,256,128]{2,1,0:T(8,128)(2,1)}), bf16[8,256,128]{2,1,0:T(8,128)(2,1)}, u32[]{:S(2)}, u32[]{:S(2)}) async-start(bf16[8,256,128]{2,1,0:T(8,128)(2,1)} %broadcast_in_dim.67), calls=%async_computation.2 | async-start | bytes 1048576 | tf_op jit(solution)/shard_map/all_to_all | solution.py:338
  77.2 5.3 %collective-permute-done.4.k2t_ref = bf16[576,1024]{1,0:T(8,128)(2,1)S(1)} collective-permute-done((bf16[576,1024]{1,0:T(8,128)(2,1)}, bf16[576,1024]{1,0:T(8,128)(2,1)S(1)}, u32[]{:S(2)}, u32[]{:S(2)}) %collective-permute-start.4) | collective-permute-done | bytes 1179680 | tf_op jit(solution)/shard_map/ppermute | solution.py:37
  84.8 7.3 %all-to-all-done.2 = bf16[8,256,128]{2,1,0:T(8,128)(2,1)} async-done(((bf16[8,256,128]{2,1,0:T(8,128)(2,1)}), bf16[8,256,128]{2,1,0:T(8,128)(2,1)}, u32[]{:S(2)}, u32[]{:S(2)}) %all-to-all-start.2) | async-done | bytes 524320 | tf_op jit(solution)/shard_map/all_to_all | solution.py:338
  92.1 3.1 %collective-permute-start.5 = (bf16[8,256,128]{2,1,0:T(8,128)(2,1)}, bf16[8,256,128]{2,1,0:T(8,128)(2,1)S(1)}, u32[]{:S(2)}, u32[]{:S(2)}) collective-permute-start(bf16[8,256,128]{2,1,0:T(8,128)(2,1)} %all-to-all-done.2), channel_id=1, source_target_pairs={{0,32},{32,0},{1,33},{33,1},{2,34},{34,2},{3,35},{35,3},{4,36},{36... | collective-permute-start | bytes 1572872 | tf_op jit(solution)/shard_map/ppermute | solution.py:37
  95.4 3.7 %all-to-all-start.3 = ((bf16[8,288,128]{2,1,0:T(8,128)(2,1)}), bf16[8,288,128]{2,1,0:T(8,128)(2,1)S(1)}, u32[]{:S(2)}, u32[]{:S(2)}) async-start(bf16[8,288,128]{2,1,0:T(8,128)(2,1)} %project_queries.1), calls=%async_computation.3 | async-start | bytes 1179648 | tf_op jit(solution)/shard_map/all_to_all | solution.py:353
  99.1 5.3 %collective-permute-done.5 = bf16[8,256,128]{2,1,0:T(8,128)(2,1)S(1)} collective-permute-done((bf16[8,256,128]{2,1,0:T(8,128)(2,1)}, bf16[8,256,128]{2,1,0:T(8,128)(2,1)S(1)}, u32[]{:S(2)}, u32[]{:S(2)}) %collective-permute-start.5) | collective-permute-done | bytes 524320 | tf_op jit(solution)/shard_map/ppermute | solution.py:37
  107.5 7.5 %collective-permute-start.6 = (bf16[2,8,256,128]{3,2,1,0:T(8,128)(2,1)}, bf16[2,8,256,128]{3,2,1,0:T(8,128)(2,1)}, u32[]{:S(2)}, u32[]{:S(2)}) collective-permute-start(bf16[2,8,256,128]{3,2,1,0:T(8,128)(2,1)} %pad_maximum_fusion.2), channel_id=1, source_target_pairs={{0,16},{16,0},{1,17},{17,1},{2,18},{18,2},{3,19},{19,3},{4,20},{20... | collective-permute-start | bytes 3145736 | tf_op jit(solution)/shard_map/ppermute | solution.py:37
  116.4 2.6 %prepare_keys.1 = (bf16[2048,592]{1,0:T(8,128)(2,1)}, bf16[512,2048]{1,0:T(8,128)(2,1)S(1)}) custom-call(bf16[1024,576]{1,0:T(8,128)(2,1)S(1)} %bitcast.97, bf16[576,1024]{1,0:T(8,128)(2,1)S(1)} %collective-permute-done.4.k2t_ref, bf16[2048,16]{1,0:T(8,128)(2,1)S(1)} %select_convert_fusion.mask_ref), custom_call_target="tpu_custom_call" | custom-call | tf_op jit(solution)/shard_map/prepare_keys/pallas_call | solution.py:65
  120.3 13.4 %all-gather.3.cloned.1.call-done = bf16[4096,128]{1,0:T(8,128)(2,1)} async-done(((bf16[128,128]{1,0:T(8,128)(2,1)}), bf16[4096,128]{1,0:T(8,128)(2,1)}) %all-gather.3.cloned.1.call-update) | async-done | bytes 1048592 | tf_op jit(solution)/shard_map/all_gather | solution.py:329
  137.2 16.3 %cache_attention.1 = bf16[2,4,224,128]{3,2,1,0:T(8,128)(2,1)} custom-call(bf16[2,4,288,128]{3,2,1,0:T(8,128)(2,1)S(1)} %bitcast.94, bf16[2048,592]{1,0:T(8,128)(2,1)} %get-tuple-element.32.k_ref, bf16[512,2048]{1,0:T(8,128)(2,1)S(1)} %copy-done.2, bf16[2,4,512,128]{3,2,1,0:T(8,128)(2,1)S(1)} %bitcast.98, bf16[2,4,128,512]{3,2,1,0:T(8,128)(2,1)S(1)} %bitcast.100, ...), custom_call_target="tpu_custom_call" | custom-call | tf_op jit(solution)/shard_map/cache_attention/pallas_call | solution.py:200
  153.5 7.2 %all-to-all-start.4 = ((bf16[8,224,128]{2,1,0:T(8,128)(2,1)}), bf16[8,224,128]{2,1,0:T(8,128)(2,1)S(1)}, u32[]{:S(2)}, u32[]{:S(2)}) async-start(bf16[8,224,128]{2,1,0:T(8,128)(2,1)} %bitcast.37), calls=%async_computation.4 | async-start | bytes 917504 | tf_op jit(solution)/shard_map/all_to_all | solution.py:390
  161.0 16.3 %all-to-all-done.4.part_ref = bf16[8,224,128]{2,1,0:T(8,128)(2,1)S(1)} async-done(((bf16[8,224,128]{2,1,0:T(8,128)(2,1)}), bf16[8,224,128]{2,1,0:T(8,128)(2,1)S(1)}, u32[]{:S(2)}, u32[]{:S(2)}) %all-to-all-start.4) | async-done | bytes 458784 | tf_op jit(solution)/shard_map/all_to_all | solution.py:390
  178.5 2.0 %merge_project.1 = (bf16[64,2048]{1,0:T(8,128)(2,1)}, bf16[128,576]{1,0:T(8,128)(2,1)S(1)}) custom-call(bf16[8,224,128]{2,1,0:T(8,128)(2,1)S(1)} %all-to-all-done.4.part_ref, bf16[192,128]{1,0:T(8,128)(2,1)S(1)} %pad_maximum_fusion.8.q_ref, bf16[2,512,128]{2,1,0:T(8,128)(2,1)S(1)} %dynamic-slice_bitcast_fusion.1.km_ref, ...), custom_call_target="tpu_custom_call" | custom-call | tf_op jit(solution)/shard_map/merge_project/pallas_call | solution.py:276
  180.5 3.4 %all-to-all-start.5 = ((bf16[8,8,2048]{2,1,0:T(8,128)(2,1)}), bf16[8,8,2048]{2,1,0:T(8,128)(2,1)S(1)}, u32[]{:S(2)}, u32[]{:S(2)}) async-start(bf16[8,8,2048]{2,1,0:T(8,128)(2,1)} %bitcast.47), calls=%async_computation.5 | async-start | bytes 524288 | tf_op jit(solution)/shard_map/all_to_all | solution.py:407
  189.0 4.3 %all-to-all-done.5 = bf16[8,8,2048]{2,1,0:T(8,128)(2,1)S(1)} async-done(((bf16[8,8,2048]{2,1,0:T(8,128)(2,1)}), bf16[8,8,2048]{2,1,0:T(8,128)(2,1)S(1)}, u32[]{:S(2)}, u32[]{:S(2)}) %all-to-all-start.5) | async-done | bytes 262176 | tf_op jit(solution)/shard_map/all_to_all | solution.py:407
  (136 shorter events, 33.9 us)
Async XLA Ops:
  7.9 15.0 %collective-permute-start = (bf16[146,128]{1,0:T(8,128)(2,1)S(1)}, bf16[146,128]{1,0:T(8,128)(2,1)S(1)}, u32[]{:S(2)}, u32[]{:S(2)}) collective-permute-start(bf16[146,128]{1,0:T(8,128)(2,1)S(1)} %pad_maximum_fusion.9), channel_id=1, source_target_pairs={{0,1},{1,0},{2,3},{3,2},{4,5},{5,4},{6,7},{7,6},{8,9},{9,8},{10,11... | collective-permute-start | bytes 112136 | tf_op jit(solution)/shard_map/ppermute | solution.py:37
  23.0 18.6 %copy-start.12 = (bf16[16,1,256]{2,0,1:T(8,128)(2,1)S(1)}, bf16[16,1,256]{2,0,1:T(8,128)(2,1)}, u32[]{:S(2)}) copy-start(bf16[16,1,256]{2,0,1:T(8,128)(2,1)} %param.16) | copy-start | bytes 24580
  24.1 19.2 %all-to-all-start = ((bf16[8,144,128]{2,1,0:T(8,128)(2,1)}), bf16[8,144,128]{2,1,0:T(8,128)(2,1)S(1)}, u32[]{:S(2)}, u32[]{:S(2)}) async-start(bf16[8,144,128]{2,1,0:T(8,128)(2,1)} %broadcast_in_dim.65), calls=%async_computation | async-start | bytes 589824 | tf_op jit(solution)/shard_map/all_to_all | solution.py:321
  30.9 11.8 %collective-permute-start.1 = (bf16[64,128]{1,0:T(8,128)(2,1)S(1)}, bf16[64,128]{1,0:T(8,128)(2,1)S(1)}, u32[]{:S(2)}, u32[]{:S(2)}) collective-permute-start(bf16[64,128]{1,0:T(8,128)(2,1)S(1)} %bitcast.111), channel_id=1, source_target_pairs={{0,8},{8,0},{1,9},{9,1},{2,10},{10,2},{3,11},{11,3},{4,12},{12,4},... | collective-permute-start | bytes 49160 | tf_op jit(solution)/shard_map/ppermute | solution.py:37
  44.2 14.3 %collective-permute-start.2 = (bf16[8,144,128]{2,1,0:T(8,128)(2,1)S(1)}, bf16[8,144,128]{2,1,0:T(8,128)(2,1)S(1)}, u32[]{:S(2)}, u32[]{:S(2)}) collective-permute-start(bf16[8,144,128]{2,1,0:T(8,128)(2,1)S(1)} %all-to-all-done), channel_id=1, source_target_pairs={{0,32},{32,0},{1,33},{33,1},{2,34},{34,2},{3,35},{35,3},{4,36},{36... | collective-permute-start | bytes 884744 | tf_op jit(solution)/shard_map/ppermute | solution.py:37
  46.4 24.4 %all-to-all-start.1 = ((bf16[8,144,256]{2,1,0:T(8,128)(2,1)}), bf16[8,144,256]{2,1,0:T(8,128)(2,1)S(1)}, u32[]{:S(2)}, u32[]{:S(2)}) async-start(bf16[8,144,256]{2,1,0:T(8,128)(2,1)} %broadcast_in_dim.66), calls=%async_computation.1 | async-start | bytes 1179648 | tf_op jit(solution)/shard_map/all_to_all | solution.py:328
  54.7 79.0 %all-gather.3.cloned.1.call-start = ((), (), s32[]{:S(2)}) async-start(), calls=%async_computation.6 | async-start | bytes 1081344 | tf_op jit(solution)/shard_map/all_gather | solution.py:329
  54.9 27.6 %collective-permute-start.4 = (bf16[576,1024]{1,0:T(8,128)(2,1)}, bf16[576,1024]{1,0:T(8,128)(2,1)S(1)}, u32[]{:S(2)}, u32[]{:S(2)}) collective-permute-start(bf16[576,1024]{1,0:T(8,128)(2,1)} %bitcast.8), channel_id=1, source_target_pairs={{0,1},{1,0},{2,3},{3,2},{4,5},{5,4},{6,7},{7,6},{8,9},{9,8},{10,11... | collective-permute-start | bytes 3538952 | tf_op jit(solution)/shard_map/ppermute | solution.py:37
  59.4 17.5 %collective-permute-start.3 = (bf16[2,8,144,128]{3,2,1,0:T(8,128)(2,1)}, bf16[2,8,144,128]{3,2,1,0:T(8,128)(2,1)S(1)}, u32[]{:S(2)}, u32[]{:S(2)}) collective-permute-start(bf16[2,8,144,128]{3,2,1,0:T(8,128)(2,1)} %pad_maximum_fusion.3), channel_id=1, source_target_pairs={{0,16},{16,0},{1,17},{17,1},{2,18},{18,2},{3,19},{19,3},{4,20},{20... | collective-permute-start | bytes 1769480 | tf_op jit(solution)/shard_map/ppermute | solution.py:37
  71.8 20.3 %all-to-all-start.2 = ((bf16[8,256,128]{2,1,0:T(8,128)(2,1)}), bf16[8,256,128]{2,1,0:T(8,128)(2,1)}, u32[]{:S(2)}, u32[]{:S(2)}) async-start(bf16[8,256,128]{2,1,0:T(8,128)(2,1)} %broadcast_in_dim.67), calls=%async_computation.2 | async-start | bytes 1048576 | tf_op jit(solution)/shard_map/all_to_all | solution.py:338
  83.2 11.9 %copy-start.15 = (s32[32]{0:T(128)S(1)}, s32[32]{0:T(128)}, u32[]{:S(2)}) copy-start(s32[32]{0:T(128)} %get-tuple-element.72) | copy-start | bytes 388
  83.2 12.0 %copy-start.17 = (f32[64]{0:T(128)S(1)}, f32[64]{0:T(128)}, u32[]{:S(2)}) copy-start(f32[64]{0:T(128)} %get-tuple-element.79) | copy-start | bytes 772
  83.2 12.0 %copy-start.18 = (f32[64]{0:T(128)S(1)}, f32[64]{0:T(128)}, u32[]{:S(2)}) copy-start(f32[64]{0:T(128)} %get-tuple-element.80) | copy-start | bytes 772
  83.2 12.0 %copy-start.19 = (f32[16]{0:T(128)S(1)}, f32[16]{0:T(128)}, u32[]{:S(2)}) copy-start(f32[16]{0:T(128)} %dynamic_slice.15) | copy-start | bytes 196
  92.1 12.3 %collective-permute-start.5 = (bf16[8,256,128]{2,1,0:T(8,128)(2,1)}, bf16[8,256,128]{2,1,0:T(8,128)(2,1)S(1)}, u32[]{:S(2)}, u32[]{:S(2)}) collective-permute-start(bf16[8,256,128]{2,1,0:T(8,128)(2,1)} %all-to-all-done.2), channel_id=1, source_target_pairs={{0,32},{32,0},{1,33},{33,1},{2,34},{34,2},{3,35},{35,3},{4,36},{36... | collective-permute-start | bytes 1572872 | tf_op jit(solution)/shard_map/ppermute | solution.py:37
  95.4 38.3 %all-to-all-start.3 = ((bf16[8,288,128]{2,1,0:T(8,128)(2,1)}), bf16[8,288,128]{2,1,0:T(8,128)(2,1)S(1)}, u32[]{:S(2)}, u32[]{:S(2)}) async-start(bf16[8,288,128]{2,1,0:T(8,128)(2,1)} %project_queries.1), calls=%async_computation.3 | async-start | bytes 1179648 | tf_op jit(solution)/shard_map/all_to_all | solution.py:353
  105.5 9.4 %copy-start.8 = (s32[16,64]{1,0:T(8,128)S(1)}, s32[16,64]{1,0:T(8,128)}, u32[]{:S(2)}) copy-start(s32[16,64]{1,0:T(8,128)} %slice.108) | copy-start | bytes 12292
  105.5 9.4 %copy-start.13 = (s32[128]{0:T(128)S(1)}, s32[128]{0:T(128)}, u32[]{:S(2)}) copy-start(s32[128]{0:T(128)} %select_n.239) | copy-start | bytes 1540
  105.5 9.9 %copy-start.16 = (s32[2]{0:T(128)S(1)}, s32[2]{0:T(128)}, u32[]{:S(2)}) copy-start(s32[2]{0:T(128)} %param.19) | copy-start | bytes 28
  106.3 9.9 %copy-start.9 = (f32[2,64,64]{1,2,0:T(8,128)S(1)}, f32[2,64,64]{1,2,0:T(8,128)}, u32[]{:S(2)}) copy-start(f32[2,64,64]{1,2,0:T(8,128)} %get-tuple-element.74) | copy-start | bytes 98308
  106.3 10.0 %copy-start = (bf16[16,64,576]{2,1,0:T(8,128)(2,1)S(1)}, bf16[16,64,576]{2,1,0:T(8,128)(2,1)}, u32[]{:S(2)}) copy-start(bf16[16,64,576]{2,1,0:T(8,128)(2,1)} %param.18) | copy-start | bytes 3538948
  107.5 26.3 %collective-permute-start.6 = (bf16[2,8,256,128]{3,2,1,0:T(8,128)(2,1)}, bf16[2,8,256,128]{3,2,1,0:T(8,128)(2,1)}, u32[]{:S(2)}, u32[]{:S(2)}) collective-permute-start(bf16[2,8,256,128]{3,2,1,0:T(8,128)(2,1)} %pad_maximum_fusion.2), channel_id=1, source_target_pairs={{0,16},{16,0},{1,17},{17,1},{2,18},{18,2},{3,19},{19,3},{4,20},{20... | collective-permute-start | bytes 3145736 | tf_op jit(solution)/shard_map/ppermute | solution.py:37
  153.5 23.7 %all-to-all-start.4 = ((bf16[8,224,128]{2,1,0:T(8,128)(2,1)}), bf16[8,224,128]{2,1,0:T(8,128)(2,1)S(1)}, u32[]{:S(2)}, u32[]{:S(2)}) async-start(bf16[8,224,128]{2,1,0:T(8,128)(2,1)} %bitcast.37), calls=%async_computation.4 | async-start | bytes 917504 | tf_op jit(solution)/shard_map/all_to_all | solution.py:390
  180.5 12.8 %all-to-all-start.5 = ((bf16[8,8,2048]{2,1,0:T(8,128)(2,1)}), bf16[8,8,2048]{2,1,0:T(8,128)(2,1)S(1)}, u32[]{:S(2)}, u32[]{:S(2)}) async-start(bf16[8,8,2048]{2,1,0:T(8,128)(2,1)} %bitcast.47), calls=%async_computation.5 | async-start | bytes 524288 | tf_op jit(solution)/shard_map/all_to_all | solution.py:407
  (11 other events, 29.3 us)
Sparse Core Ops, SparseCore 0:
  67.8 65.8 all-gather.2

commit v3 on v2

--- a/solution.py
+++ b/solution.py
@@ -214,6 +214,9 @@
         out_specs=pl.BlockSpec((2, 1, out_rows, lanes), lambda i: (0, i, 0, 0)),
         out_shape=jax.ShapeDtypeStruct((2, pairs, out_rows, lanes), BF),
         compiler_params=pltpu.CompilerParams(vmem_limit_bytes=48 * 1024 * 1024),
+        cost_estimate=pl.CostEstimate(
+            flops=2 * n * 8 * lanes * (WIDTH + LAT), transcendentals=n * 8 * lanes, bytes_accessed=6 << 20
+        ),
         name="cache_attention",
     )(queries, keys, values_t, key_maps, value_maps, queries, gain, cosine, sine)
 
@@ -258,10 +261,12 @@
         acc = acc + part_ref[i, :128, :].astype(F32) * factor
     head = (acc / total).T.astype(BF)
     n = head.shape[0] // 2
-    blocks = w_ref.shape[0]
-    result = jnp.zeros((n, blocks * 64), F32)
+    order = [(y, xl, c) for y in range(8) for xl in range(2) for c in range(2)]
+    result = jnp.zeros((n, len(order) * 64), F32)
     for h in range(2):
-        project = w_ref[:, 64 * h : 64 * (h + 1), :].reshape(blocks * 64, 128)
+        project = jnp.concatenate(
+            [w_ref[c, xl, y, 64 * h : 64 * (h + 1), :] for y, xl, c in order], axis=0
+        )
         result = result + lax.dot_general(
             head[h * n : (h + 1) * n],
             project,
@@ -276,7 +281,7 @@
     return pl.pallas_call(
         merge_kernel,
         out_shape=(
-            jax.ShapeDtypeStruct((lanes // 2, late.shape[0] * 64), BF),
+            jax.ShapeDtypeStruct((lanes // 2, 2048), BF),
             jax.ShapeDtypeStruct((tree_bias.shape[0], WIDTH), BF),
         ),
         compiler_params=pltpu.CompilerParams(vmem_limit_bytes=48 * 1024 * 1024),
@@ -319,14 +324,14 @@
         axis=0,
     )
     wide = lax.all_to_all(jnp.broadcast_to(pack[None], (8,) + pack.shape), "y", 0, 0, tiled=True)
-    keys_t, late, hid = lax.optimization_barrier((keys.T, out_weight.T, hid))
+    keys_t, hid = lax.optimization_barrier((keys.T, hid))
     other_t = swap(keys_t, "xh")
-    late = both(late, "zh").reshape(128, 128)
     sent = jnp.concatenate([hid, kvb_weight[:, 0, :]], axis=0)
     sent = jnp.broadcast_to(sent[None], (8,) + sent.shape)
-    wide, sent, late = lax.optimization_barrier((wide, sent, late))
+    wide, sent = lax.optimization_barrier((wide, sent))
     full_x = lax.all_to_all(sent, Z, 0, 0, tiled=True)
-    late = lax.all_gather(late, DP)
+    late, full_x = lax.optimization_barrier((out_weight.T, full_x))
+    late = both(late, "zh").reshape(128, 128)
     wide = both(both(wide, "xl"), "c")
     wide, other_t = lax.optimization_barrier((wide, other_t))
     down = wide[..., 96 : 96 + 2 * cols, :].transpose(2, 1, 0, 3, 4).reshape(32, 2, cols, 128)
@@ -351,7 +356,9 @@
     queries = project(full_x, wide, hid, down, cosine, sine)
     queries, maps, other_t = lax.optimization_barrier((queries, maps, other_t))
     queries = lax.all_to_all(queries, Z, 0, 0, tiled=True)
+    late = jnp.broadcast_to(late[None], (8,) + late.shape)
     queries, late = lax.optimization_barrier((queries, late))
+    late = lax.all_to_all(late, "y", 0, 0, tiled=True)
     maps = both(both(maps, "xl"), "c")
     slot_base = jnp.stack([mp_rank, mp_rank ^ 1]) * slots
     slot_ids = (slot_base[:, None] + jnp.arange(slots, dtype=jnp.int32)[None, :]).reshape(-1)
@@ -387,6 +394,8 @@
     partial = attend(
         queries, all_keys, values_t, key_maps, value_maps, latent_gain[None, :], mine_cos, mine_sin
     )
+    partial, late = lax.optimization_barrier((partial, late))
+    late = both(both(late, "xl"), "c")
     partial = lax.all_to_all(
         partial.reshape((8,) + partial.shape[2:]), Z, 0, 0, tiled=True
     )

time: 202 us -> 181 us (0.90); the launches traced: 201 us -> 177 us
  between operations: 15.9 us -> 2.56 us
  waiting for transfers between devices: 56.3 us -> 48.1 us
    all_gather x1 -> x0, waiting for transfers between devices: 13.4 us -> none  [per_device(): late = lax.all_gather(late, DP)]
    all_to_all x1, waiting for transfers between devices: 0.01 us -> 10.4 us  [per_device(): lax.all_to_all(jnp.broadcast_to(pack[None], (8,) + pack.shape), 'y', 0, 0...]
    all_to_all x1, waiting for transfers between devices: 16.3 us -> 7.01 us  [per_device(): lax.all_to_all(partial.reshape((8,) + partial.shape[2:]), Z, 0, 0, tiled=...]
    ppermute x7 -> x9, waiting for transfers between devices: 11.8 us -> 16.9 us  [swap(): return lax.ppermute(x, axis, [(0, 1), (1, 0)])]
    all_to_all x1, starting transfers between devices: 7.17 us -> 3.48 us  [per_device(): lax.all_to_all(partial.reshape((8,) + partial.shape[2:]), Z, 0, 0, tiled=...]
    all_to_all x0 -> x1, starting transfers between devices: none -> 3.41 us  [per_device(): late = lax.all_to_all(late, 'y', 0, 0, tiled=True)]
    ppermute x7 -> x9, starting transfers between devices: 38 us -> 37.1 us  [swap(): return lax.ppermute(x, axis, [(0, 1), (1, 0)])]
    unnamed x40 -> x42, local copies, waits for them, and re-layouts: 4.63 us -> 3.86 us
  transfers between devices with their start and end apart: 14 -> 16, of which waited for: 8 -> 10; matrix products, arithmetic and copies ran while one was open for 12% -> 14% of each run, Pallas kernels for 2% -> 12%
where the time goes in v3:
time: 181 us; the launch traced here: 177 us
  starting transfers between devices  72.4 us (40%)
  waiting for transfers between devices  48.1 us (27%)
  Pallas kernels  22.7 us (13%)
  local copies, waits for them, and re-layouts  14.7 us (8%)
  other arithmetic  13 us (7%)
  matrix products  3.66 us (2%)
  between operations  2.56 us (1%)
    ppermute x9, starting transfers between devices, swap(): return lax.ppermute(x, axis, [(0, 1), (1, 0)])  37.1 us
    ppermute x9, waiting for transfers between devices, swap(): return lax.ppermute(x, axis, [(0, 1), (1, 0)])  16.9 us
    pallas_call x1, Pallas kernels, attend(): pl.pallas_call(attn_kernel, grid=(pairs,), in_specs=[pl.BlockSpec((2, 1,...  16.3 us
    all_to_all x1, waiting for transfers between devices, per_device(): lax.all_to_all(jnp.broadcast_to(pack[None], (8,) + pack.shape), 'y', 0, 0...  10.4 us
    all_to_all x1, starting transfers between devices, per_device(): full_x = lax.all_to_all(sent, Z, 0, 0, tiled=True)  10 us
    all_to_all x1, waiting for transfers between devices, per_device(): lax.all_to_all(partial.reshape((8,) + partial.shape[2:]), Z, 0, 0, tiled=...  7.01 us
    all_to_all x1, starting transfers between devices, per_device(): lax.all_to_all(jnp.broadcast_to(pack[None], (8,) + pack.shape), 'y', 0, 0...  6.82 us
    all_to_all x1, waiting for transfers between devices, per_device(): lax.all_to_all(jnp.broadcast_to(maps[None], (8,) + maps.shape), 'y', 0, 0...  5.57 us
  transfers between devices with their start and end apart: 16, of which 10 were waited for; matrix products, arithmetic and copies ran while one was open for 14% of the time, Pallas kernels for 12%

profile of v3, /device:TPU:1, one launch (start us, length us, event | category | flops | bytes accessed | tf_op | source)
XLA Modules:
  0.0 177.1 jit_solution(7993658559894051410)
XLA Ops:
  1.4 5.5 %collective-permute-start = (bf16[146,128]{1,0:T(8,128)(2,1)S(1)}, bf16[146,128]{1,0:T(8,128)(2,1)S(1)}, u32[]{:S(2)}, u32[]{:S(2)}) collective-permute-start(bf16[146,128]{1,0:T(8,128)(2,1)S(1)} %pad_maximum_fusion.11), channel_id=1, source_target_pairs={{0,1},{1,0},{2,3},{3,2},{4,5},{5,4},{6,7},{7,6},{8,9},{9,8},{10,11... | collective-permute-start | bytes 112136 | tf_op jit(solution)/shard_map/ppermute | solution.py:37
  15.8 6.8 %all-to-all-start = ((bf16[8,144,128]{2,1,0:T(8,128)(2,1)}), bf16[8,144,128]{2,1,0:T(8,128)(2,1)S(1)}, u32[]{:S(2)}, u32[]{:S(2)}) async-start(bf16[8,144,128]{2,1,0:T(8,128)(2,1)} %broadcast_in_dim.69), calls=%async_computation | async-start | bytes 589824 | tf_op jit(solution)/shard_map/all_to_all | solution.py:326
  22.9 10.4 %all-to-all-done = bf16[8,144,128]{2,1,0:T(8,128)(2,1)S(1)} async-done(((bf16[8,144,128]{2,1,0:T(8,128)(2,1)}), bf16[8,144,128]{2,1,0:T(8,128)(2,1)S(1)}, u32[]{:S(2)}, u32[]{:S(2)}) %all-to-all-start) | async-done | bytes 294944 | tf_op jit(solution)/shard_map/all_to_all | solution.py:326
  36.4 10.0 %all-to-all-start.1 = ((bf16[8,144,256]{2,1,0:T(8,128)(2,1)}), bf16[8,144,256]{2,1,0:T(8,128)(2,1)S(1)}, u32[]{:S(2)}, u32[]{:S(2)}) async-start(bf16[8,144,256]{2,1,0:T(8,128)(2,1)} %broadcast_in_dim.70), calls=%async_computation.1 | async-start | bytes 1179648 | tf_op jit(solution)/shard_map/all_to_all | solution.py:332
  47.0 3.6 %collective-permute-start.3 = (bf16[576,1024]{1,0:T(8,128)(2,1)}, bf16[576,1024]{1,0:T(8,128)(2,1)S(1)}, u32[]{:S(2)}, u32[]{:S(2)}) collective-permute-start(bf16[576,1024]{1,0:T(8,128)(2,1)} %bitcast.9), channel_id=1, source_target_pairs={{0,1},{1,0},{2,3},{3,2},{4,5},{5,4},{6,7},{7,6},{8,9},{9,8},{10,11... | collective-permute-start | bytes 3538952 | tf_op jit(solution)/shard_map/ppermute | solution.py:37
  51.6 5.6 %collective-permute-start.2 = (bf16[2,8,144,128]{3,2,1,0:T(8,128)(2,1)}, bf16[2,8,144,128]{3,2,1,0:T(8,128)(2,1)S(1)}, u32[]{:S(2)}, u32[]{:S(2)}) collective-permute-start(bf16[2,8,144,128]{3,2,1,0:T(8,128)(2,1)} %pad_maximum_fusion.4), channel_id=1, source_target_pairs={{0,16},{16,0},{1,17},{17,1},{2,18},{18,2},{3,19},{19,3},{4,20},{20... | collective-permute-start | bytes 1769480 | tf_op jit(solution)/shard_map/ppermute | solution.py:37
  57.9 4.7 %all-to-all-done.1.x_ref = bf16[8,144,256]{2,1,0:T(8,128)(2,1)S(1)} async-done(((bf16[8,144,256]{2,1,0:T(8,128)(2,1)}), bf16[8,144,256]{2,1,0:T(8,128)(2,1)S(1)}, u32[]{:S(2)}, u32[]{:S(2)}) %all-to-all-start.1) | async-done | bytes 589856 | tf_op jit(solution)/shard_map/all_to_all | solution.py:332
  63.5 4.5 %all-to-all-start.2 = ((bf16[8,256,128]{2,1,0:T(8,128)(2,1)}), bf16[8,256,128]{2,1,0:T(8,128)(2,1)}, u32[]{:S(2)}, u32[]{:S(2)}) async-start(bf16[8,256,128]{2,1,0:T(8,128)(2,1)} %broadcast_in_dim.71), calls=%async_computation.2 | async-start | bytes 1048576 | tf_op jit(solution)/shard_map/all_to_all | solution.py:343
  68.2 6.4 %collective-permute-done.3.k2t_ref = bf16[576,1024]{1,0:T(8,128)(2,1)S(1)} collective-permute-done((bf16[576,1024]{1,0:T(8,128)(2,1)}, bf16[576,1024]{1,0:T(8,128)(2,1)S(1)}, u32[]{:S(2)}, u32[]{:S(2)}) %collective-permute-start.3) | collective-permute-done | bytes 1179680 | tf_op jit(solution)/shard_map/ppermute | solution.py:37
  76.8 5.6 %all-to-all-done.2 = bf16[8,256,128]{2,1,0:T(8,128)(2,1)} async-done(((bf16[8,256,128]{2,1,0:T(8,128)(2,1)}), bf16[8,256,128]{2,1,0:T(8,128)(2,1)}, u32[]{:S(2)}, u32[]{:S(2)}) %all-to-all-start.2) | async-done | bytes 524320 | tf_op jit(solution)/shard_map/all_to_all | solution.py:343
  82.3 3.1 %collective-permute-start.5 = (bf16[8,256,128]{2,1,0:T(8,128)(2,1)}, bf16[8,256,128]{2,1,0:T(8,128)(2,1)S(1)}, u32[]{:S(2)}, u32[]{:S(2)}) collective-permute-start(bf16[8,256,128]{2,1,0:T(8,128)(2,1)} %all-to-all-done.2), channel_id=1, source_target_pairs={{0,32},{32,0},{1,33},{33,1},{2,34},{34,2},{3,35},{35,3},{4,36},{36... | collective-permute-start | bytes 1572872 | tf_op jit(solution)/shard_map/ppermute | solution.py:37
  86.3 3.5 %all-to-all-start.3 = ((bf16[8,288,128]{2,1,0:T(8,128)(2,1)}), bf16[8,288,128]{2,1,0:T(8,128)(2,1)S(1)}, u32[]{:S(2)}, u32[]{:S(2)}) async-start(bf16[8,288,128]{2,1,0:T(8,128)(2,1)} %project_queries.1), calls=%async_computation.3 | async-start | bytes 1179648 | tf_op jit(solution)/shard_map/all_to_all | solution.py:358
  89.9 3.8 %collective-permute-done.5 = bf16[8,256,128]{2,1,0:T(8,128)(2,1)S(1)} collective-permute-done((bf16[8,256,128]{2,1,0:T(8,128)(2,1)}, bf16[8,256,128]{2,1,0:T(8,128)(2,1)S(1)}, u32[]{:S(2)}, u32[]{:S(2)}) %collective-permute-start.5) | collective-permute-done | bytes 524320 | tf_op jit(solution)/shard_map/ppermute | solution.py:37
  96.7 7.0 %collective-permute-start.6 = (bf16[2,8,256,128]{3,2,1,0:T(8,128)(2,1)}, bf16[2,8,256,128]{3,2,1,0:T(8,128)(2,1)}, u32[]{:S(2)}, u32[]{:S(2)}) collective-permute-start(bf16[2,8,256,128]{3,2,1,0:T(8,128)(2,1)} %pad_maximum_fusion.2), channel_id=1, source_target_pairs={{0,16},{16,0},{1,17},{17,1},{2,18},{18,2},{3,19},{19,3},{4,20},{20... | collective-permute-start | bytes 3145736 | tf_op jit(solution)/shard_map/ppermute | solution.py:37
  104.5 3.0 %collective-permute-start.4 = (bf16[64,128]{1,0:T(8,128)(2,1)S(1)}, bf16[64,128]{1,0:T(8,128)(2,1)S(1)}, u32[]{:S(2)}, u32[]{:S(2)}) collective-permute-start(bf16[64,128]{1,0:T(8,128)(2,1)S(1)} %bitcast.117), channel_id=1, source_target_pairs={{0,8},{8,0},{1,9},{9,1},{2,10},{10,2},{3,11},{11,3},{4,12},{12,4},... | collective-permute-start | bytes 49160 | tf_op jit(solution)/shard_map/ppermute | solution.py:37
  108.4 4.5 %collective-permute-done.4 = bf16[64,128]{1,0:T(8,128)(2,1)S(1)} collective-permute-done((bf16[64,128]{1,0:T(8,128)(2,1)S(1)}, bf16[64,128]{1,0:T(8,128)(2,1)S(1)}, u32[]{:S(2)}, u32[]{:S(2)}) %collective-permute-start.4) | collective-permute-done | bytes 16416 | tf_op jit(solution)/shard_map/ppermute | solution.py:37
  117.6 3.4 %all-to-all-start.4 = ((bf16[8,128,128]{2,1,0:T(8,128)(2,1)}), bf16[8,128,128]{2,1,0:T(8,128)(2,1)S(1)}, u32[]{:S(2)}, u32[]{:S(2)}) async-start(bf16[8,128,128]{2,1,0:T(8,128)(2,1)} %broadcast_in_dim.77), calls=%async_computation.4 | async-start | bytes 524288 | tf_op jit(solution)/shard_map/all_to_all | solution.py:361
  124.7 16.3 %cache_attention.1 = bf16[2,4,224,128]{3,2,1,0:T(8,128)(2,1)} custom-call(bf16[2,4,288,128]{3,2,1,0:T(8,128)(2,1)S(1)} %bitcast.102, bf16[2048,592]{1,0:T(8,128)(2,1)} %get-tuple-element.34.k_ref, bf16[512,2048]{1,0:T(8,128)(2,1)S(1)} %copy-done.4, bf16[2,4,512,128]{3,2,1,0:T(8,128)(2,1)S(1)} %bitcast.105, bf16[2,4,128,512]{3,2,1,0:T(8,128)(2,1)S(1)} %bitcast.107, ...), custom_call_target="tpu_custom_call" | custom-call | flops 4563402752 | bytes 6291456 | tf_op jit(solution)/shard_map/cache_attention/pallas_call | solution.py:200
  141.0 3.1 %collective-permute-start.7 = (bf16[8,128,128]{2,1,0:T(8,128)(2,1)S(1)}, bf16[8,128,128]{2,1,0:T(8,128)(2,1)S(1)}, u32[]{:S(2)}, u32[]{:S(2)}) collective-permute-start(bf16[8,128,128]{2,1,0:T(8,128)(2,1)S(1)} %all-to-all-done.4), channel_id=1, source_target_pairs={{0,32},{32,0},{1,33},{33,1},{2,34},{34,2},{3,35},{35,3},{4,36},{36... | collective-permute-start | bytes 786440 | tf_op jit(solution)/shard_map/ppermute | solution.py:37
  144.2 3.5 %all-to-all-start.5 = ((bf16[8,224,128]{2,1,0:T(8,128)(2,1)}), bf16[8,224,128]{2,1,0:T(8,128)(2,1)S(1)}, u32[]{:S(2)}, u32[]{:S(2)}) async-start(bf16[8,224,128]{2,1,0:T(8,128)(2,1)} %bitcast.36), calls=%async_computation.5 | async-start | bytes 917504 | tf_op jit(solution)/shard_map/all_to_all | solution.py:399
  149.6 4.0 %collective-permute-start.8 = (bf16[2,8,128,128]{3,2,1,0:T(8,128)(2,1)S(1)}, bf16[2,8,128,128]{3,2,1,0:T(8,128)(2,1)S(1)}, u32[]{:S(2)}, u32[]{:S(2)}) collective-permute-start(bf16[2,8,128,128]{3,2,1,0:T(8,128)(2,1)S(1)} %pad_maximum_fusion.5), channel_id=1, source_target_pairs={{0,16},{16,0},{1,17},{17,1},{2,18},{18,2},{3,19},{19,3},{4,20},{20... | collective-permute-start | bytes 1572872 | tf_op jit(solution)/shard_map/ppermute | solution.py:37
  155.4 7.0 %all-to-all-done.5.part_ref = bf16[8,224,128]{2,1,0:T(8,128)(2,1)S(1)} async-done(((bf16[8,224,128]{2,1,0:T(8,128)(2,1)}), bf16[8,224,128]{2,1,0:T(8,128)(2,1)S(1)}, u32[]{:S(2)}, u32[]{:S(2)}) %all-to-all-start.5) | async-done | bytes 458784 | tf_op jit(solution)/shard_map/all_to_all | solution.py:399
  164.4 3.4 %all-to-all-start.6 = ((bf16[8,8,2048]{2,1,0:T(8,128)(2,1)}), bf16[8,8,2048]{2,1,0:T(8,128)(2,1)S(1)}, u32[]{:S(2)}, u32[]{:S(2)}) async-start(bf16[8,8,2048]{2,1,0:T(8,128)(2,1)} %bitcast.50), calls=%async_computation.6 | async-start | bytes 524288 | tf_op jit(solution)/shard_map/all_to_all | solution.py:416
  172.9 3.4 %all-to-all-done.6 = bf16[8,8,2048]{2,1,0:T(8,128)(2,1)S(1)} async-done(((bf16[8,8,2048]{2,1,0:T(8,128)(2,1)}), bf16[8,8,2048]{2,1,0:T(8,128)(2,1)S(1)}, u32[]{:S(2)}, u32[]{:S(2)}) %all-to-all-start.6) | async-done | bytes 262176 | tf_op jit(solution)/shard_map/all_to_all | solution.py:416
  (146 shorter events, 42.2 us)
Async XLA Ops:
  1.4 13.3 %collective-permute-start = (bf16[146,128]{1,0:T(8,128)(2,1)S(1)}, bf16[146,128]{1,0:T(8,128)(2,1)S(1)}, u32[]{:S(2)}, u32[]{:S(2)}) collective-permute-start(bf16[146,128]{1,0:T(8,128)(2,1)S(1)} %pad_maximum_fusion.11), channel_id=1, source_target_pairs={{0,1},{1,0},{2,3},{3,2},{4,5},{5,4},{6,7},{7,6},{8,9},{9,8},{10,11... | collective-permute-start | bytes 112136 | tf_op jit(solution)/shard_map/ppermute | solution.py:37
  15.8 17.5 %all-to-all-start = ((bf16[8,144,128]{2,1,0:T(8,128)(2,1)}), bf16[8,144,128]{2,1,0:T(8,128)(2,1)S(1)}, u32[]{:S(2)}, u32[]{:S(2)}) async-start(bf16[8,144,128]{2,1,0:T(8,128)(2,1)} %broadcast_in_dim.69), calls=%async_computation | async-start | bytes 589824 | tf_op jit(solution)/shard_map/all_to_all | solution.py:326
  34.2 16.4 %collective-permute-start.1 = (bf16[8,144,128]{2,1,0:T(8,128)(2,1)S(1)}, bf16[8,144,128]{2,1,0:T(8,128)(2,1)S(1)}, u32[]{:S(2)}, u32[]{:S(2)}) collective-permute-start(bf16[8,144,128]{2,1,0:T(8,128)(2,1)S(1)} %all-to-all-done), channel_id=1, source_target_pairs={{0,32},{32,0},{1,33},{33,1},{2,34},{34,2},{3,35},{35,3},{4,36},{36... | collective-permute-start | bytes 884744 | tf_op jit(solution)/shard_map/ppermute | solution.py:37
  36.4 26.2 %all-to-all-start.1 = ((bf16[8,144,256]{2,1,0:T(8,128)(2,1)}), bf16[8,144,256]{2,1,0:T(8,128)(2,1)S(1)}, u32[]{:S(2)}, u32[]{:S(2)}) async-start(bf16[8,144,256]{2,1,0:T(8,128)(2,1)} %broadcast_in_dim.70), calls=%async_computation.1 | async-start | bytes 1179648 | tf_op jit(solution)/shard_map/all_to_all | solution.py:332
  47.0 27.6 %collective-permute-start.3 = (bf16[576,1024]{1,0:T(8,128)(2,1)}, bf16[576,1024]{1,0:T(8,128)(2,1)S(1)}, u32[]{:S(2)}, u32[]{:S(2)}) collective-permute-start(bf16[576,1024]{1,0:T(8,128)(2,1)} %bitcast.9), channel_id=1, source_target_pairs={{0,1},{1,0},{2,3},{3,2},{4,5},{5,4},{6,7},{7,6},{8,9},{9,8},{10,11... | collective-permute-start | bytes 3538952 | tf_op jit(solution)/shard_map/ppermute | solution.py:37
  51.6 16.5 %collective-permute-start.2 = (bf16[2,8,144,128]{3,2,1,0:T(8,128)(2,1)}, bf16[2,8,144,128]{3,2,1,0:T(8,128)(2,1)S(1)}, u32[]{:S(2)}, u32[]{:S(2)}) collective-permute-start(bf16[2,8,144,128]{3,2,1,0:T(8,128)(2,1)} %pad_maximum_fusion.4), channel_id=1, source_target_pairs={{0,16},{16,0},{1,17},{17,1},{2,18},{18,2},{3,19},{19,3},{4,20},{20... | collective-permute-start | bytes 1769480 | tf_op jit(solution)/shard_map/ppermute | solution.py:37
  63.5 18.9 %all-to-all-start.2 = ((bf16[8,256,128]{2,1,0:T(8,128)(2,1)}), bf16[8,256,128]{2,1,0:T(8,128)(2,1)}, u32[]{:S(2)}, u32[]{:S(2)}) async-start(bf16[8,256,128]{2,1,0:T(8,128)(2,1)} %broadcast_in_dim.71), calls=%async_computation.2 | async-start | bytes 1048576 | tf_op jit(solution)/shard_map/all_to_all | solution.py:343
  75.3 10.1 %copy-start.10 = (f32[64,64]{1,0:T(8,128)S(1)}, f32[64,64]{1,0:T(8,128)}, u32[]{:S(2)}) copy-start(f32[64,64]{1,0:T(8,128)} %get-tuple-element.68) | copy-start | bytes 49156
  75.3 10.1 %copy-start.11 = (f32[64,64]{1,0:T(8,128)S(1)}, f32[64,64]{1,0:T(8,128)}, u32[]{:S(2)}) copy-start(f32[64,64]{1,0:T(8,128)} %get-tuple-element.69) | copy-start | bytes 49156
  75.3 10.9 %copy-start.20 = (s32[32]{0:T(128)S(1)}, s32[32]{0:T(128)}, u32[]{:S(2)}) copy-start(s32[32]{0:T(128)} %get-tuple-element.81) | copy-start | bytes 388
  82.3 11.3 %collective-permute-start.5 = (bf16[8,256,128]{2,1,0:T(8,128)(2,1)}, bf16[8,256,128]{2,1,0:T(8,128)(2,1)S(1)}, u32[]{:S(2)}, u32[]{:S(2)}) collective-permute-start(bf16[8,256,128]{2,1,0:T(8,128)(2,1)} %all-to-all-done.2), channel_id=1, source_target_pairs={{0,32},{32,0},{1,33},{33,1},{2,34},{34,2},{3,35},{35,3},{4,36},{36... | collective-permute-start | bytes 1572872 | tf_op jit(solution)/shard_map/ppermute | solution.py:37
  86.3 30.5 %all-to-all-start.3 = ((bf16[8,288,128]{2,1,0:T(8,128)(2,1)}), bf16[8,288,128]{2,1,0:T(8,128)(2,1)S(1)}, u32[]{:S(2)}, u32[]{:S(2)}) async-start(bf16[8,288,128]{2,1,0:T(8,128)(2,1)} %project_queries.1), calls=%async_computation.3 | async-start | bytes 1179648 | tf_op jit(solution)/shard_map/all_to_all | solution.py:358
  94.8 9.7 %copy-start.13 = (bf16[128,64]{0,1:T(8,128)(2,1)S(1)}, bf16[128,64]{0,1:T(8,128)(2,1)}, u32[]{:S(2)}) copy-start(bf16[128,64]{0,1:T(8,128)(2,1)} %param.17) | copy-start | bytes 49156
  94.8 12.9 %copy-start.19 = (s32[2]{0:T(128)S(1)}, s32[2]{0:T(128)}, u32[]{:S(2)}) copy-start(s32[2]{0:T(128)} %param.19) | copy-start | bytes 28
  95.6 17.3 %copy-start = (bf16[16,64,576]{2,1,0:T(8,128)(2,1)S(1)}, bf16[16,64,576]{2,1,0:T(8,128)(2,1)}, u32[]{:S(2)}) copy-start(bf16[16,64,576]{2,1,0:T(8,128)(2,1)} %param.18) | copy-start | bytes 3538948
  96.7 24.3 %collective-permute-start.6 = (bf16[2,8,256,128]{3,2,1,0:T(8,128)(2,1)}, bf16[2,8,256,128]{3,2,1,0:T(8,128)(2,1)}, u32[]{:S(2)}, u32[]{:S(2)}) collective-permute-start(bf16[2,8,256,128]{3,2,1,0:T(8,128)(2,1)} %pad_maximum_fusion.2), channel_id=1, source_target_pairs={{0,16},{16,0},{1,17},{17,1},{2,18},{18,2},{3,19},{19,3},{4,20},{20... | collective-permute-start | bytes 3145736 | tf_op jit(solution)/shard_map/ppermute | solution.py:37
  104.5 8.4 %collective-permute-start.4 = (bf16[64,128]{1,0:T(8,128)(2,1)S(1)}, bf16[64,128]{1,0:T(8,128)(2,1)S(1)}, u32[]{:S(2)}, u32[]{:S(2)}) collective-permute-start(bf16[64,128]{1,0:T(8,128)(2,1)S(1)} %bitcast.117), channel_id=1, source_target_pairs={{0,8},{8,0},{1,9},{9,1},{2,10},{10,2},{3,11},{11,3},{4,12},{12,4},... | collective-permute-start | bytes 49160 | tf_op jit(solution)/shard_map/ppermute | solution.py:37
  117.6 23.4 %all-to-all-start.4 = ((bf16[8,128,128]{2,1,0:T(8,128)(2,1)}), bf16[8,128,128]{2,1,0:T(8,128)(2,1)S(1)}, u32[]{:S(2)}, u32[]{:S(2)}) async-start(bf16[8,128,128]{2,1,0:T(8,128)(2,1)} %broadcast_in_dim.77), calls=%async_computation.4 | async-start | bytes 524288 | tf_op jit(solution)/shard_map/all_to_all | solution.py:361
  123.1 17.9 %copy-start.2 = (bf16[8,128,512]{2,1,0:T(8,128)(2,1)}, bf16[8,128,512]{2,1,0:T(8,128)(2,1)S(1)}, u32[]{:S(2)}) copy-start(bf16[8,128,512]{2,1,0:T(8,128)(2,1)S(1)} %get-tuple-element.38) | copy-start | bytes 3145732
  141.0 8.5 %collective-permute-start.7 = (bf16[8,128,128]{2,1,0:T(8,128)(2,1)S(1)}, bf16[8,128,128]{2,1,0:T(8,128)(2,1)S(1)}, u32[]{:S(2)}, u32[]{:S(2)}) collective-permute-start(bf16[8,128,128]{2,1,0:T(8,128)(2,1)S(1)} %all-to-all-done.4), channel_id=1, source_target_pairs={{0,32},{32,0},{1,33},{33,1},{2,34},{34,2},{3,35},{35,3},{4,36},{36... | collective-permute-start | bytes 786440 | tf_op jit(solution)/shard_map/ppermute | solution.py:37
  144.2 18.1 %all-to-all-start.5 = ((bf16[8,224,128]{2,1,0:T(8,128)(2,1)}), bf16[8,224,128]{2,1,0:T(8,128)(2,1)S(1)}, u32[]{:S(2)}, u32[]{:S(2)}) async-start(bf16[8,224,128]{2,1,0:T(8,128)(2,1)} %bitcast.36), calls=%async_computation.5 | async-start | bytes 917504 | tf_op jit(solution)/shard_map/all_to_all | solution.py:399
  149.6 5.5 %collective-permute-start.8 = (bf16[2,8,128,128]{3,2,1,0:T(8,128)(2,1)S(1)}, bf16[2,8,128,128]{3,2,1,0:T(8,128)(2,1)S(1)}, u32[]{:S(2)}, u32[]{:S(2)}) collective-permute-start(bf16[2,8,128,128]{3,2,1,0:T(8,128)(2,1)S(1)} %pad_maximum_fusion.5), channel_id=1, source_target_pairs={{0,16},{16,0},{1,17},{17,1},{2,18},{18,2},{3,19},{19,3},{4,20},{20... | collective-permute-start | bytes 1572872 | tf_op jit(solution)/shard_map/ppermute | solution.py:37
  155.3 12.5 %copy-start.15 = (s32[2]{0:T(128)S(1)}, s32[2]{0:T(128)}, u32[]{:S(2)}) copy-start(s32[2]{0:T(128)} %param.20) | copy-start | bytes 28
  164.4 12.0 %all-to-all-start.6 = ((bf16[8,8,2048]{2,1,0:T(8,128)(2,1)}), bf16[8,8,2048]{2,1,0:T(8,128)(2,1)S(1)}, u32[]{:S(2)}, u32[]{:S(2)}) async-start(bf16[8,8,2048]{2,1,0:T(8,128)(2,1)} %bitcast.50), calls=%async_computation.6 | async-start | bytes 524288 | tf_op jit(solution)/shard_map/all_to_all | solution.py:416
  (14 other events, 55.8 us)

commit v4 on v3

--- a/solution.py
+++ b/solution.py
@@ -14,6 +14,7 @@
 MP = ("zh", "zl", "xh")
 Z = ("zh", "zl")
 SIDE = 80
+CHUNKS = 8
 SCALE2 = (NOPE + ROPE) ** (-0.5) * 1.4426950408889634
 NEG = -1e30
 BF = jnp.bfloat16
@@ -148,11 +149,11 @@
     )(x, wide, own, down, cosine, sine)
 
 
-def attn_kernel(q_ref, k_ref, v_ref, km_ref, vm_ref, part_ref, gain_ref, cos_ref, sin_ref, o_ref):
+def attn_kernel(q_ref, k_ref, v_ref, km_ref, vm_ref, gain_ref, cos_ref, sin_ref, o_ref, s_ref):
     comp = jnp.zeros((SIDE, 128), F32)
-    for i in range(part_ref.shape[0]):
-        for j in range(part_ref.shape[1]):
-            comp = comp + part_ref[i, j].astype(F32)
+    for i in range(q_ref.shape[0]):
+        for j in range(q_ref.shape[1]):
+            comp = comp + q_ref[i, j, :SIDE].astype(F32)
     squares = jnp.zeros((16, 128), F32)
     for k in range(4):
         lat = comp[16 * k : 16 * k + 16]
@@ -166,59 +167,75 @@
     across = jnp.where(lane < 32, pltpu.roll(rot, 96, 1), pltpu.roll(rot, 32, 1))
     fresh.append(rot * cos_ref[...] + across * sin_ref[...])
     fresh = jnp.concatenate(fresh, axis=0).astype(BF)
-    q = []
-    for h in range(2):
-        lat = jnp.dot(
-            km_ref[h, 0], q_ref[h, 0, SIDE : SIDE + NOPE, :], preferred_element_type=F32
-        ).astype(BF)
-        q.append(jnp.concatenate([lat, q_ref[h, 0, SIDE + NOPE :, :]], axis=0))
-    q = jnp.concatenate(q, axis=1)
-    scores = jnp.dot(k_ref[...], q, preferred_element_type=F32)
-    top = jnp.max(scores, axis=0, keepdims=True) * SCALE2
-    weights = jnp.exp2(scores * SCALE2 - top)
-    total = jnp.sum(weights, axis=0, keepdims=True)
-    out = jnp.dot(v_ref[...], weights.astype(BF), preferred_element_type=F32).astype(BF)
-    a = jnp.dot(vm_ref[0, 0], out[:, :128], preferred_element_type=F32)
-    b = jnp.dot(vm_ref[1, 0], out[:, 128:], preferred_element_type=F32)
-    stats = jnp.concatenate(
-        split3(top) + split3(total) + [jnp.zeros((10, top.shape[1]), F32)], axis=0
-    )
-    a = jnp.concatenate([a, stats[:, :128]], axis=0)
-    b = jnp.concatenate([b, stats[:, 128:]], axis=0)
-    low = lax.broadcasted_iota(jnp.int32, a.shape, 1) < 64
-    rows = a.shape[0]
-    o_ref[0, 0, :rows, :] = jnp.where(low, a, pltpu.roll(b, 64, 1)).astype(BF)
-    o_ref[1, 0, :rows, :] = jnp.where(low, pltpu.roll(a, 64, 1), b).astype(BF)
-    o_ref[0, 0, rows:, :] = fresh
-    o_ref[1, 0, rows:, :] = fresh
+    step = k_ref.shape[0] // CHUNKS
+    pairs = q_ref.shape[1]
+    low = lax.broadcasted_iota(jnp.int32, (144, 128), 1) < 64
+
+    def query(i):
+        q = []
+        for h in range(2):
+            lat = jnp.dot(
+                km_ref[h, i], q_ref[h, i, SIDE : SIDE + NOPE, :], preferred_element_type=F32
+            ).astype(BF)
+            q.append(jnp.concatenate([lat, q_ref[h, i, SIDE + NOPE :, :]], axis=0))
+        return jnp.concatenate(q, axis=1)
+
+    def score(i, j, q, top):
+        part = jnp.dot(k_ref[j * step : (j + 1) * step, :], q, preferred_element_type=F32)
+        s_ref[i % 2, j * step : (j + 1) * step, :] = part
+        best = jnp.max(part, axis=0, keepdims=True)
+        return best if top is None else jnp.maximum(top, best)
+
+    top = None
+    q = query(0)
+    for j in range(CHUNKS):
+        top = score(0, j, q, top)
+    for i in range(pairs):
+        if i + 1 < pairs:
+            q = query(i + 1)
+        after = None
+        top = top * SCALE2
+        total = jnp.zeros((1, 256), F32)
+        out = jnp.zeros((LAT, 256), F32)
+        for j in range(CHUNKS):
+            if i + 1 < pairs:
+                after = score(i + 1, j, q, after)
+            weights = jnp.exp2(s_ref[i % 2, j * step : (j + 1) * step, :] * SCALE2 - top)
+            total = total + jnp.sum(weights, axis=0, keepdims=True)
+            out = out + jnp.dot(
+                v_ref[:, j * step : (j + 1) * step],
+                weights.astype(BF),
+                preferred_element_type=F32,
+            )
+        out = out.astype(BF)
+        a = jnp.dot(vm_ref[0, i], out[:, :128], preferred_element_type=F32)
+        b = jnp.dot(vm_ref[1, i], out[:, 128:], preferred_element_type=F32)
+        stats = jnp.concatenate(
+            split3(top) + split3(total) + [jnp.zeros((10, top.shape[1]), F32)], axis=0
+        )
+        a = jnp.concatenate([a, stats[:, :128]], axis=0)
+        b = jnp.concatenate([b, stats[:, 128:]], axis=0)
+        o_ref[0, i, :144, :] = jnp.where(low, a, pltpu.roll(b, 64, 1)).astype(BF)
+        o_ref[1, i, :144, :] = jnp.where(low, pltpu.roll(a, 64, 1), b).astype(BF)
+        o_ref[0, i, 144:, :] = fresh
+        o_ref[1, i, 144:, :] = fresh
+        top = after
 
 
 def attend(queries, keys, values_t, key_maps, value_maps, gain, cosine, sine):
-    groups, pairs, rows, lanes = queries.shape
+    _, pairs, _, lanes = queries.shape
     n = keys.shape[0]
     out_rows = 128 + 16 + SIDE
     return pl.pallas_call(
         attn_kernel,
-        grid=(pairs,),
-        in_specs=[
-            pl.BlockSpec((2, 1, rows, lanes), lambda i: (0, i, 0, 0)),
-            pl.BlockSpec((n, WIDTH + 16), lambda i: (0, 0)),
-            pl.BlockSpec((LAT, n), lambda i: (0, 0)),
-            pl.BlockSpec((2, 1, LAT, 128), lambda i: (0, i, 0, 0)),
-            pl.BlockSpec((2, 1, 128, LAT), lambda i: (0, i, 0, 0)),
-            pl.BlockSpec((groups, pairs, SIDE, lanes), lambda i: (0, 0, 0, 0)),
-            pl.BlockSpec((1, LAT), lambda i: (0, 0)),
-            pl.BlockSpec((16, 128), lambda i: (0, 0)),
-            pl.BlockSpec((16, 128), lambda i: (0, 0)),
-        ],
-        out_specs=pl.BlockSpec((2, 1, out_rows, lanes), lambda i: (0, i, 0, 0)),
         out_shape=jax.ShapeDtypeStruct((2, pairs, out_rows, lanes), BF),
+        scratch_shapes=[pltpu.VMEM((2, n, 2 * lanes), F32)],
         compiler_params=pltpu.CompilerParams(vmem_limit_bytes=48 * 1024 * 1024),
         cost_estimate=pl.CostEstimate(
             flops=2 * n * 8 * lanes * (WIDTH + LAT), transcendentals=n * 8 * lanes, bytes_accessed=6 << 20
         ),
         name="cache_attention",
-    )(queries, keys, values_t, key_maps, value_maps, queries, gain, cosine, sine)
+    )(queries, keys, values_t, key_maps, value_maps, gain, cosine, sine)
 
 
 def merge_kernel(part_ref, q_ref, km_ref, vm_ref, tb_ref, w_ref, o_ref, f_ref):
@@ -289,6 +306,22 @@
     )(parts, q_pair, key_maps, value_maps, tree_bias, late)
 
 
+def write_kernel(k_ref, c_ref, f_ref, o_ref):
+    chosen = c_ref[...]
+    placed = jnp.dot(chosen, f_ref[...], preferred_element_type=F32)
+    written = jnp.max(chosen.astype(F32), axis=1, keepdims=True) > 0.5
+    o_ref[...] = jnp.where(written, placed, k_ref[...].astype(F32)).astype(BF)
+
+
+def write(keys, chosen, fresh):
+    return pl.pallas_call(
+        write_kernel,
+        out_shape=jax.ShapeDtypeStruct(keys.shape, BF),
+        compiler_params=pltpu.CompilerParams(vmem_limit_bytes=48 * 1024 * 1024),
+        name="write_entries",
+    )(keys, chosen, fresh)
+
+
 def per_device(
     hidden,
     q_weight,
@@ -323,9 +356,10 @@
         ],
         axis=0,
     )
-    wide = lax.all_to_all(jnp.broadcast_to(pack[None], (8,) + pack.shape), "y", 0, 0, tiled=True)
-    keys_t, hid = lax.optimization_barrier((keys.T, hid))
-    other_t = swap(keys_t, "xh")
+    pack = jnp.broadcast_to(pack[None], (8,) + pack.shape)
+    pack, parents, page_table, cache_t = lax.optimization_barrier((pack, parents, page_table, keys))
+    wide = lax.all_to_all(pack, "y", 0, 0, tiled=True)
+    other_t = swap(cache_t.T, "xh")
     sent = jnp.concatenate([hid, kvb_weight[:, 0, :]], axis=0)
     sent = jnp.broadcast_to(sent[None], (8,) + sent.shape)
     wide, sent = lax.optimization_barrier((wide, sent))
@@ -353,13 +387,6 @@
     sign = jnp.where(jnp.arange(ROPE) < ROPE // 2, -1.0, 1.0)[None, :]
     mine_cos = jnp.pad(jnp.cos(mine), ((0, 0), (0, 128 - ROPE)))
     mine_sin = jnp.pad(jnp.sin(mine) * sign, ((0, 0), (0, 128 - ROPE)))
-    queries = project(full_x, wide, hid, down, cosine, sine)
-    queries, maps, other_t = lax.optimization_barrier((queries, maps, other_t))
-    queries = lax.all_to_all(queries, Z, 0, 0, tiled=True)
-    late = jnp.broadcast_to(late[None], (8,) + late.shape)
-    queries, late = lax.optimization_barrier((queries, late))
-    late = lax.all_to_all(late, "y", 0, 0, tiled=True)
-    maps = both(both(maps, "xl"), "c")
     slot_base = jnp.stack([mp_rank, mp_rank ^ 1]) * slots
     slot_ids = (slot_base[:, None] + jnp.arange(slots, dtype=jnp.int32)[None, :]).reshape(-1)
     page_ids = jnp.arange(reqs * page_table.shape[1], dtype=jnp.int32)
@@ -387,6 +414,15 @@
     )
     chosen = chosen.reshape(slots * page_len, tokens).astype(BF)
     all_keys, values_t = prepare(keys, other_t, mask)
+    queries = project(full_x, wide, hid, down, cosine, sine)
+    late = jnp.broadcast_to(late[None], (8,) + late.shape)
+    queries, maps, all_keys, values_t, late = lax.optimization_barrier(
+        (queries, maps, all_keys, values_t, late)
+    )
+    queries = lax.all_to_all(queries, Z, 0, 0, tiled=True)
+    queries, late = lax.optimization_barrier((queries, late))
+    late = lax.all_to_all(late, "y", 0, 0, tiled=True)
+    maps = both(both(maps, "xl"), "c")
     key_maps, value_maps = arrange(maps)
     queries = queries.reshape((2, 4) + queries.shape[1:])
     key_maps = key_maps.reshape((2, 4) + key_maps.shape[1:])
@@ -418,9 +454,7 @@
     row_index = (mp_rank * rows) % draft + jnp.arange(rows, dtype=jnp.int32)
     row_count = jnp.where(zh == 0, draft_count[0], draft_count[1])
     attended = jnp.where((row_index < row_count)[:, None], mine_rows, 0.0).astype(BF)
-    placed = jnp.dot(chosen, fresh, preferred_element_type=F32).astype(BF)
-    written = jnp.sum(chosen.astype(F32), axis=1, keepdims=True) > 0.5
-    new_cache = jnp.where(written, placed, keys).reshape(cache.shape)
+    new_cache = write(keys, chosen, fresh).reshape(cache.shape)
     return (attended, new_cache)
 
 

time: 181 us -> 199 us (1.099)
  waiting for transfers between devices: 48.1 us -> 61.5 us
  starting transfers between devices: 72.4 us -> 78.7 us
  local copies, waits for them, and re-layouts: 14.7 us -> 19 us
  Pallas kernels: 22.7 us -> 19.4 us
    all_to_all x1, waiting for transfers between devices: 0.01 us -> 16.5 us  [per_device(): queries = lax.all_to_all(queries, Z, 0, 0, tiled=True)]
    ppermute x9, waiting for transfers between devices: 16.9 us -> 26.2 us  [swap(): return lax.ppermute(x, axis, [(0, 1), (1, 0)])]
    all_to_all x1, waiting for transfers between devices: 5.57 us -> 0.01 us  [per_device(): lax.all_to_all(jnp.broadcast_to(maps[None], (8,) + maps.shape), 'y', 0, 0...]
    all_to_all x1, waiting for transfers between devices: 4.74 us -> 0.01 us  [per_device(): full_x = lax.all_to_all(sent, Z, 0, 0, tiled=True)]
    all_to_all x1, waiting for transfers between devices: 10.4 us -> 5.86 us  [per_device(): wide = lax.all_to_all(pack, 'y', 0, 0, tiled=True)]
    pallas_call x1 -> x2, Pallas kernels: 16.3 us -> 12.5 us  [the longest x1 10.9 us: attend(): pl.pallas_call(attn_kernel, out_shape=jax.ShapeDtypeStruct((2, pairs, out...]
    unnamed x42 -> x46, local copies, waits for them, and re-layouts: 3.86 us -> 6.96 us
    all_to_all x1, starting transfers between devices: 3.54 us -> 6 us  [per_device(): queries = lax.all_to_all(queries, Z, 0, 0, tiled=True)]
  transfers between devices with their start and end apart: 16 -> 16, of which waited for: 10 -> 9; matrix products, arithmetic and copies ran while one was open for 14% -> 10% of each run, Pallas kernels for 12% -> 9%
where the time goes in v4:
time: 199 us; the launch traced here: 197 us
  starting transfers between devices  78.7 us (40%)
  waiting for transfers between devices  61.5 us (31%)
  Pallas kernels  19.4 us (10%)
  local copies, waits for them, and re-layouts  19 us (10%)
  other arithmetic  13.3 us (7%)
  between operations  2.56 us (1%)
  matrix products  2.17 us (1%)
    ppermute x9, starting transfers between devices, swap(): return lax.ppermute(x, axis, [(0, 1), (1, 0)])  37 us
    ppermute x9, waiting for transfers between devices, swap(): return lax.ppermute(x, axis, [(0, 1), (1, 0)])  26.2 us
    all_to_all x1, waiting for transfers between devices, per_device(): queries = lax.all_to_all(queries, Z, 0, 0, tiled=True)  16.5 us
    pallas_call x1, Pallas kernels, attend(): pl.pallas_call(attn_kernel, out_shape=jax.ShapeDtypeStruct((2, pairs, out...  10.9 us
    all_to_all x1, starting transfers between devices, per_device(): full_x = lax.all_to_all(sent, Z, 0, 0, tiled=True)  10 us
    all_to_all x1, waiting for transfers between devices, per_device(): lax.all_to_all(partial.reshape((8,) + partial.shape[2:]), Z, 0, 0, tiled=...  7.34 us
    unnamed x46, local copies, waits for them, and re-layouts  6.96 us
    all_to_all x1, starting transfers between devices, per_device(): wide = lax.all_to_all(pack, 'y', 0, 0, tiled=True)  6.82 us
  transfers between devices with their start and end apart: 16, of which 9 were waited for; matrix products, arithmetic and copies ran while one was open for 10% of the time, Pallas kernels for 9%

profile of v4, /device:TPU:1, one launch (start us, length us, event | category | flops | bytes accessed | tf_op | source)
XLA Modules:
  0.0 196.6 jit_solution(3110304963375432288)
XLA Ops:
  1.5 5.5 %collective-permute-start = (bf16[146,128]{1,0:T(8,128)(2,1)S(1)}, bf16[146,128]{1,0:T(8,128)(2,1)S(1)}, u32[]{:S(2)}, u32[]{:S(2)}) collective-permute-start(bf16[146,128]{1,0:T(8,128)(2,1)S(1)} %pad_maximum_fusion.11), channel_id=1, source_target_pairs={{0,1},{1,0},{2,3},{3,2},{4,5},{5,4},{6,7},{7,6},{8,9},{9,8},{10,11... | collective-permute-start | bytes 112136 | tf_op jit(solution)/shard_map/ppermute | solution.py:38
  12.7 6.8 %all-to-all-start = ((bf16[8,144,128]{2,1,0:T(8,128)(2,1)}), bf16[8,144,128]{2,1,0:T(8,128)(2,1)S(1)}, u32[]{:S(2)}, u32[]{:S(2)}) async-start(bf16[8,144,128]{2,1,0:T(8,128)(2,1)} %broadcast_in_dim.62), calls=%async_computation | async-start | bytes 589824 | tf_op jit(solution)/shard_map/all_to_all | solution.py:361
  21.0 2.4 %collective-permute-start.3 = (bf16[576,1024]{1,0:T(8,128)(2,1)}, bf16[576,1024]{1,0:T(8,128)(2,1)}, u32[]{:S(2)}, u32[]{:S(2)}) collective-permute-start(bf16[576,1024]{1,0:T(8,128)(2,1)} %copy.45), channel_id=1, source_target_pairs={{0,1},{1,0},{2,3},{3,2},{4,5},{5,4},{6,7},{7,6},{8,9},{9,8},{10,11... | collective-permute-start | bytes 3538952 | tf_op jit(solution)/shard_map/ppermute | solution.py:38
  24.4 5.9 %all-to-all-done = bf16[8,144,128]{2,1,0:T(8,128)(2,1)S(1)} async-done(((bf16[8,144,128]{2,1,0:T(8,128)(2,1)}), bf16[8,144,128]{2,1,0:T(8,128)(2,1)S(1)}, u32[]{:S(2)}, u32[]{:S(2)}) %all-to-all-start) | async-done | bytes 294944 | tf_op jit(solution)/shard_map/all_to_all | solution.py:361
  34.9 10.0 %all-to-all-start.1 = ((bf16[8,144,256]{2,1,0:T(8,128)(2,1)}), bf16[8,144,256]{2,1,0:T(8,128)(2,1)S(1)}, u32[]{:S(2)}, u32[]{:S(2)}) async-start(bf16[8,144,256]{2,1,0:T(8,128)(2,1)} %broadcast_in_dim.63), calls=%async_computation.1 | async-start | bytes 1179648 | tf_op jit(solution)/shard_map/all_to_all | solution.py:366
  44.9 10.5 %collective-permute-done.1 = bf16[8,144,128]{2,1,0:T(8,128)(2,1)S(1)} collective-permute-done((bf16[8,144,128]{2,1,0:T(8,128)(2,1)S(1)}, bf16[8,144,128]{2,1,0:T(8,128)(2,1)S(1)}, u32[]{:S(2)}, u32[]{:S(2)}) %collective-permute-start.1) | collective-permute-done | bytes 294944 | tf_op jit(solution)/shard_map/ppermute | solution.py:38
  56.3 4.3 %collective-permute-start.2 = (bf16[2,8,144,128]{3,2,1,0:T(8,128)(2,1)}, bf16[2,8,144,128]{3,2,1,0:T(8,128)(2,1)S(1)}, u32[]{:S(2)}, u32[]{:S(2)}) collective-permute-start(bf16[2,8,144,128]{3,2,1,0:T(8,128)(2,1)} %pad_maximum_fusion.4), channel_id=1, source_target_pairs={{0,16},{16,0},{1,17},{17,1},{2,18},{18,2},{3,19},{19,3},{4,20},{20... | collective-permute-start | bytes 1769480 | tf_op jit(solution)/shard_map/ppermute | solution.py:38
  63.6 6.6 %all-to-all-start.2 = ((bf16[8,256,128]{2,1,0:T(8,128)(2,1)}), bf16[8,256,128]{2,1,0:T(8,128)(2,1)}, u32[]{:S(2)}, u32[]{:S(2)}) async-start(bf16[8,256,128]{2,1,0:T(8,128)(2,1)} %broadcast_in_dim.64), calls=%async_computation.2 | async-start | bytes 1048576 | tf_op jit(solution)/shard_map/all_to_all | solution.py:377
  73.0 10.6 %collective-permute-start.4 = (bf16[64,128]{1,0:T(8,128)(2,1)S(1)}, bf16[64,128]{1,0:T(8,128)(2,1)S(1)}, u32[]{:S(2)}, u32[]{:S(2)}) collective-permute-start(bf16[64,128]{1,0:T(8,128)(2,1)S(1)} %bitcast.118), channel_id=1, source_target_pairs={{0,8},{8,0},{1,9},{9,1},{2,10},{10,2},{3,11},{11,3},{4,12},{12,4},... | collective-permute-start | bytes 49160 | tf_op jit(solution)/shard_map/ppermute | solution.py:38
  85.6 3.8 %prepare_keys.1 = (bf16[2048,592]{1,0:T(8,128)(2,1)}, bf16[512,2048]{1,0:T(8,128)(2,1)S(1)}) custom-call(bf16[1024,576]{1,0:T(8,128)(2,1)S(1)} %bitcast.101, bf16[576,1024]{1,0:T(8,128)(2,1)} %collective-permute-done.3.k2t_ref, bf16[2048,16]{1,0:T(8,128)(2,1)S(1)} %copy-done.1), custom_call_target="tpu_custom_call" | custom-call | tf_op jit(solution)/shard_map/prepare_keys/pallas_call | solution.py:66
  93.0 2.4 %collective-permute-start.5 = (bf16[8,256,128]{2,1,0:T(8,128)(2,1)}, bf16[8,256,128]{2,1,0:T(8,128)(2,1)S(1)}, u32[]{:S(2)}, u32[]{:S(2)}) collective-permute-start(bf16[8,256,128]{2,1,0:T(8,128)(2,1)} %all-to-all-done.2), channel_id=1, source_target_pairs={{0,32},{32,0},{1,33},{33,1},{2,34},{34,2},{3,35},{35,3},{4,36},{36... | collective-permute-start | bytes 1572872 | tf_op jit(solution)/shard_map/ppermute | solution.py:38
  95.4 12.2 %collective-permute-done.5 = bf16[8,256,128]{2,1,0:T(8,128)(2,1)S(1)} collective-permute-done((bf16[8,256,128]{2,1,0:T(8,128)(2,1)}, bf16[8,256,128]{2,1,0:T(8,128)(2,1)S(1)}, u32[]{:S(2)}, u32[]{:S(2)}) %collective-permute-start.5) | collective-permute-done | bytes 524320 | tf_op jit(solution)/shard_map/ppermute | solution.py:38
  109.8 3.7 %collective-permute-start.6 = (bf16[2,8,256,128]{3,2,1,0:T(8,128)(2,1)}, bf16[2,8,256,128]{3,2,1,0:T(8,128)(2,1)}, u32[]{:S(2)}, u32[]{:S(2)}) collective-permute-start(bf16[2,8,256,128]{3,2,1,0:T(8,128)(2,1)} %pad_maximum_fusion.2), channel_id=1, source_target_pairs={{0,16},{16,0},{1,17},{17,1},{2,18},{18,2},{3,19},{19,3},{4,20},{20... | collective-permute-start | bytes 3145736 | tf_op jit(solution)/shard_map/ppermute | solution.py:38
  113.6 6.0 %all-to-all-start.3 = ((bf16[8,288,128]{2,1,0:T(8,128)(2,1)}), bf16[8,288,128]{2,1,0:T(8,128)(2,1)S(1)}, u32[]{:S(2)}, u32[]{:S(2)}) async-start(bf16[8,288,128]{2,1,0:T(8,128)(2,1)} %project_queries.1), calls=%async_computation.3 | async-start | bytes 1179648 | tf_op jit(solution)/shard_map/all_to_all | solution.py:422
  122.5 16.5 %all-to-all-done.3 = bf16[8,288,128]{2,1,0:T(8,128)(2,1)S(1)} async-done(((bf16[8,288,128]{2,1,0:T(8,128)(2,1)}), bf16[8,288,128]{2,1,0:T(8,128)(2,1)S(1)}, u32[]{:S(2)}, u32[]{:S(2)}) %all-to-all-start.3) | async-done | bytes 589856 | tf_op jit(solution)/shard_map/all_to_all | solution.py:422
  139.0 4.9 %all-to-all-start.4 = ((bf16[8,128,128]{2,1,0:T(8,128)(2,1)}), bf16[8,128,128]{2,1,0:T(8,128)(2,1)S(1)}, u32[]{:S(2)}, u32[]{:S(2)}) async-start(bf16[8,128,128]{2,1,0:T(8,128)(2,1)} %broadcast_in_dim.122), calls=%async_computation.4 | async-start | bytes 524288 | tf_op jit(solution)/shard_map/all_to_all | solution.py:424
  147.1 10.9 %cache_attention.1 = bf16[2,4,224,128]{3,2,1,0:T(8,128)(2,1)} custom-call(bf16[2,4,288,128]{3,2,1,0:T(8,128)(2,1)S(1)} %bitcast.103, bf16[2048,592]{1,0:T(8,128)(2,1)} %get-tuple-element.42.k_ref, bf16[512,2048]{1,0:T(8,128)(2,1)S(1)} %copy-done.7, bf16[2,4,512,128]{3,2,1,0:T(8,128)(2,1)S(1)} %bitcast.106, bf16[2,4,128,512]{3,2,1,0:T(8,128)(2,1)S(1)} %bitcast.108, ...), custom_call_target="tpu_custom_call" | custom-call | flops 4563402752 | bytes 6291456 | tf_op jit(solution)/shard_map/cache_attention/pallas_call | solution.py:229
  159.0 2.4 %collective-permute-start.7 = (bf16[8,128,128]{2,1,0:T(8,128)(2,1)S(1)}, bf16[8,128,128]{2,1,0:T(8,128)(2,1)S(1)}, u32[]{:S(2)}, u32[]{:S(2)}) collective-permute-start(bf16[8,128,128]{2,1,0:T(8,128)(2,1)S(1)} %all-to-all-done.4), channel_id=1, source_target_pairs={{0,32},{32,0},{1,33},{33,1},{2,34},{34,2},{3,35},{35,3},{4,36},{36... | collective-permute-start | bytes 786440 | tf_op jit(solution)/shard_map/ppermute | solution.py:38
  161.5 3.5 %all-to-all-start.5 = ((bf16[8,224,128]{2,1,0:T(8,128)(2,1)}), bf16[8,224,128]{2,1,0:T(8,128)(2,1)S(1)}, u32[]{:S(2)}, u32[]{:S(2)}) async-start(bf16[8,224,128]{2,1,0:T(8,128)(2,1)} %bitcast.36), calls=%async_computation.5 | async-start | bytes 917504 | tf_op jit(solution)/shard_map/all_to_all | solution.py:435
  165.0 3.0 %collective-permute-done.7 = bf16[8,128,128]{2,1,0:T(8,128)(2,1)S(1)} collective-permute-done((bf16[8,128,128]{2,1,0:T(8,128)(2,1)S(1)}, bf16[8,128,128]{2,1,0:T(8,128)(2,1)S(1)}, u32[]{:S(2)}, u32[]{:S(2)}) %collective-permute-start.7) | collective-permute-done | bytes 262176 | tf_op jit(solution)/shard_map/ppermute | solution.py:38
  168.1 3.5 %collective-permute-start.8 = (bf16[2,8,128,128]{3,2,1,0:T(8,128)(2,1)S(1)}, bf16[2,8,128,128]{3,2,1,0:T(8,128)(2,1)S(1)}, u32[]{:S(2)}, u32[]{:S(2)}) collective-permute-start(bf16[2,8,128,128]{3,2,1,0:T(8,128)(2,1)S(1)} %pad_maximum_fusion.5), channel_id=1, source_target_pairs={{0,16},{16,0},{1,17},{17,1},{2,18},{18,2},{3,19},{19,3},{4,20},{20... | collective-permute-start | bytes 1572872 | tf_op jit(solution)/shard_map/ppermute | solution.py:38
  173.4 7.3 %all-to-all-done.5.part_ref = bf16[8,224,128]{2,1,0:T(8,128)(2,1)S(1)} async-done(((bf16[8,224,128]{2,1,0:T(8,128)(2,1)}), bf16[8,224,128]{2,1,0:T(8,128)(2,1)S(1)}, u32[]{:S(2)}, u32[]{:S(2)}) %all-to-all-start.5) | async-done | bytes 458784 | tf_op jit(solution)/shard_map/all_to_all | solution.py:435
  183.4 3.8 %all-to-all-start.6 = ((bf16[8,8,2048]{2,1,0:T(8,128)(2,1)}), bf16[8,8,2048]{2,1,0:T(8,128)(2,1)S(1)}, u32[]{:S(2)}, u32[]{:S(2)}) async-start(bf16[8,8,2048]{2,1,0:T(8,128)(2,1)} %bitcast.105), calls=%async_computation.6 | async-start | bytes 524288 | tf_op jit(solution)/shard_map/all_to_all | solution.py:452
  190.3 5.6 %all-to-all-done.6 = bf16[8,8,2048]{2,1,0:T(8,128)(2,1)S(1)} async-done(((bf16[8,8,2048]{2,1,0:T(8,128)(2,1)}), bf16[8,8,2048]{2,1,0:T(8,128)(2,1)S(1)}, u32[]{:S(2)}, u32[]{:S(2)}) %all-to-all-start.6) | async-done | bytes 262176 | tf_op jit(solution)/shard_map/all_to_all | solution.py:452
  (146 shorter events, 42.0 us)
Async XLA Ops:
  0.6 19.0 %copy-start = (bf16[16,64,576]{2,1,0:T(8,128)(2,1)S(1)}, bf16[16,64,576]{2,1,0:T(8,128)(2,1)}, u32[]{:S(2)}) copy-start(bf16[16,64,576]{2,1,0:T(8,128)(2,1)} %param.18) | copy-start | bytes 3538948
  1.5 9.3 %collective-permute-start = (bf16[146,128]{1,0:T(8,128)(2,1)S(1)}, bf16[146,128]{1,0:T(8,128)(2,1)S(1)}, u32[]{:S(2)}, u32[]{:S(2)}) collective-permute-start(bf16[146,128]{1,0:T(8,128)(2,1)S(1)} %pad_maximum_fusion.11), channel_id=1, source_target_pairs={{0,1},{1,0},{2,3},{3,2},{4,5},{5,4},{6,7},{7,6},{8,9},{9,8},{10,11... | collective-permute-start | bytes 112136 | tf_op jit(solution)/shard_map/ppermute | solution.py:38
  12.7 17.5 %all-to-all-start = ((bf16[8,144,128]{2,1,0:T(8,128)(2,1)}), bf16[8,144,128]{2,1,0:T(8,128)(2,1)S(1)}, u32[]{:S(2)}, u32[]{:S(2)}) async-start(bf16[8,144,128]{2,1,0:T(8,128)(2,1)} %broadcast_in_dim.62), calls=%async_computation | async-start | bytes 589824 | tf_op jit(solution)/shard_map/all_to_all | solution.py:361
  21.0 41.6 %collective-permute-start.3 = (bf16[576,1024]{1,0:T(8,128)(2,1)}, bf16[576,1024]{1,0:T(8,128)(2,1)}, u32[]{:S(2)}, u32[]{:S(2)}) collective-permute-start(bf16[576,1024]{1,0:T(8,128)(2,1)} %copy.45), channel_id=1, source_target_pairs={{0,1},{1,0},{2,3},{3,2},{4,5},{5,4},{6,7},{7,6},{8,9},{9,8},{10,11... | collective-permute-start | bytes 3538952 | tf_op jit(solution)/shard_map/ppermute | solution.py:38
  23.6 37.2 %copy-start.16 = (s32[32]{0:T(128)}, s32[32]{0:T(128)S(1)}, u32[]{:S(2)}) copy-start(s32[32]{0:T(128)S(1)} %get-tuple-element.86) | copy-start | bytes 388
  31.1 24.3 %collective-permute-start.1 = (bf16[8,144,128]{2,1,0:T(8,128)(2,1)S(1)}, bf16[8,144,128]{2,1,0:T(8,128)(2,1)S(1)}, u32[]{:S(2)}, u32[]{:S(2)}) collective-permute-start(bf16[8,144,128]{2,1,0:T(8,128)(2,1)S(1)} %all-to-all-done), channel_id=1, source_target_pairs={{0,32},{32,0},{1,33},{33,1},{2,34},{34,2},{3,35},{35,3},{4,36},{36... | collective-permute-start | bytes 884744 | tf_op jit(solution)/shard_map/ppermute | solution.py:38
  33.4 27.3 %copy-start.9 = (s32[32,64]{1,0:T(8,128)}, s32[32,64]{1,0:T(8,128)S(1)}, u32[]{:S(2)}) copy-start(s32[32,64]{1,0:T(8,128)S(1)} %iota_add_fusion) | copy-start | bytes 24580
  34.9 25.7 %copy-start.13 = (f32[2,64]{1,0:T(2,128)}, f32[2,64]{1,0:T(2,128)S(1)}, u32[]{:S(2)}) copy-start(f32[2,64]{1,0:T(2,128)S(1)} %get-tuple-element.53) | copy-start | bytes 1540
  34.9 27.8 %all-to-all-start.1 = ((bf16[8,144,256]{2,1,0:T(8,128)(2,1)}), bf16[8,144,256]{2,1,0:T(8,128)(2,1)S(1)}, u32[]{:S(2)}, u32[]{:S(2)}) async-start(bf16[8,144,256]{2,1,0:T(8,128)(2,1)} %broadcast_in_dim.63), calls=%async_computation.1 | async-start | bytes 1179648 | tf_op jit(solution)/shard_map/all_to_all | solution.py:366
  56.3 6.1 %collective-permute-start.2 = (bf16[2,8,144,128]{3,2,1,0:T(8,128)(2,1)}, bf16[2,8,144,128]{3,2,1,0:T(8,128)(2,1)S(1)}, u32[]{:S(2)}, u32[]{:S(2)}) collective-permute-start(bf16[2,8,144,128]{3,2,1,0:T(8,128)(2,1)} %pad_maximum_fusion.4), channel_id=1, source_target_pairs={{0,16},{16,0},{1,17},{17,1},{2,18},{18,2},{3,19},{19,3},{4,20},{20... | collective-permute-start | bytes 1769480 | tf_op jit(solution)/shard_map/ppermute | solution.py:38
  63.6 28.7 %all-to-all-start.2 = ((bf16[8,256,128]{2,1,0:T(8,128)(2,1)}), bf16[8,256,128]{2,1,0:T(8,128)(2,1)}, u32[]{:S(2)}, u32[]{:S(2)}) async-start(bf16[8,256,128]{2,1,0:T(8,128)(2,1)} %broadcast_in_dim.64), calls=%async_computation.2 | async-start | bytes 1048576 | tf_op jit(solution)/shard_map/all_to_all | solution.py:377
  73.0 19.2 %collective-permute-start.4 = (bf16[64,128]{1,0:T(8,128)(2,1)S(1)}, bf16[64,128]{1,0:T(8,128)(2,1)S(1)}, u32[]{:S(2)}, u32[]{:S(2)}) collective-permute-start(bf16[64,128]{1,0:T(8,128)(2,1)S(1)} %bitcast.118), channel_id=1, source_target_pairs={{0,8},{8,0},{1,9},{9,1},{2,10},{10,2},{3,11},{11,3},{4,12},{12,4},... | collective-permute-start | bytes 49160 | tf_op jit(solution)/shard_map/ppermute | solution.py:38
  93.0 14.6 %collective-permute-start.5 = (bf16[8,256,128]{2,1,0:T(8,128)(2,1)}, bf16[8,256,128]{2,1,0:T(8,128)(2,1)S(1)}, u32[]{:S(2)}, u32[]{:S(2)}) collective-permute-start(bf16[8,256,128]{2,1,0:T(8,128)(2,1)} %all-to-all-done.2), channel_id=1, source_target_pairs={{0,32},{32,0},{1,33},{33,1},{2,34},{34,2},{3,35},{35,3},{4,36},{36... | collective-permute-start | bytes 1572872 | tf_op jit(solution)/shard_map/ppermute | solution.py:38
  109.8 34.1 %collective-permute-start.6 = (bf16[2,8,256,128]{3,2,1,0:T(8,128)(2,1)}, bf16[2,8,256,128]{3,2,1,0:T(8,128)(2,1)}, u32[]{:S(2)}, u32[]{:S(2)}) collective-permute-start(bf16[2,8,256,128]{3,2,1,0:T(8,128)(2,1)} %pad_maximum_fusion.2), channel_id=1, source_target_pairs={{0,16},{16,0},{1,17},{17,1},{2,18},{18,2},{3,19},{19,3},{4,20},{20... | collective-permute-start | bytes 3145736 | tf_op jit(solution)/shard_map/ppermute | solution.py:38
  113.6 25.4 %all-to-all-start.3 = ((bf16[8,288,128]{2,1,0:T(8,128)(2,1)}), bf16[8,288,128]{2,1,0:T(8,128)(2,1)S(1)}, u32[]{:S(2)}, u32[]{:S(2)}) async-start(bf16[8,288,128]{2,1,0:T(8,128)(2,1)} %project_queries.1), calls=%async_computation.3 | async-start | bytes 1179648 | tf_op jit(solution)/shard_map/all_to_all | solution.py:422
  139.0 20.0 %all-to-all-start.4 = ((bf16[8,128,128]{2,1,0:T(8,128)(2,1)}), bf16[8,128,128]{2,1,0:T(8,128)(2,1)S(1)}, u32[]{:S(2)}, u32[]{:S(2)}) async-start(bf16[8,128,128]{2,1,0:T(8,128)(2,1)} %broadcast_in_dim.122), calls=%async_computation.4 | async-start | bytes 524288 | tf_op jit(solution)/shard_map/all_to_all | solution.py:424
  159.0 9.0 %collective-permute-start.7 = (bf16[8,128,128]{2,1,0:T(8,128)(2,1)S(1)}, bf16[8,128,128]{2,1,0:T(8,128)(2,1)S(1)}, u32[]{:S(2)}, u32[]{:S(2)}) collective-permute-start(bf16[8,128,128]{2,1,0:T(8,128)(2,1)S(1)} %all-to-all-done.4), channel_id=1, source_target_pairs={{0,32},{32,0},{1,33},{33,1},{2,34},{34,2},{3,35},{35,3},{4,36},{36... | collective-permute-start | bytes 786440 | tf_op jit(solution)/shard_map/ppermute | solution.py:38
  161.5 19.2 %all-to-all-start.5 = ((bf16[8,224,128]{2,1,0:T(8,128)(2,1)}), bf16[8,224,128]{2,1,0:T(8,128)(2,1)S(1)}, u32[]{:S(2)}, u32[]{:S(2)}) async-start(bf16[8,224,128]{2,1,0:T(8,128)(2,1)} %bitcast.36), calls=%async_computation.5 | async-start | bytes 917504 | tf_op jit(solution)/shard_map/all_to_all | solution.py:435
  168.1 5.1 %collective-permute-start.8 = (bf16[2,8,128,128]{3,2,1,0:T(8,128)(2,1)S(1)}, bf16[2,8,128,128]{3,2,1,0:T(8,128)(2,1)S(1)}, u32[]{:S(2)}, u32[]{:S(2)}) collective-permute-start(bf16[2,8,128,128]{3,2,1,0:T(8,128)(2,1)S(1)} %pad_maximum_fusion.5), channel_id=1, source_target_pairs={{0,16},{16,0},{1,17},{17,1},{2,18},{18,2},{3,19},{19,3},{4,20},{20... | collective-permute-start | bytes 1572872 | tf_op jit(solution)/shard_map/ppermute | solution.py:38
  173.3 13.9 %copy-start.14 = (f32[2,64]{1,0:T(2,128)S(1)}, f32[2,64]{1,0:T(2,128)}, u32[]{:S(2)}) copy-start(f32[2,64]{1,0:T(2,128)} %copy-done.13) | copy-start | bytes 1540
  173.3 14.1 %slice-start = ((s32[32,64]{1,0:T(8,128)}), s32[16,64]{1,0:T(8,128)S(1)}, s32[]{:S(2)}) async-start(s32[32,64]{1,0:T(8,128)} %copy-done.9), calls=%async_computation.7 | async-start | bytes 16384 | tf_op jit(solution)/shard_map/slice | solution.py:413
  173.3 14.1 %copy-start.17 = (s32[32]{0:T(128)S(1)}, s32[32]{0:T(128)}, u32[]{:S(2)}) copy-start(s32[32]{0:T(128)} %copy-done.16) | copy-start | bytes 388
  173.4 14.1 %copy-start.21 = (s32[128]{0:T(128)S(1)}, s32[128]{0:T(128)}, u32[]{:S(2)}) copy-start(s32[128]{0:T(128)} %and_select_fusion) | copy-start | bytes 1540
  183.4 12.5 %all-to-all-start.6 = ((bf16[8,8,2048]{2,1,0:T(8,128)(2,1)}), bf16[8,8,2048]{2,1,0:T(8,128)(2,1)S(1)}, u32[]{:S(2)}, u32[]{:S(2)}) async-start(bf16[8,8,2048]{2,1,0:T(8,128)(2,1)} %bitcast.105), calls=%async_computation.6 | async-start | bytes 524288 | tf_op jit(solution)/shard_map/all_to_all | solution.py:452
  (16 other events, 76.0 us)

commit v5 on v4

--- a/solution.py
+++ b/solution.py
@@ -415,11 +415,11 @@
     chosen = chosen.reshape(slots * page_len, tokens).astype(BF)
     all_keys, values_t = prepare(keys, other_t, mask)
     queries = project(full_x, wide, hid, down, cosine, sine)
+    queries, maps, all_keys, values_t = lax.optimization_barrier(
+        (queries, maps, all_keys, values_t)
+    )
+    queries = lax.all_to_all(queries, Z, 0, 0, tiled=True)
     late = jnp.broadcast_to(late[None], (8,) + late.shape)
-    queries, maps, all_keys, values_t, late = lax.optimization_barrier(
-        (queries, maps, all_keys, values_t, late)
-    )
-    queries = lax.all_to_all(queries, Z, 0, 0, tiled=True)
     queries, late = lax.optimization_barrier((queries, late))
     late = lax.all_to_all(late, "y", 0, 0, tiled=True)
     maps = both(both(maps, "xl"), "c")

time: 199 us -> 185 us (0.930)
  the two profiles are of different devices: /device:TPU:1 before, /device:TPU:8 now
where the time goes in v5:
time: 185 us; the launch traced here: 184 us
  starting transfers between devices  86.6 us (47%)
  waiting for transfers between devices  40.6 us (22%)
  local copies, waits for them, and re-layouts  20.5 us (11%)
  Pallas kernels  18.7 us (10%)
  other arithmetic  12.7 us (7%)
  between operations  2.53 us (1%)
  matrix products  2.16 us (1%)
    ppermute x9, starting transfers between devices, swap(): return lax.ppermute(x, axis, [(0, 1), (1, 0)])  33.2 us
    ppermute x9, waiting for transfers between devices, swap(): return lax.ppermute(x, axis, [(0, 1), (1, 0)])  15.1 us
    pallas_call x1, Pallas kernels, attend(): pl.pallas_call(attn_kernel, out_shape=jax.ShapeDtypeStruct((2, pairs, out...  11 us
    all_to_all x1, starting transfers between devices, per_device(): full_x = lax.all_to_all(sent, Z, 0, 0, tiled=True)  10.3 us
    all_to_all x1, starting transfers between devices, per_device(): queries = lax.all_to_all(queries, Z, 0, 0, tiled=True)  10.3 us
    all_to_all x1, waiting for transfers between devices, per_device(): lax.all_to_all(partial.reshape((8,) + partial.shape[2:]), Z, 0, 0, tiled=...  9.92 us
    unnamed x54, local copies, waits for them, and re-layouts  7.79 us
    all_to_all x1, starting transfers between devices, per_device(): wide = lax.all_to_all(pack, 'y', 0, 0, tiled=True)  7.73 us
  transfers between devices with their start and end apart: 16, of which 8 were waited for; matrix products, arithmetic and copies ran while one was open for 13% of the time, Pallas kernels for 9%

profile of v5, /device:TPU:8, one launch (start us, length us, event | category | flops | bytes accessed | tf_op | source)
XLA Modules:
  0.0 183.8 jit_solution(9551820795347308892)
XLA Ops:
  1.5 4.9 %collective-permute-start = (bf16[146,128]{1,0:T(8,128)(2,1)S(1)}, bf16[146,128]{1,0:T(8,128)(2,1)S(1)}, u32[]{:S(2)}, u32[]{:S(2)}) collective-permute-start(bf16[146,128]{1,0:T(8,128)(2,1)S(1)} %pad_maximum_fusion.11), channel_id=1, source_target_pairs={{0,1},{1,0},{2,3},{3,2},{4,5},{5,4},{6,7},{7,6},{8,9},{9,8},{10,11... | collective-permute-start | bytes 112136 | tf_op jit(solution)/shard_map/ppermute | solution.py:38
  12.2 7.7 %all-to-all-start = ((bf16[8,144,128]{2,1,0:T(8,128)(2,1)}), bf16[8,144,128]{2,1,0:T(8,128)(2,1)S(1)}, u32[]{:S(2)}, u32[]{:S(2)}) async-start(bf16[8,144,128]{2,1,0:T(8,128)(2,1)} %broadcast_in_dim.62), calls=%async_computation | async-start | bytes 589824 | tf_op jit(solution)/shard_map/all_to_all | solution.py:361
  21.4 3.8 %collective-permute-start.3 = (bf16[576,1024]{1,0:T(8,128)(2,1)}, bf16[576,1024]{1,0:T(8,128)(2,1)}, u32[]{:S(2)}, u32[]{:S(2)}) collective-permute-start(bf16[576,1024]{1,0:T(8,128)(2,1)} %copy.45), channel_id=1, source_target_pairs={{0,1},{1,0},{2,3},{3,2},{4,5},{5,4},{6,7},{7,6},{8,9},{9,8},{10,11... | collective-permute-start | bytes 3538952 | tf_op jit(solution)/shard_map/ppermute | solution.py:38
  27.7 2.9 %all-to-all-done = bf16[8,144,128]{2,1,0:T(8,128)(2,1)S(1)} async-done(((bf16[8,144,128]{2,1,0:T(8,128)(2,1)}), bf16[8,144,128]{2,1,0:T(8,128)(2,1)S(1)}, u32[]{:S(2)}, u32[]{:S(2)}) %all-to-all-start) | async-done | bytes 294944 | tf_op jit(solution)/shard_map/all_to_all | solution.py:361
  31.4 2.5 %collective-permute-start.1 = (bf16[8,144,128]{2,1,0:T(8,128)(2,1)S(1)}, bf16[8,144,128]{2,1,0:T(8,128)(2,1)S(1)}, u32[]{:S(2)}, u32[]{:S(2)}) collective-permute-start(bf16[8,144,128]{2,1,0:T(8,128)(2,1)S(1)} %all-to-all-done), channel_id=1, source_target_pairs={{0,32},{32,0},{1,33},{33,1},{2,34},{34,2},{3,35},{35,3},{4,36},{36... | collective-permute-start | bytes 884744 | tf_op jit(solution)/shard_map/ppermute | solution.py:38
  33.9 10.3 %all-to-all-start.1 = ((bf16[8,144,256]{2,1,0:T(8,128)(2,1)}), bf16[8,144,256]{2,1,0:T(8,128)(2,1)S(1)}, u32[]{:S(2)}, u32[]{:S(2)}) async-start(bf16[8,144,256]{2,1,0:T(8,128)(2,1)} %broadcast_in_dim.63), calls=%async_computation.1 | async-start | bytes 1179648 | tf_op jit(solution)/shard_map/all_to_all | solution.py:366
  44.4 12.0 %collective-permute-done.1 = bf16[8,144,128]{2,1,0:T(8,128)(2,1)S(1)} collective-permute-done((bf16[8,144,128]{2,1,0:T(8,128)(2,1)S(1)}, bf16[8,144,128]{2,1,0:T(8,128)(2,1)S(1)}, u32[]{:S(2)}, u32[]{:S(2)}) %collective-permute-start.1) | collective-permute-done | bytes 294944 | tf_op jit(solution)/shard_map/ppermute | solution.py:38
  57.4 1.9 %collective-permute-start.2 = (bf16[2,8,144,128]{3,2,1,0:T(8,128)(2,1)}, bf16[2,8,144,128]{3,2,1,0:T(8,128)(2,1)S(1)}, u32[]{:S(2)}, u32[]{:S(2)}) collective-permute-start(bf16[2,8,144,128]{3,2,1,0:T(8,128)(2,1)} %pad_maximum_fusion.4), channel_id=1, source_target_pairs={{0,16},{16,0},{1,17},{17,1},{2,18},{18,2},{3,19},{19,3},{4,20},{20... | collective-permute-start | bytes 1769480 | tf_op jit(solution)/shard_map/ppermute | solution.py:38
  61.7 7.2 %all-to-all-start.2 = ((bf16[8,256,128]{2,1,0:T(8,128)(2,1)}), bf16[8,256,128]{2,1,0:T(8,128)(2,1)}, u32[]{:S(2)}, u32[]{:S(2)}) async-start(bf16[8,256,128]{2,1,0:T(8,128)(2,1)} %broadcast_in_dim.64), calls=%async_computation.2 | async-start | bytes 1048576 | tf_op jit(solution)/shard_map/all_to_all | solution.py:377
  73.0 3.8 %prepare_keys.1 = (bf16[2048,592]{1,0:T(8,128)(2,1)}, bf16[512,2048]{1,0:T(8,128)(2,1)S(1)}) custom-call(bf16[1024,576]{1,0:T(8,128)(2,1)S(1)} %bitcast.101, bf16[576,1024]{1,0:T(8,128)(2,1)} %collective-permute-done.3.k2t_ref, bf16[2048,16]{1,0:T(8,128)(2,1)S(1)} %copy-done.2), custom_call_target="tpu_custom_call" | custom-call | tf_op jit(solution)/shard_map/prepare_keys/pallas_call | solution.py:66
  79.7 6.0 %all-to-all-done.2 = bf16[8,256,128]{2,1,0:T(8,128)(2,1)} async-done(((bf16[8,256,128]{2,1,0:T(8,128)(2,1)}), bf16[8,256,128]{2,1,0:T(8,128)(2,1)}, u32[]{:S(2)}, u32[]{:S(2)}) %all-to-all-start.2) | async-done | bytes 524320 | tf_op jit(solution)/shard_map/all_to_all | solution.py:377
  85.7 2.7 %collective-permute-start.5 = (bf16[8,256,128]{2,1,0:T(8,128)(2,1)}, bf16[8,256,128]{2,1,0:T(8,128)(2,1)S(1)}, u32[]{:S(2)}, u32[]{:S(2)}) collective-permute-start(bf16[8,256,128]{2,1,0:T(8,128)(2,1)} %all-to-all-done.2), channel_id=1, source_target_pairs={{0,32},{32,0},{1,33},{33,1},{2,34},{34,2},{3,35},{35,3},{4,36},{36... | collective-permute-start | bytes 1572872 | tf_op jit(solution)/shard_map/ppermute | solution.py:38
  89.7 10.3 %all-to-all-start.3 = ((bf16[8,288,128]{2,1,0:T(8,128)(2,1)}), bf16[8,288,128]{2,1,0:T(8,128)(2,1)S(1)}, u32[]{:S(2)}, u32[]{:S(2)}) async-start(bf16[8,288,128]{2,1,0:T(8,128)(2,1)} %copy-done.1), calls=%async_computation.3 | async-start | bytes 1179648 | tf_op jit(solution)/shard_map/all_to_all | solution.py:421
  102.9 1.9 %collective-permute-start.6 = (bf16[2,8,256,128]{3,2,1,0:T(8,128)(2,1)}, bf16[2,8,256,128]{3,2,1,0:T(8,128)(2,1)}, u32[]{:S(2)}, u32[]{:S(2)}) collective-permute-start(bf16[2,8,256,128]{3,2,1,0:T(8,128)(2,1)} %pad_maximum_fusion.2), channel_id=1, source_target_pairs={{0,16},{16,0},{1,17},{17,1},{2,18},{18,2},{3,19},{19,3},{4,20},{20... | collective-permute-start | bytes 3145736 | tf_op jit(solution)/shard_map/ppermute | solution.py:38
  106.4 10.9 %collective-permute-start.4 = (bf16[64,128]{1,0:T(8,128)(2,1)S(1)}, bf16[64,128]{1,0:T(8,128)(2,1)S(1)}, u32[]{:S(2)}, u32[]{:S(2)}) collective-permute-start(bf16[64,128]{1,0:T(8,128)(2,1)S(1)} %bitcast.118), channel_id=1, source_target_pairs={{0,8},{8,0},{1,9},{9,1},{2,10},{10,2},{3,11},{11,3},{4,12},{12,4},... | collective-permute-start | bytes 49160 | tf_op jit(solution)/shard_map/ppermute | solution.py:38
  117.5 1.6 collective-permute-done.4
  119.9 6.4 %all-to-all-start.4 = ((bf16[8,128,128]{2,1,0:T(8,128)(2,1)}), bf16[8,128,128]{2,1,0:T(8,128)(2,1)}, u32[]{:S(2)}, u32[]{:S(2)}) async-start(bf16[8,128,128]{2,1,0:T(8,128)(2,1)} %broadcast_in_dim.122), calls=%async_computation.4 | async-start | bytes 524288 | tf_op jit(solution)/shard_map/all_to_all | solution.py:424
  129.4 11.0 %cache_attention.1 = bf16[2,4,224,128]{3,2,1,0:T(8,128)(2,1)} custom-call(bf16[2,4,288,128]{3,2,1,0:T(8,128)(2,1)S(1)} %bitcast.103, bf16[2048,592]{1,0:T(8,128)(2,1)} %get-tuple-element.40.k_ref, bf16[512,2048]{1,0:T(8,128)(2,1)S(1)} %copy-done.8, bf16[2,4,512,128]{3,2,1,0:T(8,128)(2,1)S(1)} %bitcast.106, bf16[2,4,128,512]{3,2,1,0:T(8,128)(2,1)S(1)} %bitcast.108, ...), custom_call_target="tpu_custom_call" | custom-call | flops 4563402752 | bytes 6291456 | tf_op jit(solution)/shard_map/cache_attention/pallas_call | solution.py:229
  141.4 2.7 %collective-permute-start.7 = (bf16[8,128,128]{2,1,0:T(8,128)(2,1)}, bf16[8,128,128]{2,1,0:T(8,128)(2,1)S(1)}, u32[]{:S(2)}, u32[]{:S(2)}) collective-permute-start(bf16[8,128,128]{2,1,0:T(8,128)(2,1)} %all-to-all-done.4), channel_id=1, source_target_pairs={{0,32},{32,0},{1,33},{33,1},{2,34},{34,2},{3,35},{35,3},{4,36},{36... | collective-permute-start | bytes 786440 | tf_op jit(solution)/shard_map/ppermute | solution.py:38
  144.2 7.4 %all-to-all-start.5 = ((bf16[8,224,128]{2,1,0:T(8,128)(2,1)}), bf16[8,224,128]{2,1,0:T(8,128)(2,1)S(1)}, u32[]{:S(2)}, u32[]{:S(2)}) async-start(bf16[8,224,128]{2,1,0:T(8,128)(2,1)} %bitcast.36), calls=%async_computation.5 | async-start | bytes 917504 | tf_op jit(solution)/shard_map/all_to_all | solution.py:435
  152.6 1.9 %collective-permute-start.8 = (bf16[2,8,128,128]{3,2,1,0:T(8,128)(2,1)S(1)}, bf16[2,8,128,128]{3,2,1,0:T(8,128)(2,1)S(1)}, u32[]{:S(2)}, u32[]{:S(2)}) collective-permute-start(bf16[2,8,128,128]{3,2,1,0:T(8,128)(2,1)S(1)} %pad_maximum_fusion.5), channel_id=1, source_target_pairs={{0,16},{16,0},{1,17},{17,1},{2,18},{18,2},{3,19},{19,3},{4,20},{20... | collective-permute-start | bytes 1572872 | tf_op jit(solution)/shard_map/ppermute | solution.py:38
  156.7 9.9 %all-to-all-done.5.part_ref = bf16[8,224,128]{2,1,0:T(8,128)(2,1)S(1)} async-done(((bf16[8,224,128]{2,1,0:T(8,128)(2,1)}), bf16[8,224,128]{2,1,0:T(8,128)(2,1)S(1)}, u32[]{:S(2)}, u32[]{:S(2)}) %all-to-all-start.5) | async-done | bytes 458784 | tf_op jit(solution)/shard_map/all_to_all | solution.py:435
  169.3 4.1 %all-to-all-start.6 = ((bf16[8,8,2048]{2,1,0:T(8,128)(2,1)}), bf16[8,8,2048]{2,1,0:T(8,128)(2,1)S(1)}, u32[]{:S(2)}, u32[]{:S(2)}) async-start(bf16[8,8,2048]{2,1,0:T(8,128)(2,1)} %bitcast.105), calls=%async_computation.6 | async-start | bytes 524288 | tf_op jit(solution)/shard_map/all_to_all | solution.py:452
  176.4 6.7 %all-to-all-done.6 = bf16[8,8,2048]{2,1,0:T(8,128)(2,1)S(1)} async-done(((bf16[8,8,2048]{2,1,0:T(8,128)(2,1)}), bf16[8,8,2048]{2,1,0:T(8,128)(2,1)S(1)}, u32[]{:S(2)}, u32[]{:S(2)}) %all-to-all-start.6) | async-done | bytes 262176 | tf_op jit(solution)/shard_map/all_to_all | solution.py:452
  (154 shorter events, 40.7 us)
Async XLA Ops:
  0.6 19.3 %copy-start = (bf16[16,64,576]{2,1,0:T(8,128)(2,1)S(1)}, bf16[16,64,576]{2,1,0:T(8,128)(2,1)}, u32[]{:S(2)}) copy-start(bf16[16,64,576]{2,1,0:T(8,128)(2,1)} %param.18) | copy-start | bytes 3538948
  1.5 8.8 %collective-permute-start = (bf16[146,128]{1,0:T(8,128)(2,1)S(1)}, bf16[146,128]{1,0:T(8,128)(2,1)S(1)}, u32[]{:S(2)}, u32[]{:S(2)}) collective-permute-start(bf16[146,128]{1,0:T(8,128)(2,1)S(1)} %pad_maximum_fusion.11), channel_id=1, source_target_pairs={{0,1},{1,0},{2,3},{3,2},{4,5},{5,4},{6,7},{7,6},{8,9},{9,8},{10,11... | collective-permute-start | bytes 112136 | tf_op jit(solution)/shard_map/ppermute | solution.py:38
  8.2 52.4 %copy-start.21 = (f32[32]{0:T(128)}, f32[32]{0:T(128)S(1)}, u32[]{:S(2)}) copy-start(f32[32]{0:T(128)S(1)} %multiply_power_fusion) | copy-start | bytes 388
  12.2 18.4 %all-to-all-start = ((bf16[8,144,128]{2,1,0:T(8,128)(2,1)}), bf16[8,144,128]{2,1,0:T(8,128)(2,1)S(1)}, u32[]{:S(2)}, u32[]{:S(2)}) async-start(bf16[8,144,128]{2,1,0:T(8,128)(2,1)} %broadcast_in_dim.62), calls=%async_computation | async-start | bytes 589824 | tf_op jit(solution)/shard_map/all_to_all | solution.py:361
  21.4 47.7 %collective-permute-start.3 = (bf16[576,1024]{1,0:T(8,128)(2,1)}, bf16[576,1024]{1,0:T(8,128)(2,1)}, u32[]{:S(2)}, u32[]{:S(2)}) collective-permute-start(bf16[576,1024]{1,0:T(8,128)(2,1)} %copy.45), channel_id=1, source_target_pairs={{0,1},{1,0},{2,3},{3,2},{4,5},{5,4},{6,7},{7,6},{8,9},{9,8},{10,11... | collective-permute-start | bytes 3538952 | tf_op jit(solution)/shard_map/ppermute | solution.py:38
  31.4 25.0 %collective-permute-start.1 = (bf16[8,144,128]{2,1,0:T(8,128)(2,1)S(1)}, bf16[8,144,128]{2,1,0:T(8,128)(2,1)S(1)}, u32[]{:S(2)}, u32[]{:S(2)}) collective-permute-start(bf16[8,144,128]{2,1,0:T(8,128)(2,1)S(1)} %all-to-all-done), channel_id=1, source_target_pairs={{0,32},{32,0},{1,33},{33,1},{2,34},{34,2},{3,35},{35,3},{4,36},{36... | collective-permute-start | bytes 884744 | tf_op jit(solution)/shard_map/ppermute | solution.py:38
  33.9 26.8 %all-to-all-start.1 = ((bf16[8,144,256]{2,1,0:T(8,128)(2,1)}), bf16[8,144,256]{2,1,0:T(8,128)(2,1)S(1)}, u32[]{:S(2)}, u32[]{:S(2)}) async-start(bf16[8,144,256]{2,1,0:T(8,128)(2,1)} %broadcast_in_dim.63), calls=%async_computation.1 | async-start | bytes 1179648 | tf_op jit(solution)/shard_map/all_to_all | solution.py:366
  44.4 24.7 %copy-start.11 = (s32[32,64]{1,0:T(8,128)}, s32[32,64]{1,0:T(8,128)S(1)}, u32[]{:S(2)}) copy-start(s32[32,64]{1,0:T(8,128)S(1)} %iota_add_fusion) | copy-start | bytes 24580
  57.4 11.5 %collective-permute-start.2 = (bf16[2,8,144,128]{3,2,1,0:T(8,128)(2,1)}, bf16[2,8,144,128]{3,2,1,0:T(8,128)(2,1)S(1)}, u32[]{:S(2)}, u32[]{:S(2)}) collective-permute-start(bf16[2,8,144,128]{3,2,1,0:T(8,128)(2,1)} %pad_maximum_fusion.4), channel_id=1, source_target_pairs={{0,16},{16,0},{1,17},{17,1},{2,18},{18,2},{3,19},{19,3},{4,20},{20... | collective-permute-start | bytes 1769480 | tf_op jit(solution)/shard_map/ppermute | solution.py:38
  61.7 24.0 %all-to-all-start.2 = ((bf16[8,256,128]{2,1,0:T(8,128)(2,1)}), bf16[8,256,128]{2,1,0:T(8,128)(2,1)}, u32[]{:S(2)}, u32[]{:S(2)}) async-start(bf16[8,256,128]{2,1,0:T(8,128)(2,1)} %broadcast_in_dim.64), calls=%async_computation.2 | async-start | bytes 1048576 | tf_op jit(solution)/shard_map/all_to_all | solution.py:377
  85.7 15.0 %collective-permute-start.5 = (bf16[8,256,128]{2,1,0:T(8,128)(2,1)}, bf16[8,256,128]{2,1,0:T(8,128)(2,1)S(1)}, u32[]{:S(2)}, u32[]{:S(2)}) collective-permute-start(bf16[8,256,128]{2,1,0:T(8,128)(2,1)} %all-to-all-done.2), channel_id=1, source_target_pairs={{0,32},{32,0},{1,33},{33,1},{2,34},{34,2},{3,35},{35,3},{4,36},{36... | collective-permute-start | bytes 1572872 | tf_op jit(solution)/shard_map/ppermute | solution.py:38
  89.7 29.4 %all-to-all-start.3 = ((bf16[8,288,128]{2,1,0:T(8,128)(2,1)}), bf16[8,288,128]{2,1,0:T(8,128)(2,1)S(1)}, u32[]{:S(2)}, u32[]{:S(2)}) async-start(bf16[8,288,128]{2,1,0:T(8,128)(2,1)} %copy-done.1), calls=%async_computation.3 | async-start | bytes 1179648 | tf_op jit(solution)/shard_map/all_to_all | solution.py:421
  102.9 23.3 %collective-permute-start.6 = (bf16[2,8,256,128]{3,2,1,0:T(8,128)(2,1)}, bf16[2,8,256,128]{3,2,1,0:T(8,128)(2,1)}, u32[]{:S(2)}, u32[]{:S(2)}) collective-permute-start(bf16[2,8,256,128]{3,2,1,0:T(8,128)(2,1)} %pad_maximum_fusion.2), channel_id=1, source_target_pairs={{0,16},{16,0},{1,17},{17,1},{2,18},{18,2},{3,19},{19,3},{4,20},{20... | collective-permute-start | bytes 3145736 | tf_op jit(solution)/shard_map/ppermute | solution.py:38
  106.4 12.6 %collective-permute-start.4 = (bf16[64,128]{1,0:T(8,128)(2,1)S(1)}, bf16[64,128]{1,0:T(8,128)(2,1)S(1)}, u32[]{:S(2)}, u32[]{:S(2)}) collective-permute-start(bf16[64,128]{1,0:T(8,128)(2,1)S(1)} %bitcast.118), channel_id=1, source_target_pairs={{0,8},{8,0},{1,9},{9,1},{2,10},{10,2},{3,11},{11,3},{4,12},{12,4},... | collective-permute-start | bytes 49160 | tf_op jit(solution)/shard_map/ppermute | solution.py:38
  119.9 21.5 %all-to-all-start.4 = ((bf16[8,128,128]{2,1,0:T(8,128)(2,1)}), bf16[8,128,128]{2,1,0:T(8,128)(2,1)}, u32[]{:S(2)}, u32[]{:S(2)}) async-start(bf16[8,128,128]{2,1,0:T(8,128)(2,1)} %broadcast_in_dim.122), calls=%async_computation.4 | async-start | bytes 524288 | tf_op jit(solution)/shard_map/all_to_all | solution.py:424
  141.4 10.2 %collective-permute-start.7 = (bf16[8,128,128]{2,1,0:T(8,128)(2,1)}, bf16[8,128,128]{2,1,0:T(8,128)(2,1)S(1)}, u32[]{:S(2)}, u32[]{:S(2)}) collective-permute-start(bf16[8,128,128]{2,1,0:T(8,128)(2,1)} %all-to-all-done.4), channel_id=1, source_target_pairs={{0,32},{32,0},{1,33},{33,1},{2,34},{34,2},{3,35},{35,3},{4,36},{36... | collective-permute-start | bytes 786440 | tf_op jit(solution)/shard_map/ppermute | solution.py:38
  144.2 22.4 %all-to-all-start.5 = ((bf16[8,224,128]{2,1,0:T(8,128)(2,1)}), bf16[8,224,128]{2,1,0:T(8,128)(2,1)S(1)}, u32[]{:S(2)}, u32[]{:S(2)}) async-start(bf16[8,224,128]{2,1,0:T(8,128)(2,1)} %bitcast.36), calls=%async_computation.5 | async-start | bytes 917504 | tf_op jit(solution)/shard_map/all_to_all | solution.py:435
  152.6 3.8 %collective-permute-start.8 = (bf16[2,8,128,128]{3,2,1,0:T(8,128)(2,1)S(1)}, bf16[2,8,128,128]{3,2,1,0:T(8,128)(2,1)S(1)}, u32[]{:S(2)}, u32[]{:S(2)}) collective-permute-start(bf16[2,8,128,128]{3,2,1,0:T(8,128)(2,1)S(1)} %pad_maximum_fusion.5), channel_id=1, source_target_pairs={{0,16},{16,0},{1,17},{17,1},{2,18},{18,2},{3,19},{19,3},{4,20},{20... | collective-permute-start | bytes 1572872 | tf_op jit(solution)/shard_map/ppermute | solution.py:38
  156.6 16.8 %copy-start.16 = (f32[2,64]{1,0:T(2,128)S(1)}, f32[2,64]{1,0:T(2,128)}, u32[]{:S(2)}) copy-start(f32[2,64]{1,0:T(2,128)} %copy-done.15) | copy-start | bytes 1540
  156.6 16.8 %copy-start.19 = (f32[2,64]{1,0:T(2,128)S(1)}, f32[2,64]{1,0:T(2,128)}, u32[]{:S(2)}) copy-start(f32[2,64]{1,0:T(2,128)} %get-tuple-element.50) | copy-start | bytes 1540
  156.6 16.8 %copy-start.25 = (s32[2]{0:T(128)S(1)}, s32[2]{0:T(128)}, u32[]{:S(2)}) copy-start(s32[2]{0:T(128)} %param.19) | copy-start | bytes 28
  156.6 16.9 %slice-start = ((s32[32,64]{1,0:T(8,128)}), s32[16,64]{1,0:T(8,128)S(1)}, s32[]{:S(2)}) async-start(s32[32,64]{1,0:T(8,128)} %copy-done.11), calls=%async_computation.7 | async-start | bytes 16384 | tf_op jit(solution)/shard_map/slice | solution.py:413
  156.7 17.0 %copy-start.18 = (s32[32]{0:T(128)S(1)}, s32[32]{0:T(128)}, u32[]{:S(2)}) copy-start(s32[32]{0:T(128)} %copy-done.17) | copy-start | bytes 388
  169.3 13.8 %all-to-all-start.6 = ((bf16[8,8,2048]{2,1,0:T(8,128)(2,1)}), bf16[8,8,2048]{2,1,0:T(8,128)(2,1)S(1)}, u32[]{:S(2)}, u32[]{:S(2)}) async-start(bf16[8,8,2048]{2,1,0:T(8,128)(2,1)} %bitcast.105), calls=%async_computation.6 | async-start | bytes 524288 | tf_op jit(solution)/shard_map/all_to_all | solution.py:452
  (20 other events, 80.7 us)

commit v6 on v5

--- a/solution.py
+++ b/solution.py
@@ -362,10 +362,10 @@
     other_t = swap(cache_t.T, "xh")
     sent = jnp.concatenate([hid, kvb_weight[:, 0, :]], axis=0)
     sent = jnp.broadcast_to(sent[None], (8,) + sent.shape)
-    wide, sent = lax.optimization_barrier((wide, sent))
+    wide, sent, late = lax.optimization_barrier((wide, sent, out_weight.T))
     full_x = lax.all_to_all(sent, Z, 0, 0, tiled=True)
-    late, full_x = lax.optimization_barrier((out_weight.T, full_x))
     late = both(late, "zh").reshape(128, 128)
+    late, full_x = lax.optimization_barrier((late, full_x))
     wide = both(both(wide, "xl"), "c")
     wide, other_t = lax.optimization_barrier((wide, other_t))
     down = wide[..., 96 : 96 + 2 * cols, :].transpose(2, 1, 0, 3, 4).reshape(32, 2, cols, 128)
@@ -413,16 +413,14 @@
         slot_req[:slots, None, None] == token_req, key_pos[:slots, :, None] == write_at
     )
     chosen = chosen.reshape(slots * page_len, tokens).astype(BF)
-    all_keys, values_t = prepare(keys, other_t, mask)
     queries = project(full_x, wide, hid, down, cosine, sine)
-    queries, maps, all_keys, values_t = lax.optimization_barrier(
-        (queries, maps, all_keys, values_t)
-    )
+    queries, maps, other_t = lax.optimization_barrier((queries, maps, other_t))
     queries = lax.all_to_all(queries, Z, 0, 0, tiled=True)
     late = jnp.broadcast_to(late[None], (8,) + late.shape)
     queries, late = lax.optimization_barrier((queries, late))
     late = lax.all_to_all(late, "y", 0, 0, tiled=True)
     maps = both(both(maps, "xl"), "c")
+    all_keys, values_t = prepare(keys, other_t, mask)
     key_maps, value_maps = arrange(maps)
     queries = queries.reshape((2, 4) + queries.shape[1:])
     key_maps = key_maps.reshape((2, 4) + key_maps.shape[1:])

time: 185 us -> 186 us (level)
  the two profiles are of different devices: /device:TPU:8 before, /device:TPU:1 now
where the time goes in v6:
time: 186 us; the launch traced here: 185 us
  starting transfers between devices  77.7 us (42%)
  waiting for transfers between devices  48.5 us (26%)
  local copies, waits for them, and re-layouts  19 us (10%)
  Pallas kernels  18.7 us (10%)
  other arithmetic  16 us (9%)
  between operations  2.56 us (1%)
  matrix products  2.17 us (1%)
    ppermute x9, starting transfers between devices, swap(): return lax.ppermute(x, axis, [(0, 1), (1, 0)])  32.4 us
    all_to_all x1, waiting for transfers between devices, per_device(): lax.all_to_all(jnp.broadcast_to(maps[None], (8,) + maps.shape), 'y', 0, 0...  14.1 us
    pallas_call x1, Pallas kernels, attend(): pl.pallas_call(attn_kernel, out_shape=jax.ShapeDtypeStruct((2, pairs, out...  11 us
    all_to_all x1, starting transfers between devices, per_device(): queries = lax.all_to_all(queries, Z, 0, 0, tiled=True)  10.4 us
    all_to_all x1, starting transfers between devices, per_device(): full_x = lax.all_to_all(sent, Z, 0, 0, tiled=True)  10 us
    all_to_all x1, waiting for transfers between devices, per_device(): queries = lax.all_to_all(queries, Z, 0, 0, tiled=True)  8.08 us
    ppermute x9, waiting for transfers between devices, swap(): return lax.ppermute(x, axis, [(0, 1), (1, 0)])  8.07 us
    all_to_all x1, waiting for transfers between devices, per_device(): lax.all_to_all(partial.reshape((8,) + partial.shape[2:]), Z, 0, 0, tiled=...  7.66 us
  transfers between devices with their start and end apart: 16, of which 8 were waited for; matrix products, arithmetic and copies ran while one was open for 15% of the time, Pallas kernels for 9%

profile of v6, /device:TPU:1, one launch (start us, length us, event | category | flops | bytes accessed | tf_op | source)
XLA Modules:
  0.0 184.6 jit_solution(6779972378103947394)
XLA Ops:
  1.5 5.5 %collective-permute-start = (bf16[146,128]{1,0:T(8,128)(2,1)S(1)}, bf16[146,128]{1,0:T(8,128)(2,1)S(1)}, u32[]{:S(2)}, u32[]{:S(2)}) collective-permute-start(bf16[146,128]{1,0:T(8,128)(2,1)S(1)} %pad_maximum_fusion.11), channel_id=1, source_target_pairs={{0,1},{1,0},{2,3},{3,2},{4,5},{5,4},{6,7},{7,6},{8,9},{9,8},{10,11... | collective-permute-start | bytes 112136 | tf_op jit(solution)/shard_map/ppermute | solution.py:38
  13.8 6.8 %all-to-all-start = ((bf16[8,144,128]{2,1,0:T(8,128)(2,1)}), bf16[8,144,128]{2,1,0:T(8,128)(2,1)S(1)}, u32[]{:S(2)}, u32[]{:S(2)}) async-start(bf16[8,144,128]{2,1,0:T(8,128)(2,1)} %broadcast_in_dim.60), calls=%async_computation | async-start | bytes 589824 | tf_op jit(solution)/shard_map/all_to_all | solution.py:361
  22.1 2.3 %collective-permute-start.4 = (bf16[576,1024]{1,0:T(8,128)(2,1)}, bf16[576,1024]{1,0:T(8,128)(2,1)}, u32[]{:S(2)}, u32[]{:S(2)}) collective-permute-start(bf16[576,1024]{1,0:T(8,128)(2,1)} %copy.45), channel_id=1, source_target_pairs={{0,1},{1,0},{2,3},{3,2},{4,5},{5,4},{6,7},{7,6},{8,9},{9,8},{10,11... | collective-permute-start | bytes 3538952 | tf_op jit(solution)/shard_map/ppermute | solution.py:38
  26.7 4.6 %all-to-all-done = bf16[8,144,128]{2,1,0:T(8,128)(2,1)S(1)} async-done(((bf16[8,144,128]{2,1,0:T(8,128)(2,1)}), bf16[8,144,128]{2,1,0:T(8,128)(2,1)S(1)}, u32[]{:S(2)}, u32[]{:S(2)}) %all-to-all-start) | async-done | bytes 294944 | tf_op jit(solution)/shard_map/all_to_all | solution.py:361
  32.1 2.2 %collective-permute-start.2 = (bf16[8,144,128]{2,1,0:T(8,128)(2,1)S(1)}, bf16[8,144,128]{2,1,0:T(8,128)(2,1)S(1)}, u32[]{:S(2)}, u32[]{:S(2)}) collective-permute-start(bf16[8,144,128]{2,1,0:T(8,128)(2,1)S(1)} %all-to-all-done), channel_id=1, source_target_pairs={{0,32},{32,0},{1,33},{33,1},{2,34},{34,2},{3,35},{35,3},{4,36},{36... | collective-permute-start | bytes 884744 | tf_op jit(solution)/shard_map/ppermute | solution.py:38
  34.4 10.0 %all-to-all-start.1 = ((bf16[8,144,256]{2,1,0:T(8,128)(2,1)}), bf16[8,144,256]{2,1,0:T(8,128)(2,1)S(1)}, u32[]{:S(2)}, u32[]{:S(2)}) async-start(bf16[8,144,256]{2,1,0:T(8,128)(2,1)} %broadcast_in_dim.61), calls=%async_computation.1 | async-start | bytes 1179648 | tf_op jit(solution)/shard_map/all_to_all | solution.py:366
  44.6 7.3 %collective-permute-start.1 = (bf16[64,128]{1,0:T(8,128)(2,1)S(1)}, bf16[64,128]{1,0:T(8,128)(2,1)S(1)}, u32[]{:S(2)}, u32[]{:S(2)}) collective-permute-start(bf16[64,128]{1,0:T(8,128)(2,1)S(1)} %bitcast.118), channel_id=1, source_target_pairs={{0,8},{8,0},{1,9},{9,1},{2,10},{10,2},{3,11},{11,3},{4,12},{12,4},... | collective-permute-start | bytes 49160 | tf_op jit(solution)/shard_map/ppermute | solution.py:38
  51.9 4.9 %collective-permute-done.2 = bf16[8,144,128]{2,1,0:T(8,128)(2,1)S(1)} collective-permute-done((bf16[8,144,128]{2,1,0:T(8,128)(2,1)S(1)}, bf16[8,144,128]{2,1,0:T(8,128)(2,1)S(1)}, u32[]{:S(2)}, u32[]{:S(2)}) %collective-permute-start.2) | collective-permute-done | bytes 294944 | tf_op jit(solution)/shard_map/ppermute | solution.py:38
  57.7 4.1 %collective-permute-start.3 = (bf16[2,8,144,128]{3,2,1,0:T(8,128)(2,1)}, bf16[2,8,144,128]{3,2,1,0:T(8,128)(2,1)S(1)}, u32[]{:S(2)}, u32[]{:S(2)}) collective-permute-start(bf16[2,8,144,128]{3,2,1,0:T(8,128)(2,1)} %pad_maximum_fusion.4), channel_id=1, source_target_pairs={{0,16},{16,0},{1,17},{17,1},{2,18},{18,2},{3,19},{19,3},{4,20},{20... | collective-permute-start | bytes 1769480 | tf_op jit(solution)/shard_map/ppermute | solution.py:38
  63.4 6.6 %all-to-all-start.2 = ((bf16[8,256,128]{2,1,0:T(8,128)(2,1)}), bf16[8,256,128]{2,1,0:T(8,128)(2,1)}, u32[]{:S(2)}, u32[]{:S(2)}) async-start(bf16[8,256,128]{2,1,0:T(8,128)(2,1)} %broadcast_in_dim.62), calls=%async_computation.2 | async-start | bytes 1048576 | tf_op jit(solution)/shard_map/all_to_all | solution.py:377
  73.9 14.1 %all-to-all-done.2 = bf16[8,256,128]{2,1,0:T(8,128)(2,1)} async-done(((bf16[8,256,128]{2,1,0:T(8,128)(2,1)}), bf16[8,256,128]{2,1,0:T(8,128)(2,1)}, u32[]{:S(2)}, u32[]{:S(2)}) %all-to-all-start.2) | async-done | bytes 524320 | tf_op jit(solution)/shard_map/all_to_all | solution.py:377
  95.3 10.4 %all-to-all-start.3 = ((bf16[8,288,128]{2,1,0:T(8,128)(2,1)}), bf16[8,288,128]{2,1,0:T(8,128)(2,1)S(1)}, u32[]{:S(2)}, u32[]{:S(2)}) async-start(bf16[8,288,128]{2,1,0:T(8,128)(2,1)} %copy-done.1), calls=%async_computation.3 | async-start | bytes 1179648 | tf_op jit(solution)/shard_map/all_to_all | solution.py:418
  107.9 2.9 %collective-permute-start.6 = (bf16[2,8,256,128]{3,2,1,0:T(8,128)(2,1)}, bf16[2,8,256,128]{3,2,1,0:T(8,128)(2,1)}, u32[]{:S(2)}, u32[]{:S(2)}) collective-permute-start(bf16[2,8,256,128]{3,2,1,0:T(8,128)(2,1)} %pad_maximum_fusion.2), channel_id=1, source_target_pairs={{0,16},{16,0},{1,17},{17,1},{2,18},{18,2},{3,19},{19,3},{4,20},{20... | collective-permute-start | bytes 3145736 | tf_op jit(solution)/shard_map/ppermute | solution.py:38
  111.8 3.8 %prepare_keys.1 = (bf16[2048,592]{1,0:T(8,128)(2,1)}, bf16[512,2048]{1,0:T(8,128)(2,1)S(1)}) custom-call(bf16[1024,576]{1,0:T(8,128)(2,1)S(1)} %bitcast.101, bf16[576,1024]{1,0:T(8,128)(2,1)} %collective-permute-done.4.k2t_ref, bf16[2048,16]{1,0:T(8,128)(2,1)S(1)} %select_convert_fusion.mask_ref), custom_call_target="tpu_custom_call" | custom-call | tf_op jit(solution)/shard_map/prepare_keys/pallas_call | solution.py:66
  116.9 8.1 %all-to-all-done.3 = bf16[8,288,128]{2,1,0:T(8,128)(2,1)S(1)} async-done(((bf16[8,288,128]{2,1,0:T(8,128)(2,1)}), bf16[8,288,128]{2,1,0:T(8,128)(2,1)S(1)}, u32[]{:S(2)}, u32[]{:S(2)}) %all-to-all-start.3) | async-done | bytes 589856 | tf_op jit(solution)/shard_map/all_to_all | solution.py:418
  125.8 4.2 %all-to-all-start.4 = ((bf16[8,128,128]{2,1,0:T(8,128)(2,1)}), bf16[8,128,128]{2,1,0:T(8,128)(2,1)}, u32[]{:S(2)}, u32[]{:S(2)}) async-start(bf16[8,128,128]{2,1,0:T(8,128)(2,1)} %broadcast_in_dim.63), calls=%async_computation.4 | async-start | bytes 524288 | tf_op jit(solution)/shard_map/all_to_all | solution.py:421
  133.2 11.0 %cache_attention.1 = bf16[2,4,224,128]{3,2,1,0:T(8,128)(2,1)} custom-call(bf16[2,4,288,128]{3,2,1,0:T(8,128)(2,1)S(1)} %bitcast.103, bf16[2048,592]{1,0:T(8,128)(2,1)} %get-tuple-element.40.k_ref, bf16[512,2048]{1,0:T(8,128)(2,1)S(1)} %copy-done.7, bf16[2,4,512,128]{3,2,1,0:T(8,128)(2,1)S(1)} %bitcast.106, bf16[2,4,128,512]{3,2,1,0:T(8,128)(2,1)S(1)} %bitcast.108, ...), custom_call_target="tpu_custom_call" | custom-call | flops 4563402752 | bytes 6291456 | tf_op jit(solution)/shard_map/cache_attention/pallas_call | solution.py:229
  145.2 3.1 %collective-permute-start.7 = (bf16[8,128,128]{2,1,0:T(8,128)(2,1)}, bf16[8,128,128]{2,1,0:T(8,128)(2,1)S(1)}, u32[]{:S(2)}, u32[]{:S(2)}) collective-permute-start(bf16[8,128,128]{2,1,0:T(8,128)(2,1)} %all-to-all-done.4), channel_id=1, source_target_pairs={{0,32},{32,0},{1,33},{33,1},{2,34},{34,2},{3,35},{35,3},{4,36},{36... | collective-permute-start | bytes 786440 | tf_op jit(solution)/shard_map/ppermute | solution.py:38
  148.4 3.5 %all-to-all-start.5 = ((bf16[8,224,128]{2,1,0:T(8,128)(2,1)}), bf16[8,224,128]{2,1,0:T(8,128)(2,1)S(1)}, u32[]{:S(2)}, u32[]{:S(2)}) async-start(bf16[8,224,128]{2,1,0:T(8,128)(2,1)} %bitcast.36), calls=%async_computation.5 | async-start | bytes 917504 | tf_op jit(solution)/shard_map/all_to_all | solution.py:433
  151.9 2.7 %collective-permute-done.7 = bf16[8,128,128]{2,1,0:T(8,128)(2,1)S(1)} collective-permute-done((bf16[8,128,128]{2,1,0:T(8,128)(2,1)}, bf16[8,128,128]{2,1,0:T(8,128)(2,1)S(1)}, u32[]{:S(2)}, u32[]{:S(2)}) %collective-permute-start.7) | collective-permute-done | bytes 262176 | tf_op jit(solution)/shard_map/ppermute | solution.py:38
  155.7 3.2 %collective-permute-start.8 = (bf16[2,8,128,128]{3,2,1,0:T(8,128)(2,1)S(1)}, bf16[2,8,128,128]{3,2,1,0:T(8,128)(2,1)S(1)}, u32[]{:S(2)}, u32[]{:S(2)}) collective-permute-start(bf16[2,8,128,128]{3,2,1,0:T(8,128)(2,1)S(1)} %pad_maximum_fusion.5), channel_id=1, source_target_pairs={{0,16},{16,0},{1,17},{17,1},{2,18},{18,2},{3,19},{19,3},{4,20},{20... | collective-permute-start | bytes 1572872 | tf_op jit(solution)/shard_map/ppermute | solution.py:38
  160.7 7.7 %all-to-all-done.5.part_ref = bf16[8,224,128]{2,1,0:T(8,128)(2,1)S(1)} async-done(((bf16[8,224,128]{2,1,0:T(8,128)(2,1)}), bf16[8,224,128]{2,1,0:T(8,128)(2,1)S(1)}, u32[]{:S(2)}, u32[]{:S(2)}) %all-to-all-start.5) | async-done | bytes 458784 | tf_op jit(solution)/shard_map/all_to_all | solution.py:433
  171.1 3.7 %all-to-all-start.6 = ((bf16[8,8,2048]{2,1,0:T(8,128)(2,1)}), bf16[8,8,2048]{2,1,0:T(8,128)(2,1)S(1)}, u32[]{:S(2)}, u32[]{:S(2)}) async-start(bf16[8,8,2048]{2,1,0:T(8,128)(2,1)} %bitcast.105), calls=%async_computation.6 | async-start | bytes 524288 | tf_op jit(solution)/shard_map/all_to_all | solution.py:450
  177.9 6.0 %all-to-all-done.6 = bf16[8,8,2048]{2,1,0:T(8,128)(2,1)S(1)} async-done(((bf16[8,8,2048]{2,1,0:T(8,128)(2,1)}), bf16[8,8,2048]{2,1,0:T(8,128)(2,1)S(1)}, u32[]{:S(2)}, u32[]{:S(2)}) %all-to-all-start.6) | async-done | bytes 262176 | tf_op jit(solution)/shard_map/all_to_all | solution.py:450
  (151 shorter events, 43.3 us)
Async XLA Ops:
  0.6 20.0 %copy-start = (bf16[16,64,576]{2,1,0:T(8,128)(2,1)S(1)}, bf16[16,64,576]{2,1,0:T(8,128)(2,1)}, u32[]{:S(2)}) copy-start(bf16[16,64,576]{2,1,0:T(8,128)(2,1)} %param.18) | copy-start | bytes 3538948
  1.5 10.4 %collective-permute-start = (bf16[146,128]{1,0:T(8,128)(2,1)S(1)}, bf16[146,128]{1,0:T(8,128)(2,1)S(1)}, u32[]{:S(2)}, u32[]{:S(2)}) collective-permute-start(bf16[146,128]{1,0:T(8,128)(2,1)S(1)} %pad_maximum_fusion.11), channel_id=1, source_target_pairs={{0,1},{1,0},{2,3},{3,2},{4,5},{5,4},{6,7},{7,6},{8,9},{9,8},{10,11... | collective-permute-start | bytes 112136 | tf_op jit(solution)/shard_map/ppermute | solution.py:38
  8.7 35.7 %copy-start.18 = (f32[32]{0:T(128)}, f32[32]{0:T(128)S(1)}, u32[]{:S(2)}) copy-start(f32[32]{0:T(128)S(1)} %multiply_power_fusion) | copy-start | bytes 388
  13.8 17.5 %all-to-all-start = ((bf16[8,144,128]{2,1,0:T(8,128)(2,1)}), bf16[8,144,128]{2,1,0:T(8,128)(2,1)S(1)}, u32[]{:S(2)}, u32[]{:S(2)}) async-start(bf16[8,144,128]{2,1,0:T(8,128)(2,1)} %broadcast_in_dim.60), calls=%async_computation | async-start | bytes 589824 | tf_op jit(solution)/shard_map/all_to_all | solution.py:361
  22.1 22.5 %copy-start.11 = (bf16[128,64]{0,1:T(8,128)(2,1)S(1)}, bf16[128,64]{0,1:T(8,128)(2,1)}, u32[]{:S(2)}) copy-start(bf16[128,64]{0,1:T(8,128)(2,1)} %param.17) | copy-start | bytes 49156
  22.1 48.1 %collective-permute-start.4 = (bf16[576,1024]{1,0:T(8,128)(2,1)}, bf16[576,1024]{1,0:T(8,128)(2,1)}, u32[]{:S(2)}, u32[]{:S(2)}) collective-permute-start(bf16[576,1024]{1,0:T(8,128)(2,1)} %copy.45), channel_id=1, source_target_pairs={{0,1},{1,0},{2,3},{3,2},{4,5},{5,4},{6,7},{7,6},{8,9},{9,8},{10,11... | collective-permute-start | bytes 3538952 | tf_op jit(solution)/shard_map/ppermute | solution.py:38
  26.7 25.2 %copy-start.19 = (f32[128]{0:T(128)}, f32[128]{0:T(128)S(1)}, u32[]{:S(2)}) copy-start(f32[128]{0:T(128)S(1)} %add.147) | copy-start | bytes 1540
  32.1 24.7 %collective-permute-start.2 = (bf16[8,144,128]{2,1,0:T(8,128)(2,1)S(1)}, bf16[8,144,128]{2,1,0:T(8,128)(2,1)S(1)}, u32[]{:S(2)}, u32[]{:S(2)}) collective-permute-start(bf16[8,144,128]{2,1,0:T(8,128)(2,1)S(1)} %all-to-all-done), channel_id=1, source_target_pairs={{0,32},{32,0},{1,33},{33,1},{2,34},{34,2},{3,35},{35,3},{4,36},{36... | collective-permute-start | bytes 884744 | tf_op jit(solution)/shard_map/ppermute | solution.py:38
  34.4 28.1 %all-to-all-start.1 = ((bf16[8,144,256]{2,1,0:T(8,128)(2,1)}), bf16[8,144,256]{2,1,0:T(8,128)(2,1)S(1)}, u32[]{:S(2)}, u32[]{:S(2)}) async-start(bf16[8,144,256]{2,1,0:T(8,128)(2,1)} %broadcast_in_dim.61), calls=%async_computation.1 | async-start | bytes 1179648 | tf_op jit(solution)/shard_map/all_to_all | solution.py:366
  44.6 17.2 %collective-permute-start.1 = (bf16[64,128]{1,0:T(8,128)(2,1)S(1)}, bf16[64,128]{1,0:T(8,128)(2,1)S(1)}, u32[]{:S(2)}, u32[]{:S(2)}) collective-permute-start(bf16[64,128]{1,0:T(8,128)(2,1)S(1)} %bitcast.118), channel_id=1, source_target_pairs={{0,8},{8,0},{1,9},{9,1},{2,10},{10,2},{3,11},{11,3},{4,12},{12,4},... | collective-permute-start | bytes 49160 | tf_op jit(solution)/shard_map/ppermute | solution.py:38
  57.7 12.3 %collective-permute-start.3 = (bf16[2,8,144,128]{3,2,1,0:T(8,128)(2,1)}, bf16[2,8,144,128]{3,2,1,0:T(8,128)(2,1)S(1)}, u32[]{:S(2)}, u32[]{:S(2)}) collective-permute-start(bf16[2,8,144,128]{3,2,1,0:T(8,128)(2,1)} %pad_maximum_fusion.4), channel_id=1, source_target_pairs={{0,16},{16,0},{1,17},{17,1},{2,18},{18,2},{3,19},{19,3},{4,20},{20... | collective-permute-start | bytes 1769480 | tf_op jit(solution)/shard_map/ppermute | solution.py:38
  63.4 24.7 %all-to-all-start.2 = ((bf16[8,256,128]{2,1,0:T(8,128)(2,1)}), bf16[8,256,128]{2,1,0:T(8,128)(2,1)}, u32[]{:S(2)}, u32[]{:S(2)}) async-start(bf16[8,256,128]{2,1,0:T(8,128)(2,1)} %broadcast_in_dim.62), calls=%async_computation.2 | async-start | bytes 1048576 | tf_op jit(solution)/shard_map/all_to_all | solution.py:377
  88.0 17.6 %collective-permute-start.5 = (bf16[8,256,128]{2,1,0:T(8,128)(2,1)}, bf16[8,256,128]{2,1,0:T(8,128)(2,1)S(1)}, u32[]{:S(2)}, u32[]{:S(2)}) collective-permute-start(bf16[8,256,128]{2,1,0:T(8,128)(2,1)} %all-to-all-done.2), channel_id=1, source_target_pairs={{0,32},{32,0},{1,33},{33,1},{2,34},{34,2},{3,35},{35,3},{4,36},{36... | collective-permute-start | bytes 1572872 | tf_op jit(solution)/shard_map/ppermute | solution.py:38
  95.3 29.7 %all-to-all-start.3 = ((bf16[8,288,128]{2,1,0:T(8,128)(2,1)}), bf16[8,288,128]{2,1,0:T(8,128)(2,1)S(1)}, u32[]{:S(2)}, u32[]{:S(2)}) async-start(bf16[8,288,128]{2,1,0:T(8,128)(2,1)} %copy-done.1), calls=%async_computation.3 | async-start | bytes 1179648 | tf_op jit(solution)/shard_map/all_to_all | solution.py:418
  107.9 22.1 %collective-permute-start.6 = (bf16[2,8,256,128]{3,2,1,0:T(8,128)(2,1)}, bf16[2,8,256,128]{3,2,1,0:T(8,128)(2,1)}, u32[]{:S(2)}, u32[]{:S(2)}) collective-permute-start(bf16[2,8,256,128]{3,2,1,0:T(8,128)(2,1)} %pad_maximum_fusion.2), channel_id=1, source_target_pairs={{0,16},{16,0},{1,17},{17,1},{2,18},{18,2},{3,19},{19,3},{4,20},{20... | collective-permute-start | bytes 3145736 | tf_op jit(solution)/shard_map/ppermute | solution.py:38
  125.8 19.4 %all-to-all-start.4 = ((bf16[8,128,128]{2,1,0:T(8,128)(2,1)}), bf16[8,128,128]{2,1,0:T(8,128)(2,1)}, u32[]{:S(2)}, u32[]{:S(2)}) async-start(bf16[8,128,128]{2,1,0:T(8,128)(2,1)} %broadcast_in_dim.63), calls=%async_computation.4 | async-start | bytes 524288 | tf_op jit(solution)/shard_map/all_to_all | solution.py:421
  145.2 9.5 %collective-permute-start.7 = (bf16[8,128,128]{2,1,0:T(8,128)(2,1)}, bf16[8,128,128]{2,1,0:T(8,128)(2,1)S(1)}, u32[]{:S(2)}, u32[]{:S(2)}) collective-permute-start(bf16[8,128,128]{2,1,0:T(8,128)(2,1)} %all-to-all-done.4), channel_id=1, source_target_pairs={{0,32},{32,0},{1,33},{33,1},{2,34},{34,2},{3,35},{35,3},{4,36},{36... | collective-permute-start | bytes 786440 | tf_op jit(solution)/shard_map/ppermute | solution.py:38
  148.4 20.0 %all-to-all-start.5 = ((bf16[8,224,128]{2,1,0:T(8,128)(2,1)}), bf16[8,224,128]{2,1,0:T(8,128)(2,1)S(1)}, u32[]{:S(2)}, u32[]{:S(2)}) async-start(bf16[8,224,128]{2,1,0:T(8,128)(2,1)} %bitcast.36), calls=%async_computation.5 | async-start | bytes 917504 | tf_op jit(solution)/shard_map/all_to_all | solution.py:433
  155.7 4.8 %collective-permute-start.8 = (bf16[2,8,128,128]{3,2,1,0:T(8,128)(2,1)S(1)}, bf16[2,8,128,128]{3,2,1,0:T(8,128)(2,1)S(1)}, u32[]{:S(2)}, u32[]{:S(2)}) collective-permute-start(bf16[2,8,128,128]{3,2,1,0:T(8,128)(2,1)S(1)} %pad_maximum_fusion.5), channel_id=1, source_target_pairs={{0,16},{16,0},{1,17},{17,1},{2,18},{18,2},{3,19},{19,3},{4,20},{20... | collective-permute-start | bytes 1572872 | tf_op jit(solution)/shard_map/ppermute | solution.py:38
  160.6 14.2 %copy-start.14 = (f32[2,64]{1,0:T(2,128)S(1)}, f32[2,64]{1,0:T(2,128)}, u32[]{:S(2)}) copy-start(f32[2,64]{1,0:T(2,128)} %copy-done.13) | copy-start | bytes 1540
  160.6 14.2 %copy-start.17 = (f32[2,64]{1,0:T(2,128)S(1)}, f32[2,64]{1,0:T(2,128)}, u32[]{:S(2)}) copy-start(f32[2,64]{1,0:T(2,128)} %get-tuple-element.50) | copy-start | bytes 1540
  160.7 14.4 %copy-start.16 = (s32[32]{0:T(128)S(1)}, s32[32]{0:T(128)}, u32[]{:S(2)}) copy-start(s32[32]{0:T(128)} %copy-done.15) | copy-start | bytes 388
  160.7 14.4 %copy-start.22 = (s32[128]{0:T(128)S(1)}, s32[128]{0:T(128)}, u32[]{:S(2)}) copy-start(s32[128]{0:T(128)} %and_select_fusion) | copy-start | bytes 1540
  171.1 12.8 %all-to-all-start.6 = ((bf16[8,8,2048]{2,1,0:T(8,128)(2,1)}), bf16[8,8,2048]{2,1,0:T(8,128)(2,1)S(1)}, u32[]{:S(2)}, u32[]{:S(2)}) async-start(bf16[8,8,2048]{2,1,0:T(8,128)(2,1)} %bitcast.105), calls=%async_computation.6 | async-start | bytes 524288 | tf_op jit(solution)/shard_map/all_to_all | solution.py:450
  (18 other events, 70.4 us)
